TPU v7x, 32 devices: a whole 2x2x4 slice. The times are simulated.
32 devices in a mesh: dp: 8 (over z, y), tensor: 4 (over x, core).
Axes of the slice: x: 2, y: 2, z: 4, core: 2. Of those that a mesh axis runs over, the one named last changes fastest.
Arguments:
- hidden: bfloat16 [4096, 2048], P('dp'), may hold values from -6 to 6
- embedding: bfloat16 [4096, 2048], P('dp'), may hold values from -6 to 6
- teacher_mid: bfloat16 [4096, 2048], P('dp'), may hold values from -6 to 6
- teacher_out: bfloat16 [4096, 2048], P('dp'), may hold values from -6 to 6
- segment_ids: int32 [4096], P('dp'), may hold values from 0 to 7, as said below
- rope_pos: int32 [4096], P('dp'), may hold values from 0 to 255, as said below
- valid_mask: int32 [4096], P('dp'), may hold values from 0 to 1, as said below
- gain_attn: bfloat16 [4096], P('dp'), may hold values from 0.5 to 1.5
- w_query: bfloat16 [4096, 4096], P('dp', 'tensor'), may hold values from -0.09375 to 0.09375
- w_key: bfloat16 [4096, 4096], P('dp', 'tensor'), may hold values from -0.09375 to 0.09375
- w_value: bfloat16 [4096, 4096], P('dp', 'tensor'), may hold values from -0.09375 to 0.09375
- query_down: bfloat16 [4096, 128], P('dp'), may hold values from -0.09375 to 0.09375
- query_up: bfloat16 [128, 4096], P('dp', 'tensor'), may hold values from -0.25 to 0.25
- w_attn_out: bfloat16 [2048, 4096], P('dp', 'tensor'), may hold values from -0.75 to 0.75
- gain_mlp: bfloat16 [2048], P('dp'), may hold values from 0.5 to 1.5
- w_gate: bfloat16 [2048, 8192], P('dp', 'tensor'), may hold values from -0.125 to 0.125
- w_up: bfloat16 [2048, 8192], P('dp', 'tensor'), may hold values from -0.125 to 0.125
- gate_down: bfloat16 [2048, 128], P('dp'), may hold values from -0.125 to 0.125
- gate_up: bfloat16 [128, 8192], P('dp', 'tensor'), may hold values from -0.25 to 0.25
- w_down: bfloat16 [2048, 8192], P('dp', 'tensor'), may hold values from -0.0625 to 0.0625
- w_proj: bfloat16 [2048, 2048], P('dp', 'tensor'), may hold values from -0.125 to 0.125
- gain_mamba: bfloat16 [2048], P('dp'), may hold values from 0.5 to 1.5
- w_in_gate: bfloat16 [2048, 4096], P('dp', 'tensor'), may hold values from -0.125 to 0.125
- w_in_main: bfloat16 [2048, 4096], P('dp', 'tensor'), may hold values from -0.125 to 0.125
- w_in_state: bfloat16 [2048, 256], P('dp'), may hold values from -0.125 to 0.125
- w_in_step: bfloat16 [2048, 64], P('dp', 'tensor'), may hold values from -0.125 to 0.125
- conv_main: bfloat16 [4096, 4], P(('tensor', 'dp')), may hold values from -3 to 3
- conv_main_bias: bfloat16 [4096], P(('tensor', 'dp')), may hold values from -0.5 to 0.5
- conv_state: bfloat16 [256, 4], P('dp'), may hold values from -3 to 3
- conv_state_bias: bfloat16 [256], P('dp'), may hold values from -0.5 to 0.5
- gain_gated: bfloat16 [4096], P(('tensor', 'dp')), may hold values from 0.5 to 1.5
- w_mamba_out: bfloat16 [2048, 4096], P('dp', 'tensor'), may hold values from -0.09375 to 0.09375
- step_bias: bfloat16 [64], P('tensor'), may hold values from -5 to -2
- decay_log: bfloat16 [64], P('tensor'), may hold values from -1 to 2.5
- skip_scale: bfloat16 [64], P('tensor'), may hold values from 0.5 to 1.5
Outputs:
- output: bfloat16 [4096, 2048], P('dp')
- loss_mid: float32 [], replicated
- loss_out: float32 [], replicated
- grad_hidden: float32 [4096, 2048], P('dp')
- grad_embedding: float32 [4096, 2048], P('dp')
- grad_gain_attn: float32 [4096], P('dp')
- grad_w_query: float32 [4096, 4096], P('dp', 'tensor')
- grad_w_key: float32 [4096, 4096], P('dp', 'tensor')
- grad_w_value: float32 [4096, 4096], P('dp', 'tensor')
- grad_query_down: float32 [4096, 128], P('dp')
- grad_query_up: float32 [128, 4096], P('dp', 'tensor')
- grad_w_attn_out: float32 [2048, 4096], P('dp', 'tensor')
- grad_gain_mlp: float32 [2048], P('dp')
- grad_w_gate: float32 [2048, 8192], P('dp', 'tensor')
- grad_w_up: float32 [2048, 8192], P('dp', 'tensor')
- grad_gate_down: float32 [2048, 128], P('dp')
- grad_gate_up: float32 [128, 8192], P('dp', 'tensor')
- grad_w_down: float32 [2048, 8192], P('dp', 'tensor')
- grad_w_proj: float32 [2048, 2048], P('dp', 'tensor')
- grad_gain_mamba: float32 [2048], P('dp')
- grad_w_in_gate: float32 [2048, 4096], P('dp', 'tensor')
- grad_w_in_main: float32 [2048, 4096], P('dp', 'tensor')
- grad_w_in_state: float32 [2048, 256], P('dp')
- grad_w_in_step: float32 [2048, 64], P('dp', 'tensor')
- grad_conv_main: float32 [4096, 4], P(('tensor', 'dp'))
- grad_conv_main_bias: float32 [4096], P(('tensor', 'dp'))
- grad_conv_state: float32 [256, 4], P('dp')
- grad_conv_state_bias: float32 [256], P('dp')
- grad_gain_gated: float32 [4096], P(('tensor', 'dp'))
- grad_w_mamba_out: float32 [2048, 4096], P('dp', 'tensor')
- grad_step_bias: float32 [64], P('tensor')
- grad_decay_log: float32 [64], P('tensor')
- grad_skip_scale: float32 [64], P('tensor')
Inputs may be any that keep to these rules, and one draw needn't show every extreme that they name: `segment_ids`: numbers count the documents of each sequence of 512 tokens from 0 and never fall inside it. `rope_pos`: the token's place within its document, 0 at a document's first token. `valid_mask`: the first token of every sequence is valid.
All inputs are finite; a program needn't handle non-finite values.
Results may differ from a plain program's by a relative error of at most 0.035.
Values may be sent and summed in bfloat16 or wider, within the bound.
No kernel may reach another device: no remote copies, remote signals or barrier semaphores. Data moves between devices by JAX's collectives and lax.ppermute only.
A program may use at most 384 MiB of HBM per device.

v0:
```python
from functools import partial

import jax
import jax.numpy as jnp
from jax import lax
from jax.sharding import PartitionSpec as P

D = 2048
HEADS = 32
HEAD_SIZE = 128
STATE = 128
NHM = 64
DI = 4096
HEAD_M = 64


eps = 1e-05


def narrow(values):
    return values.astype(jnp.bfloat16)


def times_right(left, right):
    return jnp.dot(left, right, preferred_element_type=jnp.float32)


def times_trans(left, right):
    return lax.dot_general(
        left, right, (((1,), (1,)), ((), ())), preferred_element_type=jnp.float32
    )


def trans_times(left, right):
    return lax.dot_general(
        left, right, (((0,), (0,)), ((), ())), preferred_element_type=jnp.float32
    )


def rms_scale(values, gain):
    return values * lax.rsqrt(jnp.mean(values * values, axis=-1, keepdims=True) + eps) * gain


def rotary(values, cosine, sine):
    half = values.shape[-1] // 2
    first = values[..., :half]
    second = values[..., half:]
    return jnp.concatenate(
        [first * cosine - second * sine, second * cosine + first * sine], axis=-1
    )


def conv_act(pre, weight, bias, segments):
    length = pre.shape[0]
    taps = weight.shape[1]
    total = jnp.zeros_like(pre) + bias
    for tap in range(taps):
        lag = taps - 1 - tap
        shifted = jnp.pad(pre, ((lag, 0), (0, 0)))[:length]
        earlier = jnp.pad(segments, ((lag, 0),), constant_values=-1)[:length]
        keeping = (earlier == segments).astype(jnp.float32)[:, None]
        total = total + weight[:, tap] * shifted * keeping
    return jax.nn.silu(total)


def gelu_product(gate_pre, up_pre):
    return jax.nn.gelu(gate_pre, approximate=True) * up_pre


def decay_piece(step_pre, step_bias, decay_log, same):
    sizes = jax.nn.softplus(step_pre + step_bias)
    accum = jnp.cumsum(sizes * -jnp.exp(decay_log), axis=0)
    lagged = accum.T[:, :, None] - accum.T[:, None, :]
    kernel = jnp.where(same[None], jnp.exp(jnp.where(same[None], lagged, 0.0)), 0.0)
    return (kernel, sizes)


def mixed_piece(core, mamba_heads, mamba_gate, skip_scale):
    rows = core.shape[0]
    with_skip = (core + skip_scale[:, None] * mamba_heads).reshape(rows, -1)
    return with_skip * jax.nn.silu(mamba_gate)


def score_block(query_rot, key_rot):
    return jnp.einsum(
        "qhe,khe->hqk", query_rot, key_rot, preferred_element_type=jnp.float32
    ) * HEAD_SIZE ** (-0.5)


def attend_forward(query_rot, key_rot, value_low, allowed):
    masked = jnp.where(allowed[None], score_block(query_rot, key_rot), -1e30)
    row_max = jnp.max(masked, axis=-1, keepdims=True)
    exp_scores = jnp.exp(masked - row_max)
    row_sum = jnp.sum(exp_scores, axis=-1, keepdims=True)
    attention_probabilities = narrow(exp_scores / row_sum)
    attended = jnp.einsum(
        "hqk,khe->qhe", attention_probabilities, value_low, preferred_element_type=jnp.float32
    )
    return (attended, row_max + jnp.log(row_sum))


def attend_backward(query_rot, key_rot, value_low, allowed, log_total, grad_out):
    attention_scores = score_block(query_rot, key_rot)
    attention_probabilities = jnp.where(
        allowed[None], jnp.exp(jnp.where(allowed[None], attention_scores, 0.0) - log_total), 0.0
    )
    grad_probs = jnp.einsum("qhe,khe->hqk", grad_out, value_low, preferred_element_type=jnp.float32)
    grad_value = jnp.einsum(
        "hqk,qhe->khe",
        narrow(attention_probabilities),
        grad_out,
        preferred_element_type=jnp.float32,
    )
    inner_sum = jnp.sum(attention_probabilities * grad_probs, axis=-1, keepdims=True)
    grad_scores = narrow(attention_probabilities * (grad_probs - inner_sum))
    grad_query = jnp.einsum(
        "hqk,khe->qhe", grad_scores, key_rot, preferred_element_type=jnp.float32
    ) * HEAD_SIZE ** (-0.5)
    grad_key = jnp.einsum(
        "hqk,qhe->khe", grad_scores, query_rot, preferred_element_type=jnp.float32
    ) * HEAD_SIZE ** (-0.5)
    return (grad_query, grad_key, grad_value)


def body(
    hidden,
    embedding,
    teacher_mid,
    teacher_out,
    segment_ids,
    rope_pos,
    valid_mask,
    gain_attn,
    w_query,
    w_key,
    w_value,
    query_down,
    query_up,
    w_attn_out,
    gain_mlp,
    w_gate,
    w_up,
    gate_down,
    gate_up,
    w_down,
    w_proj,
    gain_mamba,
    w_in_gate,
    w_in_main,
    w_in_state,
    w_in_step,
    conv_main,
    conv_main_bias,
    conv_state,
    conv_state_bias,
    gain_gated,
    w_mamba_out,
    step_bias,
    decay_log,
    skip_scale,
):
    (
        gain_attn,
        w_query,
        w_key,
        w_value,
        query_down,
        query_up,
        w_attn_out,
        gain_mlp,
        w_gate,
        w_up,
        gate_down,
        gate_up,
        w_down,
        w_proj,
        gain_mamba,
        w_in_gate,
        w_in_main,
        w_in_state,
        w_in_step,
        conv_main,
        conv_main_bias,
        conv_state,
        conv_state_bias,
        gain_gated,
        w_mamba_out,
    ) = (
        lax.all_gather(gain_attn, "dp", axis=0, tiled=True),
        lax.all_gather(w_query, "dp", axis=0, tiled=True),
        lax.all_gather(w_key, "dp", axis=0, tiled=True),
        lax.all_gather(w_value, "dp", axis=0, tiled=True),
        lax.all_gather(query_down, "dp", axis=0, tiled=True),
        lax.all_gather(query_up, "dp", axis=0, tiled=True),
        lax.all_gather(w_attn_out, "dp", axis=0, tiled=True),
        lax.all_gather(gain_mlp, "dp", axis=0, tiled=True),
        lax.all_gather(w_gate, "dp", axis=0, tiled=True),
        lax.all_gather(w_up, "dp", axis=0, tiled=True),
        lax.all_gather(gate_down, "dp", axis=0, tiled=True),
        lax.all_gather(gate_up, "dp", axis=0, tiled=True),
        lax.all_gather(w_down, "dp", axis=0, tiled=True),
        lax.all_gather(w_proj, "dp", axis=0, tiled=True),
        lax.all_gather(gain_mamba, "dp", axis=0, tiled=True),
        lax.all_gather(w_in_gate, "dp", axis=0, tiled=True),
        lax.all_gather(w_in_main, "dp", axis=0, tiled=True),
        lax.all_gather(w_in_state, "dp", axis=0, tiled=True),
        lax.all_gather(w_in_step, "dp", axis=0, tiled=True),
        lax.all_gather(conv_main, "dp", axis=0, tiled=True),
        lax.all_gather(conv_main_bias, "dp", axis=0, tiled=True),
        lax.all_gather(conv_state, "dp", axis=0, tiled=True),
        lax.all_gather(conv_state_bias, "dp", axis=0, tiled=True),
        lax.all_gather(gain_gated, "dp", axis=0, tiled=True),
        lax.all_gather(w_mamba_out, "dp", axis=0, tiled=True),
    )
    length = hidden.shape[0]
    tensor_count = lax.axis_size("tensor")
    heads_here = HEADS // tensor_count
    mamba_here = NHM // tensor_count
    width_here = D // tensor_count
    hidden_f = hidden.astype(jnp.float32)
    places = jnp.arange(length)
    allowed = (places[:, None] >= places[None, :]) & (segment_ids[:, None] == segment_ids[None, :])
    valid_rows = valid_mask.astype(jnp.float32)[:, None]
    half = HEAD_SIZE // 2
    inverse = 10000.0 ** (-jnp.arange(half, dtype=jnp.float32) / half)
    angles = rope_pos.astype(jnp.float32)[:, None] * inverse[None, :]
    turning = partial(rotary, cosine=jnp.cos(angles)[:, None, :], sine=jnp.sin(angles)[:, None, :])
    concat = jnp.concatenate([hidden_f, embedding.astype(jnp.float32)], axis=1)
    normed_cat, cat_back = jax.vjp(rms_scale, concat, gain_attn.astype(jnp.float32))
    normed_cat = narrow(normed_cat)
    query_low = narrow(times_right(normed_cat, query_down))
    query_pre = times_right(normed_cat, w_query) + times_right(query_low, query_up)
    key_pre = times_right(normed_cat, w_key)
    value_low = narrow(times_right(normed_cat, w_value)).reshape(length, heads_here, HEAD_SIZE)
    query_rot, query_turn_back = jax.vjp(turning, query_pre.reshape(length, heads_here, HEAD_SIZE))
    key_rot, key_turn_back = jax.vjp(turning, key_pre.reshape(length, heads_here, HEAD_SIZE))
    query_rot = narrow(query_rot)
    key_rot = narrow(key_rot)
    attended, log_total = attend_forward(query_rot, key_rot, value_low, allowed)
    attended_low = narrow(attended.reshape(length, -1))
    attn_branch = lax.psum(times_trans(attended_low, w_attn_out), "tensor")
    first_sum = hidden_f + attn_branch
    normed_mid, mid_back = jax.vjp(rms_scale, first_sum, gain_mlp.astype(jnp.float32))
    normed_mid = narrow(normed_mid)
    gate_low = narrow(times_right(normed_mid, gate_down))
    gate_pre = times_right(normed_mid, w_gate) + times_right(gate_low, gate_up)
    up_pre = times_right(normed_mid, w_up)
    inner, inner_back = jax.vjp(gelu_product, gate_pre, up_pre)
    inner = narrow(inner)
    mlp_part = lax.psum_scatter(
        times_trans(inner, w_down), "tensor", scatter_dimension=1, tiled=True
    )
    offset = lax.axis_index("tensor") * width_here
    shared_out = narrow(lax.dynamic_slice_in_dim(attn_branch, offset, width_here, 1) + mlp_part)
    projected = lax.psum(times_trans(shared_out, w_proj), "tensor")
    middle = hidden_f + projected
    normed_last, last_back = jax.vjp(rms_scale, middle, gain_mamba.astype(jnp.float32))
    normed_last = narrow(normed_last)
    mamba_gate = times_right(normed_last, w_in_gate)
    mamba_pre = times_right(normed_last, w_in_main)
    state_pre = times_right(normed_last, w_in_state)
    step_pre = times_right(normed_last, w_in_step)
    convolve = partial(conv_act, segments=segment_ids)
    mamba_act, main_conv_back = jax.vjp(
        convolve, mamba_pre, conv_main.astype(jnp.float32), conv_main_bias.astype(jnp.float32)
    )
    state_act, state_conv_back = jax.vjp(
        convolve, state_pre, conv_state.astype(jnp.float32), conv_state_bias.astype(jnp.float32)
    )
    state_in = narrow(state_act[:, :STATE])
    state_out = narrow(state_act[:, STATE:])
    (decay, step_sizes), decay_back = jax.vjp(
        partial(decay_piece, same=allowed),
        step_pre,
        step_bias.astype(jnp.float32),
        decay_log.astype(jnp.float32),
    )
    mamba_heads = mamba_act.reshape(length, mamba_here, HEAD_M)
    weighted = narrow(mamba_heads * step_sizes[:, :, None])
    gram = times_trans(state_out, state_in)
    mixing = narrow(gram[None] * decay)
    core = jnp.einsum("hts,she->the", mixing, weighted, preferred_element_type=jnp.float32)
    mixed, mixed_back = jax.vjp(
        mixed_piece, core, mamba_heads, mamba_gate, skip_scale.astype(jnp.float32)
    )
    square_total = lax.psum(jnp.sum(mixed * mixed, axis=1), "tensor")
    inverse_rms = lax.rsqrt(square_total / DI + eps)[:, None]
    gain_float = gain_gated.astype(jnp.float32)
    normed_mixed = mixed * inverse_rms
    gated = narrow(normed_mixed * gain_float)
    mamba_branch = lax.psum(times_trans(gated, w_mamba_out).astype(jnp.bfloat16), "tensor").astype(
        jnp.float32
    )
    final_sum = middle + mamba_branch
    miss_mid = middle - teacher_mid.astype(jnp.float32)
    miss_out = final_sum - teacher_out.astype(jnp.float32)
    count, square_mid, square_out = lax.psum(
        (
            jnp.sum(valid_rows),
            jnp.sum(valid_rows * miss_mid * miss_mid),
            jnp.sum(valid_rows * miss_out * miss_out),
        ),
        "dp",
    )
    loss_mid = square_mid / (count * D)
    loss_out = square_out / (count * D)
    factor = length * lax.axis_size("dp") / count
    grad_final = factor * valid_rows * miss_out
    branch_grad = narrow(grad_final)
    grad_w_mamba_out = trans_times(branch_grad, gated)
    grad_gated_f = times_right(branch_grad, w_mamba_out)
    grad_gain_gated = jnp.sum(grad_gated_f * normed_mixed, axis=0)
    grad_normed = grad_gated_f * gain_float
    row_inner = lax.psum(jnp.sum(grad_normed * normed_mixed, axis=1), "tensor")
    grad_mixed = inverse_rms * (grad_normed - normed_mixed * (row_inner / DI)[:, None])
    grad_core, grad_heads, grad_gate_z, grad_skip_scale = mixed_back(grad_mixed)
    core_grad = narrow(grad_core)
    grad_mixing = jnp.einsum(
        "the,she->hts", core_grad, weighted, preferred_element_type=jnp.float32
    )
    grad_weighted = jnp.einsum(
        "hts,the->she", mixing, core_grad, preferred_element_type=jnp.float32
    )
    gram_part = jnp.sum(grad_mixing * decay, axis=0)
    grad_step_pre, grad_step_bias, grad_decay_log = decay_back(
        (grad_mixing * gram[None], jnp.sum(grad_weighted * mamba_heads, axis=-1))
    )
    grad_heads = grad_heads + grad_weighted * step_sizes[:, :, None]
    grad_mamba_pre, grad_conv_main, grad_conv_main_bias = main_conv_back(
        grad_heads.reshape(length, -1)
    )
    gate_grad_low = narrow(grad_gate_z)
    main_grad_low = narrow(grad_mamba_pre)
    step_grad_low = narrow(grad_step_pre)
    grad_w_in_gate = trans_times(normed_last, gate_grad_low)
    grad_w_in_main = trans_times(normed_last, main_grad_low)
    grad_w_in_step = trans_times(normed_last, step_grad_low)
    last_part = (
        times_trans(gate_grad_low, w_in_gate)
        + times_trans(main_grad_low, w_in_main)
        + times_trans(step_grad_low, w_in_step)
    )
    last_sum, gram_grad = (
        lax.psum(last_part.astype(jnp.bfloat16), "tensor").astype(jnp.float32),
        lax.psum(gram_part.astype(jnp.bfloat16), "tensor").astype(jnp.float32),
    )
    gram_grad = narrow(gram_grad)
    grad_state = jnp.concatenate(
        [trans_times(gram_grad, state_out), times_right(gram_grad, state_in)], axis=1
    )
    grad_state_pre, grad_conv_state, grad_conv_state_bias = state_conv_back(grad_state)
    state_grad_low = narrow(grad_state_pre)
    grad_w_in_state = trans_times(normed_last, state_grad_low)
    grad_middle, grad_gain_mamba = last_back(last_sum + times_trans(state_grad_low, w_in_state))
    grad_middle = grad_middle + grad_final + factor * valid_rows * miss_mid
    mamba_shards = ()
    projected_grad = narrow(grad_middle)
    grad_w_proj = trans_times(projected_grad, shared_out)
    grad_shared = lax.all_gather(
        times_right(projected_grad, w_proj).astype(jnp.bfloat16), "tensor", axis=1, tiled=True
    ).astype(jnp.float32)
    mlp_grad = narrow(grad_shared)
    grad_w_down = trans_times(mlp_grad, inner)
    grad_gate_pre, grad_up_pre = inner_back(times_right(mlp_grad, w_down))
    gate_grad = narrow(grad_gate_pre)
    up_grad = narrow(grad_up_pre)
    grad_w_gate = trans_times(normed_mid, gate_grad)
    grad_w_up = trans_times(normed_mid, up_grad)
    grad_gate_up = trans_times(gate_low, gate_grad)
    mid_part = times_trans(gate_grad, w_gate) + times_trans(up_grad, w_up)
    mid_sum, gate_low_grad = (
        lax.psum(mid_part.astype(jnp.bfloat16), "tensor").astype(jnp.float32),
        lax.psum(times_trans(gate_grad, gate_up).astype(jnp.bfloat16), "tensor").astype(
            jnp.float32
        ),
    )
    gate_low_grad = narrow(gate_low_grad)
    grad_gate_down = trans_times(normed_mid, gate_low_grad)
    grad_first, grad_gain_mlp = mid_back(mid_sum + times_trans(gate_low_grad, gate_down))
    joined = (
        lax.psum_scatter(
            grad_gain_mlp.astype(jnp.bfloat16), "dp", scatter_dimension=0, tiled=True
        ).astype(jnp.float32),
        lax.psum_scatter(
            grad_w_gate.astype(jnp.bfloat16), "dp", scatter_dimension=0, tiled=True
        ).astype(jnp.float32),
        lax.psum_scatter(
            grad_w_up.astype(jnp.bfloat16), "dp", scatter_dimension=0, tiled=True
        ).astype(jnp.float32),
        lax.psum_scatter(
            grad_gate_down.astype(jnp.bfloat16), "dp", scatter_dimension=0, tiled=True
        ).astype(jnp.float32),
        lax.psum_scatter(
            grad_gate_up.astype(jnp.bfloat16), "dp", scatter_dimension=0, tiled=True
        ).astype(jnp.float32),
        lax.psum_scatter(
            grad_w_down.astype(jnp.bfloat16), "dp", scatter_dimension=0, tiled=True
        ).astype(jnp.float32),
        lax.psum_scatter(
            grad_w_proj.astype(jnp.bfloat16), "dp", scatter_dimension=0, tiled=True
        ).astype(jnp.float32),
        lax.psum_scatter(
            grad_gain_mamba.astype(jnp.bfloat16), "dp", scatter_dimension=0, tiled=True
        ).astype(jnp.float32),
        lax.psum_scatter(
            grad_w_in_gate.astype(jnp.bfloat16), "dp", scatter_dimension=0, tiled=True
        ).astype(jnp.float32),
        lax.psum_scatter(
            grad_w_in_main.astype(jnp.bfloat16), "dp", scatter_dimension=0, tiled=True
        ).astype(jnp.float32),
        lax.psum_scatter(
            grad_w_in_state.astype(jnp.bfloat16), "dp", scatter_dimension=0, tiled=True
        ).astype(jnp.float32),
        lax.psum_scatter(
            grad_w_in_step.astype(jnp.bfloat16), "dp", scatter_dimension=0, tiled=True
        ).astype(jnp.float32),
        lax.psum_scatter(
            grad_conv_main.astype(jnp.bfloat16), "dp", scatter_dimension=0, tiled=True
        ).astype(jnp.float32),
        lax.psum_scatter(
            grad_conv_main_bias.astype(jnp.bfloat16), "dp", scatter_dimension=0, tiled=True
        ).astype(jnp.float32),
        lax.psum_scatter(
            grad_conv_state.astype(jnp.bfloat16), "dp", scatter_dimension=0, tiled=True
        ).astype(jnp.float32),
        lax.psum_scatter(
            grad_conv_state_bias.astype(jnp.bfloat16), "dp", scatter_dimension=0, tiled=True
        ).astype(jnp.float32),
        lax.psum_scatter(
            grad_gain_gated.astype(jnp.bfloat16), "dp", scatter_dimension=0, tiled=True
        ).astype(jnp.float32),
        lax.psum_scatter(
            grad_w_mamba_out.astype(jnp.bfloat16), "dp", scatter_dimension=0, tiled=True
        ).astype(jnp.float32),
    )
    block_shards = tuple(joined[:7])
    mamba_shards = tuple(joined[7:])
    attn_grad = narrow(grad_shared + grad_first)
    grad_w_attn_out = trans_times(attn_grad, attended_low)
    attended_grad = narrow(times_right(attn_grad, w_attn_out)).reshape(
        length, heads_here, HEAD_SIZE
    )
    grad_query_rot, grad_key_rot, grad_value = attend_backward(
        query_rot, key_rot, value_low, allowed, log_total, attended_grad
    )
    query_grad = narrow(query_turn_back(grad_query_rot)[0].reshape(length, -1))
    key_grad = narrow(key_turn_back(grad_key_rot)[0].reshape(length, -1))
    value_grad = narrow(grad_value.reshape(length, -1))
    grad_w_query = trans_times(normed_cat, query_grad)
    grad_w_key = trans_times(normed_cat, key_grad)
    grad_w_value = trans_times(normed_cat, value_grad)
    grad_query_up = trans_times(query_low, query_grad)
    cat_part = (
        times_trans(query_grad, w_query)
        + times_trans(key_grad, w_key)
        + times_trans(value_grad, w_value)
    )
    cat_sum, query_low_grad = (
        lax.psum(cat_part.astype(jnp.bfloat16), "tensor").astype(jnp.float32),
        lax.psum(times_trans(query_grad, query_up).astype(jnp.bfloat16), "tensor").astype(
            jnp.float32
        ),
    )
    query_low_grad = narrow(query_low_grad)
    grad_query_down = trans_times(normed_cat, query_low_grad)
    grad_concat, grad_gain_attn = cat_back(cat_sum + times_trans(query_low_grad, query_down))
    grad_hidden = grad_concat[:, :D] + grad_first + grad_middle
    grad_embedding = grad_concat[:, D:]
    attn_shards = (
        lax.psum_scatter(
            grad_gain_attn.astype(jnp.bfloat16), "dp", scatter_dimension=0, tiled=True
        ).astype(jnp.float32),
        lax.psum_scatter(
            grad_w_query.astype(jnp.bfloat16), "dp", scatter_dimension=0, tiled=True
        ).astype(jnp.float32),
        lax.psum_scatter(
            grad_w_key.astype(jnp.bfloat16), "dp", scatter_dimension=0, tiled=True
        ).astype(jnp.float32),
        lax.psum_scatter(
            grad_w_value.astype(jnp.bfloat16), "dp", scatter_dimension=0, tiled=True
        ).astype(jnp.float32),
        lax.psum_scatter(
            grad_query_down.astype(jnp.bfloat16), "dp", scatter_dimension=0, tiled=True
        ).astype(jnp.float32),
        lax.psum_scatter(
            grad_query_up.astype(jnp.bfloat16), "dp", scatter_dimension=0, tiled=True
        ).astype(jnp.float32),
        lax.psum_scatter(
            grad_w_attn_out.astype(jnp.bfloat16), "dp", scatter_dimension=0, tiled=True
        ).astype(jnp.float32),
    )
    head_sums = lax.psum((grad_step_bias, grad_decay_log, grad_skip_scale), "dp")
    return (
        narrow(final_sum),
        loss_mid,
        loss_out,
        grad_hidden,
        grad_embedding,
        attn_shards[0],
        attn_shards[1],
        attn_shards[2],
        attn_shards[3],
        attn_shards[4],
        attn_shards[5],
        attn_shards[6],
        block_shards[0],
        block_shards[1],
        block_shards[2],
        block_shards[3],
        block_shards[4],
        block_shards[5],
        block_shards[6],
        mamba_shards[0],
        mamba_shards[1],
        mamba_shards[2],
        mamba_shards[3],
        mamba_shards[4],
        mamba_shards[5],
        mamba_shards[6],
        mamba_shards[7],
        mamba_shards[8],
        mamba_shards[9],
        mamba_shards[10],
        head_sums[0],
        head_sums[1],
        head_sums[2],
    )


def solution(mesh):
    in_specs = (
        P("dp", None),
        P("dp", None),
        P("dp", None),
        P("dp", None),
        P("dp"),
        P("dp"),
        P("dp"),
        P("dp"),
        P("dp", "tensor"),
        P("dp", "tensor"),
        P("dp", "tensor"),
        P("dp", None),
        P("dp", "tensor"),
        P("dp", "tensor"),
        P("dp"),
        P("dp", "tensor"),
        P("dp", "tensor"),
        P("dp", None),
        P("dp", "tensor"),
        P("dp", "tensor"),
        P("dp", "tensor"),
        P("dp"),
        P("dp", "tensor"),
        P("dp", "tensor"),
        P("dp", None),
        P("dp", "tensor"),
        P(("tensor", "dp"), None),
        P(("tensor", "dp")),
        P("dp", None),
        P("dp"),
        P(("tensor", "dp")),
        P("dp", "tensor"),
        P("tensor"),
        P("tensor"),
        P("tensor"),
    )
    out_specs = (
        P("dp", None),
        P(),
        P(),
        P("dp", None),
        P("dp", None),
        P("dp"),
        P("dp", "tensor"),
        P("dp", "tensor"),
        P("dp", "tensor"),
        P("dp", None),
        P("dp", "tensor"),
        P("dp", "tensor"),
        P("dp"),
        P("dp", "tensor"),
        P("dp", "tensor"),
        P("dp", None),
        P("dp", "tensor"),
        P("dp", "tensor"),
        P("dp", "tensor"),
        P("dp"),
        P("dp", "tensor"),
        P("dp", "tensor"),
        P("dp", None),
        P("dp", "tensor"),
        P(("tensor", "dp"), None),
        P(("tensor", "dp")),
        P("dp", None),
        P("dp"),
        P(("tensor", "dp")),
        P("dp", "tensor"),
        P("tensor"),
        P("tensor"),
        P("tensor"),
    )
    return jax.shard_map(body, mesh=mesh, in_specs=in_specs, out_specs=out_specs, check_vma=False)
```

profile of v0, /device:TPU:0, one launch (start us, length us, event | category | flops | bytes accessed | tf_op | source)
XLA Modules:
  0.0 3788.4 jit_solution(8582137441952307349)
XLA Ops:
  12.0 27.8 all-gather
  40.8 31.5 all_gather.82
  85.3 94.4 %all-gather.27.cloned.1.call-done = bf16[4096,1024]{1,0:T(8,128)(2,1)} async-done(((bf16[512,1024]{1,0:T(8,128)(2,1)}), bf16[4096,1024]{1,0:T(8,128)(2,1)}) %all-gather.27.cloned.1.call-update) | async-done | bytes 8388624 | tf_op jit(solution)/shard_map/all_gather | solution.py:191
  189.6 115.3 %all-gather.23.cloned.1.call-done = bf16[4096,1024]{1,0:T(8,128)(2,1)} async-done(((bf16[512,1024]{1,0:T(8,128)(2,1)}), bf16[4096,1024]{1,0:T(8,128)(2,1)}) %all-gather.23.cloned.1.call-update) | async-done | bytes 8388624 | tf_op jit(solution)/shard_map/all_gather | solution.py:190
  325.9 104.1 %all-gather.21.cloned.1.call-done = bf16[4096,1024]{1,0:T(8,128)(2,1)} async-done(((bf16[512,1024]{1,0:T(8,128)(2,1)}), bf16[4096,1024]{1,0:T(8,128)(2,1)}) %all-gather.21.cloned.1.call-update) | async-done | bytes 8388624 | tf_op jit(solution)/shard_map/all_gather | solution.py:192
  430.1 9.3 fusion.39
  440.4 15.5 fusion.35
  455.9 47.8 %all-gather.29.cloned.1.call-done = bf16[2048,1024]{1,0:T(8,128)(2,1)} async-done(((bf16[256,1024]{1,0:T(8,128)(2,1)}), bf16[2048,1024]{1,0:T(8,128)(2,1)}) %all-gather.29.cloned.1.call-update) | async-done | bytes 4194320 | tf_op jit(solution)/shard_map/all_gather | solution.py:195
  512.6 17.8 all-gather.1
  530.5 31.6 all_gather.87
  562.0 31.4 all_gather.88
  600.5 121.1 %all-gather.31.cloned.1.call-done = bf16[2048,2048]{1,0:T(8,128)(2,1)} async-done(((bf16[256,2048]{1,0:T(8,128)(2,1)}), bf16[2048,2048]{1,0:T(8,128)(2,1)}) %all-gather.31.cloned.1.call-update) | async-done | bytes 8388624 | tf_op jit(solution)/shard_map/all_gather | solution.py:197
  731.9 115.2 %all-gather.33.cloned.1.call-done = bf16[2048,2048]{1,0:T(8,128)(2,1)} async-done(((bf16[256,2048]{1,0:T(8,128)(2,1)}), bf16[2048,2048]{1,0:T(8,128)(2,1)}) %all-gather.33.cloned.1.call-update) | async-done | bytes 8388624 | tf_op jit(solution)/shard_map/all_gather | solution.py:198
  847.1 13.1 multiply_convert_fusion.7
  860.2 112.4 %all-gather.35.cloned.1.call-done = bf16[2048,2048]{1,0:T(8,128)(2,1)} async-done(((bf16[256,2048]{1,0:T(8,128)(2,1)}), bf16[2048,2048]{1,0:T(8,128)(2,1)}) %all-gather.35.cloned.1.call-update) | async-done | bytes 8388624 | tf_op jit(solution)/shard_map/all_gather | solution.py:201
  972.6 10.7 fusion.116
  984.1 42.1 %reduce-scatter.25.cloned.1.call-done = f32[512,512]{1,0:T(8,128)} async-done(((f32[512,2048]{1,0:T(8,128)}), f32[512,512]{1,0:T(8,128)}) %reduce-scatter.25.cloned.1.call-update) | async-done | bytes 1048592 | tf_op jit(solution)/shard_map/reduce_scatter | solution.py:250
  1027.9 49.8 %all-gather.37.cloned.1.call-done = bf16[2048,512]{1,0:T(8,128)(2,1)} async-done(((bf16[256,512]{1,0:T(8,128)(2,1)}), bf16[2048,512]{1,0:T(8,128)(2,1)}) %all-gather.37.cloned.1.call-update) | async-done | bytes 2097168 | tf_op jit(solution)/shard_map/all_gather | solution.py:202
  1085.2 18.1 all-gather.4
  1106.8 17.3 all-reduce.27
  1124.7 17.9 all-gather.2
  1142.7 16.4 all-gather.5
  1159.6 18.1 all-gather.3
  1177.8 16.6 all_gather.93
  1194.4 31.0 all_gather.96
  1232.7 10.7 all-gather.39.cloned.1.call-done
  1256.1 28.0 all-gather.41.cloned.1.call-done
  1298.0 60.4 %all-gather.43.cloned.1.call-done = bf16[2048,1024]{1,0:T(8,128)(2,1)} async-done(((bf16[256,1024]{1,0:T(8,128)(2,1)}), bf16[2048,1024]{1,0:T(8,128)(2,1)}) %all-gather.43.cloned.1.call-update) | async-done | bytes 4194320 | tf_op jit(solution)/shard_map/all_gather | solution.py:204
  1372.1 60.2 %all-gather.45.cloned.1.call-done = bf16[2048,1024]{1,0:T(8,128)(2,1)} async-done(((bf16[256,1024]{1,0:T(8,128)(2,1)}), bf16[2048,1024]{1,0:T(8,128)(2,1)}) %all-gather.45.cloned.1.call-update) | async-done | bytes 4194320 | tf_op jit(solution)/shard_map/all_gather | solution.py:213
  1439.7 19.5 psum.124
  1459.9 29.0 all-reduce.50.cloned.1.call-done
  1513.3 13.3 fusion.2
  1564.2 60.9 %all-reduce.56.cloned.1.call-done = (bf16[512,2048]{1,0:T(8,128)(2,1)}, bf16[512,512]{1,0:T(8,128)(2,1)}) async-done(((bf16[512,2048]{1,0:T(8,128)(2,1)}, bf16[512,512]{1,0:T(8,128)(2,1)}), (bf16[512,2048]{1,0:T(8,128)(2,1)}, bf16[512,512]{1,0:T(8,128)(2,1)})) %all-reduce.56.cloned.1.call-update) | async-done | bytes 2621456 | tf_op jit(solution)/shard_map/psum | solution.py:344
  1643.7 22.7 all-gather.47.cloned.1.call-done
  1666.5 12.1 multiply_convert_fusion.5
  1687.5 9.6 add_convert_fusion.2
  1697.2 53.8 %all-reduce.54.cloned.1.call-done = (bf16[512,2048]{1,0:T(8,128)(2,1)}, bf16[512,128]{1,0:T(8,128)(2,1)}) async-done(((bf16[512,2048]{1,0:T(8,128)(2,1)}, bf16[512,128]{1,0:T(8,128)(2,1)}), (bf16[512,2048]{1,0:T(8,128)(2,1)}, bf16[512,128]{1,0:T(8,128)(2,1)})) %all-reduce.54.cloned.1.call-update) | async-done | bytes 2228240 | tf_op jit(solution)/shard_map/psum | solution.py:372
  1793.0 10.6 fusion.123
  1803.6 10.4 fusion.124
  1814.0 12.3 add_convert_fusion
  1863.1 51.4 %all-reduce.52.cloned.1.call-done = (bf16[512,4096]{1,0:T(8,128)(2,1)}, bf16[512,128]{1,0:T(8,128)(2,1)}) async-done(((bf16[512,4096]{1,0:T(8,128)(2,1)}, bf16[512,128]{1,0:T(8,128)(2,1)}), (bf16[512,4096]{1,0:T(8,128)(2,1)}, bf16[512,128]{1,0:T(8,128)(2,1)})) %all-reduce.52.cloned.1.call-update) | async-done | bytes 4325392 | tf_op jit(solution)/shard_map/psum | solution.py:459
  1926.8 10.1 convolution_convert_fusion
  1988.7 47.6 %reduce-scatter.57.cloned.1.call-done = bf16[256,16]{0,1:T(8,128)(2,1)} async-done(((bf16[2048,16]{0,1:T(8,128)(2,1)}), bf16[256,16]{0,1:T(8,128)(2,1)}) %reduce-scatter.57.cloned.1.call-update) | async-done | bytes 8208 | tf_op jit(solution)/shard_map/reduce_scatter | solution.py:414
  2037.6 20.1 all-reduce.34
  2059.1 40.8 %reduce-scatter.63.cloned.1.call-done = bf16[32,4]{1,0:T(8,128)(2,1)} async-done(((bf16[256,4]{1,0:T(8,128)(2,1)}), bf16[32,4]{1,0:T(8,128)(2,1)}) %reduce-scatter.63.cloned.1.call-update) | async-done | bytes 272
  2101.2 65.2 %reduce-scatter.55.cloned.1.call-done = bf16[256,256]{1,0:T(8,128)(2,1)} async-done(((bf16[2048,256]{1,0:T(8,128)(2,1)}), bf16[256,256]{1,0:T(8,128)(2,1)}) %reduce-scatter.55.cloned.1.call-update) | async-done | bytes 131088 | tf_op jit(solution)/shard_map/reduce_scatter | solution.py:411
  2168.0 69.7 %reduce-scatter.49.cloned.1.call-done = bf16[256,512]{1,0:T(8,128)(2,1)} async-done(((bf16[2048,512]{1,0:T(8,128)(2,1)}), bf16[256,512]{1,0:T(8,128)(2,1)}) %reduce-scatter.49.cloned.1.call-update) | async-done | bytes 262160 | tf_op jit(solution)/shard_map/reduce_scatter | solution.py:399
  2239.6 62.7 %reduce-scatter.45.cloned.1.call-done = bf16[16,2048]{1,0:T(8,128)(2,1)} async-done(((bf16[128,2048]{1,0:T(8,128)(2,1)}), bf16[16,2048]{1,0:T(8,128)(2,1)}) %reduce-scatter.45.cloned.1.call-update) | async-done | bytes 65552 | tf_op jit(solution)/shard_map/reduce_scatter | solution.py:393
  2303.8 62.7 %reduce-scatter.35.cloned.1.call-done = bf16[16,1024]{1,0:T(8,128)(2,1)} async-done(((bf16[128,1024]{1,0:T(8,128)(2,1)}), bf16[16,1024]{1,0:T(8,128)(2,1)}) %reduce-scatter.35.cloned.1.call-update) | async-done | bytes 32784 | tf_op jit(solution)/shard_map/reduce_scatter | solution.py:485
  2367.8 63.6 %reduce-scatter.43.cloned.1.call-done = bf16[256,128]{1,0:T(8,128)(2,1)} async-done(((bf16[2048,128]{1,0:T(8,128)(2,1)}), bf16[256,128]{1,0:T(8,128)(2,1)}) %reduce-scatter.43.cloned.1.call-update) | async-done | bytes 65552 | tf_op jit(solution)/shard_map/reduce_scatter | solution.py:390
  2441.2 37.7 all-reduce.35
  2482.6 9.9 add_add_fusion
  2492.5 10.4 fusion.107
  2503.0 20.1 reduce-scatter.59.cloned.1.call-done
  2525.2 89.2 %reduce-scatter.51.cloned.1.call-done = bf16[256,1024]{1,0:T(8,128)(2,1)} async-done(((bf16[2048,1024]{1,0:T(8,128)(2,1)}), bf16[256,1024]{1,0:T(8,128)(2,1)}) %reduce-scatter.51.cloned.1.call-update) | async-done | bytes 524304 | tf_op jit(solution)/shard_map/reduce_scatter | solution.py:405
  2616.5 89.6 %reduce-scatter.53.cloned.1.call-done = bf16[256,1024]{1,0:T(8,128)(2,1)} async-done(((bf16[2048,1024]{1,0:T(8,128)(2,1)}), bf16[256,1024]{1,0:T(8,128)(2,1)}) %reduce-scatter.53.cloned.1.call-update) | async-done | bytes 524304 | tf_op jit(solution)/shard_map/reduce_scatter | solution.py:408
  2708.2 65.0 %reduce-scatter.33.cloned.1.call-done = bf16[512,128]{1,0:T(8,128)(2,1)} async-done(((bf16[4096,128]{1,0:T(8,128)(2,1)}), bf16[512,128]{1,0:T(8,128)(2,1)}) %reduce-scatter.33.cloned.1.call-update) | async-done | bytes 131088 | tf_op jit(solution)/shard_map/reduce_scatter | solution.py:482
  2774.8 89.4 %reduce-scatter.37.cloned.1.call-done = bf16[256,1024]{1,0:T(8,128)(2,1)} async-done(((bf16[2048,1024]{1,0:T(8,128)(2,1)}), bf16[256,1024]{1,0:T(8,128)(2,1)}) %reduce-scatter.37.cloned.1.call-update) | async-done | bytes 524304 | tf_op jit(solution)/shard_map/reduce_scatter | solution.py:488
  2866.3 150.3 %reduce-scatter.47.cloned.1.call-done = bf16[256,2048]{1,0:T(8,128)(2,1)} async-done(((bf16[2048,2048]{1,0:T(8,128)(2,1)}), bf16[256,2048]{1,0:T(8,128)(2,1)}) %reduce-scatter.47.cloned.1.call-update) | async-done | bytes 1048592 | tf_op jit(solution)/shard_map/reduce_scatter | solution.py:396
  3019.4 149.2 %reduce-scatter.39.cloned.1.call-done = bf16[256,2048]{1,0:T(8,128)(2,1)} async-done(((bf16[2048,2048]{1,0:T(8,128)(2,1)}), bf16[256,2048]{1,0:T(8,128)(2,1)}) %reduce-scatter.39.cloned.1.call-update) | async-done | bytes 1048592 | tf_op jit(solution)/shard_map/reduce_scatter | solution.py:384
  3171.4 148.8 %reduce-scatter.41.cloned.1.call-done = bf16[256,2048]{1,0:T(8,128)(2,1)} async-done(((bf16[2048,2048]{1,0:T(8,128)(2,1)}), bf16[256,2048]{1,0:T(8,128)(2,1)}) %reduce-scatter.41.cloned.1.call-update) | async-done | bytes 1048592 | tf_op jit(solution)/shard_map/reduce_scatter | solution.py:387
  3323.0 149.3 %reduce-scatter.27.cloned.1.call-done = bf16[512,1024]{1,0:T(8,128)(2,1)} async-done(((bf16[4096,1024]{1,0:T(8,128)(2,1)}), bf16[512,1024]{1,0:T(8,128)(2,1)}) %reduce-scatter.27.cloned.1.call-update) | async-done | bytes 1048592 | tf_op jit(solution)/shard_map/reduce_scatter | solution.py:473
  3475.1 148.8 %reduce-scatter.31.cloned.1.call-done = bf16[512,1024]{1,0:T(8,128)(2,1)} async-done(((bf16[4096,1024]{1,0:T(8,128)(2,1)}), bf16[512,1024]{1,0:T(8,128)(2,1)}) %reduce-scatter.31.cloned.1.call-update) | async-done | bytes 1048592 | tf_op jit(solution)/shard_map/reduce_scatter | solution.py:479
  3626.7 149.4 %reduce-scatter.29.cloned.1.call-done = bf16[512,1024]{1,0:T(8,128)(2,1)} async-done(((bf16[4096,1024]{1,0:T(8,128)(2,1)}), bf16[512,1024]{1,0:T(8,128)(2,1)}) %reduce-scatter.29.cloned.1.call-update) | async-done | bytes 1048592 | tf_op jit(solution)/shard_map/reduce_scatter | solution.py:476
  (564 shorter events, 422.4 us)
Async XLA Ops:
  7.2 74.3 %all-gather.25.cloned.1.call-start = ((), (), s32[]{:S(2)}) async-start(), calls=%async_computation.22 | async-start | bytes 1179648 | tf_op jit(solution)/shard_map/all_gather | solution.py:193
  7.9 171.7 %all-gather.27.cloned.1.call-start = ((), (), s32[]{:S(2)}) async-start(), calls=%async_computation.23 | async-start | bytes 9437184 | tf_op jit(solution)/shard_map/all_gather | solution.py:191
  8.7 296.2 %all-gather.23.cloned.1.call-start = ((), (), s32[]{:S(2)}) async-start(), calls=%async_computation.21 | async-start | bytes 9437184 | tf_op jit(solution)/shard_map/all_gather | solution.py:190
  9.4 420.6 %all-gather.21.cloned.1.call-start = ((), (), s32[]{:S(2)}) async-start(), calls=%async_computation.20 | async-start | bytes 9437184 | tf_op jit(solution)/shard_map/all_gather | solution.py:192
  10.0 493.6 %all-gather.29.cloned.1.call-start = ((), (), s32[]{:S(2)}) async-start(), calls=%async_computation.24 | async-start | bytes 4718592 | tf_op jit(solution)/shard_map/all_gather | solution.py:195
  10.6 583.6 %all-reduce.46.cloned.1.call-start = ((), (), s32[]{:S(2)}) async-start(), calls=%async_computation.25 | async-start | bytes 8388608 | tf_op jit(solution)/shard_map/psum | solution.py:241
  40.8 1062.5 %copy-start.33 = (pred[512,512]{0,1:T(8,128)(4,1)}, pred[512,512]{0,1:T(8,128)(4,1)S(1)}, u32[]{:S(2)}) copy-start(pred[512,512]{0,1:T(8,128)(4,1)S(1)} %fusion.47) | copy-start | bytes 786436
  72.3 241.0 %copy-start.44 = (bf16[128,1024]{1,0:T(8,128)(2,1)}, bf16[128,1024]{1,0:T(8,128)(2,1)S(1)}, u32[]{:S(2)}) copy-start(bf16[128,1024]{1,0:T(8,128)(2,1)S(1)} %all_gather.82) | copy-start | bytes 786436
  78.8 237.6 %copy-start.40 = (f32[512,64]{1,0:T(8,128)}, f32[512,64]{1,0:T(8,128)S(1)}, u32[]{:S(2)}) copy-start(f32[512,64]{1,0:T(8,128)S(1)} %get-tuple-element.129) | copy-start | bytes 393220
  78.8 237.6 %copy-start.42 = (f32[512,64]{1,0:T(8,128)}, f32[512,64]{1,0:T(8,128)S(1)}, u32[]{:S(2)}) copy-start(f32[512,64]{1,0:T(8,128)S(1)} %get-tuple-element.130) | copy-start | bytes 393220
  85.3 228.1 %copy-start.62 = (bf16[512,128]{1,0:T(8,128)(2,1)}, bf16[512,128]{1,0:T(8,128)(2,1)S(1)}, u32[]{:S(2)}) copy-start(bf16[512,128]{1,0:T(8,128)(2,1)S(1)} %convolution_convert_fusion.23) | copy-start | bytes 393220
  320.9 118.5 %copy-start.67 = (f32[8,512]{1,0:T(8,128)}, f32[8,512]{1,0:T(8,128)S(1)}, u32[]{:S(2)}) copy-start(f32[8,512]{1,0:T(8,128)S(1)} %get-tuple-element.136) | copy-start | bytes 49156
  325.9 113.5 %copy-start.74 = (f32[8,512]{1,0:T(8,128)}, f32[8,512]{1,0:T(8,128)S(1)}, u32[]{:S(2)}) copy-start(f32[8,512]{1,0:T(8,128)S(1)} %fusion.5) | copy-start | bytes 49156
  510.3 211.4 %all-gather.31.cloned.1.call-start = ((), (), s32[]{:S(2)}) async-start(), calls=%async_computation.26 | async-start | bytes 9437184 | tf_op jit(solution)/shard_map/all_gather | solution.py:197
  511.0 336.1 %all-gather.33.cloned.1.call-start = ((), (), s32[]{:S(2)}) async-start(), calls=%async_computation.27 | async-start | bytes 9437184 | tf_op jit(solution)/shard_map/all_gather | solution.py:198
  511.8 460.9 %all-gather.35.cloned.1.call-start = ((), (), s32[]{:S(2)}) async-start(), calls=%async_computation.28 | async-start | bytes 9437184 | tf_op jit(solution)/shard_map/all_gather | solution.py:201
  512.5 513.7 %reduce-scatter.25.cloned.1.call-start = ((), (), s32[]{:S(2)}) async-start(), calls=%async_computation.29 | async-start | bytes 5242880 | tf_op jit(solution)/shard_map/reduce_scatter | solution.py:250
  530.4 67.3 %copy-start.72 = (f32[8,1,256]{2,1,0:T(1,128)}, f32[8,1,256]{2,1,0:T(1,128)S(1)}, u32[]{:S(2)}) copy-start(f32[8,1,256]{2,1,0:T(1,128)S(1)} %convert_element_type.507) | copy-start | bytes 24580
  593.4 135.8 %copy-start.38 = (bf16[128,2048]{1,0:T(8,128)(2,1)}, bf16[128,2048]{1,0:T(8,128)(2,1)S(1)}, u32[]{:S(2)}) copy-start(bf16[128,2048]{1,0:T(8,128)(2,1)S(1)} %all_gather.88) | copy-start | bytes 1572868
  600.5 128.7 %copy-start.53 = (bf16[512,128]{1,0:T(8,128)(2,1)}, bf16[512,128]{1,0:T(8,128)(2,1)S(1)}, u32[]{:S(2)}) copy-start(bf16[512,128]{1,0:T(8,128)(2,1)S(1)} %convolution_convert_fusion.22) | copy-start | bytes 393220
  983.4 94.3 %all-gather.37.cloned.1.call-start = ((), (), s32[]{:S(2)}) async-start(), calls=%async_computation.30 | async-start | bytes 2359296 | tf_op jit(solution)/shard_map/all_gather | solution.py:202
  984.1 242.1 %all-reduce.48.cloned.1.call-start = ((), (), s32[]{:S(2)}) async-start(), calls=%async_computation.31 | async-start | bytes 8388608 | tf_op jit(solution)/shard_map/psum | solution.py:255
  1082.6 95.2 %copy-start.125 = (bf16[128,4]{0,1:T(4,128)(2,1)S(1)}, bf16[128,4]{0,1:T(4,128)(2,1)}, u32[]{:S(2)}) copy-start(bf16[128,4]{0,1:T(4,128)(2,1)} %param.61) | copy-start | bytes 3076
  1082.6 111.8 %copy-start.114 = (bf16[256,16]{0,1:T(8,128)(2,1)S(1)}, bf16[256,16]{0,1:T(8,128)(2,1)}, u32[]{:S(2)}) copy-start(bf16[256,16]{0,1:T(8,128)(2,1)} %param.60) | copy-start | bytes 24580
  1082.6 142.8 %copy-start.140 = (bf16[16]{0:T(256)(128)(2,1)S(1)}, bf16[16]{0:T(256)(128)(2,1)}, u32[]{:S(2)}) copy-start(bf16[16]{0:T(256)(128)(2,1)} %param.68) | copy-start | bytes 100
  1082.6 142.8 %copy-start.86 = (s32[512]{0:T(512)S(1)}, s32[512]{0:T(512)}, u32[]{:S(2)}) copy-start(s32[512]{0:T(512)} %param.39) | copy-start | bytes 6148
  1082.7 160.7 %all-gather.39.cloned.1.call-start = ((), (), s32[]{:S(2)}) async-start(), calls=%async_computation.32 | async-start | bytes 4718592 | tf_op jit(solution)/shard_map/all_gather | solution.py:205
  1083.4 200.6 %all-gather.41.cloned.1.call-start = ((), (), s32[]{:S(2)}) async-start(), calls=%async_computation.33 | async-start | bytes 1179648 | tf_op jit(solution)/shard_map/all_gather | solution.py:206
  1084.0 274.4 %all-gather.43.cloned.1.call-start = ((), (), s32[]{:S(2)}) async-start(), calls=%async_computation.34 | async-start | bytes 4718592 | tf_op jit(solution)/shard_map/all_gather | solution.py:204
  1084.6 347.7 %all-gather.45.cloned.1.call-start = ((), (), s32[]{:S(2)}) async-start(), calls=%async_computation.35 | async-start | bytes 4718592 | tf_op jit(solution)/shard_map/all_gather | solution.py:213
  1085.2 403.7 %all-reduce.50.cloned.1.call-start = ((), (), s32[]{:S(2)}) async-start(), calls=%async_computation.36 | async-start | bytes 4194304 | tf_op jit(solution)/shard_map/psum | solution.py:291
  1229.4 129.0 %copy-start.14 = (bf16[512,2048]{1,0:T(8,128)(2,1)}, bf16[512,2048]{1,0:T(8,128)(2,1)S(1)}, u32[]{:S(2)}) copy-start(bf16[512,2048]{1,0:T(8,128)(2,1)S(1)} %multiply_convert_fusion.6) | copy-start | bytes 6291460
  1298.0 134.3 %copy-start.104 = (f32[8,1,128]{2,1,0:T(1,128)S(1)}, f32[8,1,128]{2,1,0:T(1,128)}, u32[]{:S(2)}) copy-start(f32[8,1,128]{2,1,0:T(1,128)} %convert_element_type.511) | copy-start | bytes 12292
  1439.0 186.0 %all-reduce.56.cloned.1.call-start = ((), (), s32[]{:S(2)}) async-start(), calls=%async_computation.59 | async-start | bytes 5242880 | tf_op jit(solution)/shard_map/psum | solution.py:344
  1564.1 65.6 %copy-start.111 = (f32[256,1]{0,1:T(1,128)S(1)}, f32[256,1]{0,1:T(1,128)}, u32[]{:S(2)}) copy-start(f32[256,1]{0,1:T(1,128)} %get-tuple-element.127) | copy-start | bytes 3076
  1564.1 65.6 %copy-start.112 = (f32[256,1]{0,1:T(1,128)S(1)}, f32[256,1]{0,1:T(1,128)}, u32[]{:S(2)}) copy-start(f32[256,1]{0,1:T(1,128)} %get-tuple-element.128) | copy-start | bytes 3076
  1564.1 65.9 %copy-start.109 = (f32[256,1]{0,1:T(1,128)S(1)}, f32[256,1]{0,1:T(1,128)}, u32[]{:S(2)}) copy-start(f32[256,1]{0,1:T(1,128)} %copy-done.108) | copy-start | bytes 3076
  1564.1 66.1 %copy-start.52 = (bf16[512,2048]{1,0:T(8,128)(2,1)S(1)}, bf16[512,2048]{1,0:T(8,128)(2,1)}, u32[]{:S(2)}) copy-start(bf16[512,2048]{1,0:T(8,128)(2,1)} %param.37) | copy-start | bytes 6291460
  1564.1 102.4 %all-gather.47.cloned.1.call-start = ((), (), s32[]{:S(2)}) async-start(), calls=%async_computation.37 | async-start | bytes 2621440 | tf_op jit(solution)/shard_map/all_gather | solution.py:359
  1643.7 107.2 %all-reduce.54.cloned.1.call-start = ((), (), s32[]{:S(2)}) async-start(), calls=%async_computation.58 | async-start | bytes 4456448 | tf_op jit(solution)/shard_map/psum | solution.py:372
  1697.1 217.4 %all-reduce.52.cloned.1.call-start = ((), (), s32[]{:S(2)}) async-start(), calls=%async_computation.57 | async-start | bytes 8650752 | tf_op jit(solution)/shard_map/psum | solution.py:459
  1826.5 160.8 %reduce-scatter.61.cloned.1.call-start = ((), (), s32[]{:S(2)}) async-start(), calls=%async_computation.55 | async-start | bytes 294912
  1828.0 208.3 %reduce-scatter.57.cloned.1.call-start = ((), (), s32[]{:S(2)}) async-start(), calls=%async_computation.53 | async-start | bytes 73728 | tf_op jit(solution)/shard_map/reduce_scatter | solution.py:414
  1829.1 270.7 %reduce-scatter.63.cloned.1.call-start = ((), (), s32[]{:S(2)}) async-start(), calls=%async_computation.56 | async-start | bytes 73728
  1830.0 336.4 %reduce-scatter.55.cloned.1.call-start = ((), (), s32[]{:S(2)}) async-start(), calls=%async_computation.52 | async-start | bytes 1179648 | tf_op jit(solution)/shard_map/reduce_scatter | solution.py:411
  1831.8 406.0 %reduce-scatter.49.cloned.1.call-start = ((), (), s32[]{:S(2)}) async-start(), calls=%async_computation.49 | async-start | bytes 2359296 | tf_op jit(solution)/shard_map/reduce_scatter | solution.py:399
  1837.1 465.1 %reduce-scatter.45.cloned.1.call-start = ((), (), s32[]{:S(2)}) async-start(), calls=%async_computation.47 | async-start | bytes 589824 | tf_op jit(solution)/shard_map/reduce_scatter | solution.py:393
  1840.3 526.1 %reduce-scatter.35.cloned.1.call-start = ((), (), s32[]{:S(2)}) async-start(), calls=%async_computation.42 | async-start | bytes 294912 | tf_op jit(solution)/shard_map/reduce_scatter | solution.py:485
  1841.6 589.8 %reduce-scatter.43.cloned.1.call-start = ((), (), s32[]{:S(2)}) async-start(), calls=%async_computation.46 | async-start | bytes 589824 | tf_op jit(solution)/shard_map/reduce_scatter | solution.py:390
  1843.2 679.8 %reduce-scatter.59.cloned.1.call-start = ((), (), s32[]{:S(2)}) async-start(), calls=%async_computation.54 | async-start | bytes 4718592 | tf_op jit(solution)/shard_map/reduce_scatter | solution.py:432
  1850.3 764.0 %reduce-scatter.51.cloned.1.call-start = ((), (), s32[]{:S(2)}) async-start(), calls=%async_computation.50 | async-start | bytes 4718592 | tf_op jit(solution)/shard_map/reduce_scatter | solution.py:405
  1856.6 849.5 %reduce-scatter.53.cloned.1.call-start = ((), (), s32[]{:S(2)}) async-start(), calls=%async_computation.51 | async-start | bytes 4718592 | tf_op jit(solution)/shard_map/reduce_scatter | solution.py:408
  1863.1 910.1 %reduce-scatter.33.cloned.1.call-start = ((), (), s32[]{:S(2)}) async-start(), calls=%async_computation.41 | async-start | bytes 1179648 | tf_op jit(solution)/shard_map/reduce_scatter | solution.py:482
  1919.0 945.2 %reduce-scatter.37.cloned.1.call-start = ((), (), s32[]{:S(2)}) async-start(), calls=%async_computation.43 | async-start | bytes 4718592 | tf_op jit(solution)/shard_map/reduce_scatter | solution.py:488
  1926.5 1090.1 %reduce-scatter.47.cloned.1.call-start = ((), (), s32[]{:S(2)}) async-start(), calls=%async_computation.48 | async-start | bytes 9437184 | tf_op jit(solution)/shard_map/reduce_scatter | solution.py:396
  1936.9 1231.7 %reduce-scatter.39.cloned.1.call-start = ((), (), s32[]{:S(2)}) async-start(), calls=%async_computation.44 | async-start | bytes 9437184 | tf_op jit(solution)/shard_map/reduce_scatter | solution.py:384
  1945.5 1374.7 %reduce-scatter.41.cloned.1.call-start = ((), (), s32[]{:S(2)}) async-start(), calls=%async_computation.45 | async-start | bytes 9437184 | tf_op jit(solution)/shard_map/reduce_scatter | solution.py:387
  1953.9 1518.4 %reduce-scatter.27.cloned.1.call-start = ((), (), s32[]{:S(2)}) async-start(), calls=%async_computation.38 | async-start | bytes 9437184 | tf_op jit(solution)/shard_map/reduce_scatter | solution.py:473
  1963.0 1660.9 %reduce-scatter.31.cloned.1.call-start = ((), (), s32[]{:S(2)}) async-start(), calls=%async_computation.40 | async-start | bytes 9437184 | tf_op jit(solution)/shard_map/reduce_scatter | solution.py:479
  1973.3 1802.7 %reduce-scatter.29.cloned.1.call-start = ((), (), s32[]{:S(2)}) async-start(), calls=%async_computation.39 | async-start | bytes 9437184 | tf_op jit(solution)/shard_map/reduce_scatter | solution.py:476
  1983.6 449.3 %copy-start.70 = (f32[8,1,512]{2,1,0:T(1,128)S(1)}, f32[8,1,512]{2,1,0:T(1,128)}, u32[]{:S(2)}) copy-start(f32[8,1,512]{2,1,0:T(1,128)} %copy-done.69) | copy-start | bytes 49156
  1983.6 449.2 %copy-start.71 = (bf16[512,128]{1,0:T(8,128)(2,1)S(1)}, bf16[512,128]{1,0:T(8,128)(2,1)}, u32[]{:S(2)}) copy-start(bf16[512,128]{1,0:T(8,128)(2,1)} %get-tuple-element.70) | copy-start | bytes 393220
  1983.7 449.2 %copy-start.93 = (f32[512]{0:T(512)S(1)}, f32[512]{0:T(512)}, u32[]{:S(2)}) copy-start(f32[512]{0:T(512)} %copy-done.92) | copy-start | bytes 6148
  1983.7 449.2 %copy-start.134 = (bf16[4096,128]{1,0:T(8,128)(2,1)S(1)}, bf16[4096,128]{1,0:T(8,128)(2,1)}, u32[]{:S(2)}) copy-start(bf16[4096,128]{1,0:T(8,128)(2,1)} %all-gather.25.cloned.1.call-done) | copy-start | bytes 3145732
  (129 other events, 1691.5 us)
Sparse Core Ops, SparseCore 0:
  10.2 43.7 all-gather.24
  56.1 123.5 all-gather.26
  181.8 123.1 all-gather.22
  306.9 123.1 all-gather.20
  432.0 71.5 all-gather.28
  510.4 83.7 all-reduce.45
  596.5 125.0 all-gather.30
  724.0 123.1 all-gather.32
  849.5 123.1 all-gather.34
  983.5 42.6 reduce-scatter.24
  1028.3 49.2 all-gather.36
  1082.8 83.9 all-reduce.47
  1169.1 74.1 all-gather.38
  1245.6 38.4 all-gather.40
  1286.2 72.1 all-gather.42
  1360.6 71.6 all-gather.44
  1439.2 49.6 all-reduce.49
  1564.2 60.7 all-reduce.55
  1643.8 22.6 all-gather.46
  1697.2 53.6 all-reduce.53
  1826.6 87.8 all-reduce.51
  1918.4 61.3 reduce-scatter.60
  1983.5 52.7 reduce-scatter.56
  2039.6 60.2 reduce-scatter.62
  2103.8 62.5 reduce-scatter.54
  2170.8 66.9 reduce-scatter.48
  2241.3 60.8 reduce-scatter.44
  2306.2 60.2 reduce-scatter.34
  2370.4 60.9 reduce-scatter.42
  2435.3 87.6 reduce-scatter.58
  2526.7 87.6 reduce-scatter.50
  2618.4 87.6 reduce-scatter.52
  2709.9 63.2 reduce-scatter.32
  2777.3 86.9 reduce-scatter.36
  2867.8 148.7 reduce-scatter.46
  3020.6 148.0 reduce-scatter.38
  3172.1 148.0 reduce-scatter.40
  3324.2 148.0 reduce-scatter.26
  3475.8 148.0 reduce-scatter.30
  3627.9 148.0 reduce-scatter.28
where the time goes:
time: 3800 us; the launch traced here: 3790 us
  waiting for transfers between devices  2850 us (75%)
  matrix products  365 us (10%)
  blocking collectives  364 us (10%)
  other arithmetic  135 us (4%)
  local copies, waits for them, and re-layouts  47.1 us (1%)
    reduce_scatter x1, waiting for transfers between devices, body(): lax.psum_scatter(grad_w_down.astype(jnp.bfloat16), 'dp', scatter_dimensio...  150 us
    reduce_scatter x1, waiting for transfers between devices, body(): lax.psum_scatter(grad_w_key.astype(jnp.bfloat16), 'dp', scatter_dimension...  149 us
    reduce_scatter x1, waiting for transfers between devices, body(): lax.psum_scatter(grad_w_query.astype(jnp.bfloat16), 'dp', scatter_dimensi...  149 us
    reduce_scatter x1, waiting for transfers between devices, body(): lax.psum_scatter(grad_w_gate.astype(jnp.bfloat16), 'dp', scatter_dimensio...  149 us
    reduce_scatter x1, waiting for transfers between devices, body(): lax.psum_scatter(grad_w_value.astype(jnp.bfloat16), 'dp', scatter_dimensi...  149 us
    reduce_scatter x1, waiting for transfers between devices, body(): lax.psum_scatter(grad_w_up.astype(jnp.bfloat16), 'dp', scatter_dimension=...  149 us
    all_gather x1, waiting for transfers between devices, body(): lax.all_gather(w_gate, 'dp', axis=0, tiled=True)  121 us
    all_gather x1, waiting for transfers between devices, body(): lax.all_gather(w_query, 'dp', axis=0, tiled=True)  115 us
  transfers between devices with their start and end apart: 40, of which 37 were waited for; matrix products, arithmetic and copies ran while one was open for 8% of the time, Pallas kernels for 0%

commit v1 on v0

v1 whole, which is shorter than its diff:
```python
from functools import partial

import jax
import jax.numpy as jnp
from jax import lax
from jax.experimental import pallas as pl
from jax.experimental.pallas import tpu as pltpu
from jax.sharding import PartitionSpec as P

D = 2048
HEAD_SIZE = 128
STATE = 128
DI = 4096
HEAD_M = 64
PAIR = 2

eps = 1e-05
f32 = jnp.float32


def narrow(values):
    return values.astype(jnp.bfloat16)


def times_right(left, right, out=f32):
    return jnp.dot(left, right, preferred_element_type=f32).astype(out)


def times_trans(left, right, out=f32):
    return lax.dot_general(
        left, right, (((1,), (1,)), ((), ())), preferred_element_type=f32
    ).astype(out)


def trans_times(left, right, out=f32):
    return lax.dot_general(
        left, right, (((0,), (0,)), ((), ())), preferred_element_type=f32
    ).astype(out)


def rms_scale(values, gain):
    return values * lax.rsqrt(jnp.mean(values * values, axis=-1, keepdims=True) + eps) * gain


def flip(values, axis, bit):
    count = lax.axis_size(axis)
    return lax.ppermute(values, axis, [(i, i ^ bit) for i in range(count)])


def pick(values, axis, index):
    return lax.dynamic_index_in_dim(values, index, axis, keepdims=False)


def move_kernel(loads, stores, n_in, n_out, at_ref, *refs):
    ins, outs = refs[:n_in], refs[n_in : n_in + n_out]
    rooms, came, left = refs[n_in + n_out : -2], refs[-2], refs[-1]
    arrivals = []
    for i, (row, rows) in enumerate(loads):
        source = ins[i]
        if row is not None:
            source = source.at[pl.ds(pl.multiple_of(at_ref[row], rows), rows)]
        arrivals.append(pltpu.make_async_copy(source, rooms[i], came.at[i]))
        arrivals[-1].start()
    waiting, seen = [], set()
    for k, (i, column, width, out, row, to) in enumerate(stores):
        if i not in seen:
            arrivals[i].wait()
            seen.add(i)
        source = rooms[i].at[:, column : column + width]
        rows = loads[i][1]
        target = outs[out]
        if row is not None:
            target = target.at[pl.ds(pl.multiple_of(at_ref[row], rows), rows)]
        if isinstance(to, tuple):
            target = target.at[:, pl.ds(pl.multiple_of(at_ref[to[0]], width), width)]
        else:
            target = target.at[:, to : to + width]
        waiting.append(pltpu.make_async_copy(source, target, left.at[k]))
        waiting[-1].start()
    for store in waiting:
        store.wait()


def move(pieces, at, loads, stores, shapes):
    dtype = pieces[0].dtype
    at = jnp.stack(at).astype(jnp.int32) if at else jnp.zeros((1,), jnp.int32)
    return pl.pallas_call(
        partial(move_kernel, tuple(loads), tuple(stores), len(pieces), len(shapes)),
        out_shape=[jax.ShapeDtypeStruct(shape, dtype) for shape in shapes],
        in_specs=[pl.BlockSpec(memory_space=pltpu.SMEM)]
        + [pl.BlockSpec(memory_space=pl.ANY)] * len(pieces),
        out_specs=[pl.BlockSpec(memory_space=pl.ANY)] * len(shapes),
        scratch_shapes=[
            pltpu.VMEM((load[1], piece.shape[1]), dtype) for load, piece in zip(loads, pieces)
        ]
        + [pltpu.SemaphoreType.DMA((len(pieces),)), pltpu.SemaphoreType.DMA((len(stores),))],
    )(at, *pieces)


def place(pieces, starts, along, total, columns=None, widths=None):
    shape = list(pieces[0].shape)
    wide = shape[1]
    shape[along] = total
    if widths is not None:
        stores = []
        for i in range(len(pieces)):
            first = 0
            for out, width in enumerate(widths):
                stores.append((i, first, width, out, i, 0))
                first += width
        loads = [(None, piece.shape[0]) for piece in pieces]
        return move(pieces, starts, loads, stores, [(total, width) for width in widths])
    columns = columns or [(0, wide, 0)]
    stores = []
    for i in range(len(pieces)):
        for first, width, to in columns:
            if along == 0:
                stores.append((i, first, width, 0, i, to))
            else:
                stores.append((i, 0, wide, 0, None, (i,)))
    loads = [(None, piece.shape[0]) for piece in pieces]
    return move(pieces, starts, loads, stores, [tuple(shape)])[0]


class Place:
    def __init__(self):
        self.dp = lax.axis_index("dp")
        self.tensor = lax.axis_index("tensor")
        self.n_dp = lax.axis_size("dp")
        self.z = (self.dp // PAIR) % 2
        self.x = self.tensor // 2
        self.c = self.tensor % 2
        bits = [1 << k for k in range(self.n_dp.bit_length() - 1)]
        self.dp_bits = bits
        self.far_bits = [b for b in bits if b not in (1, PAIR)]
        self.pairs = [[i, i + 1] for i in range(0, self.n_dp, 2)]
        self.square = [
            [y + PAIR * z + 4 * far for y in (0, 1) for far in range(self.n_dp // 4)]
            for z in (0, 1)
        ]
        self.gates = {"pair": [], "far": []}
        self.marks = {}

    def dp_bit(self, bit):
        return (self.dp // bit) % 2


    def half(self, shard, which):
        width = shard.shape[1] // 2
        return lax.dynamic_slice_in_dim(shard, which * width, width, 1)

    def send(self, values, bit):
        gate = self.gates["pair" if bit == PAIR else "far"]
        if gate:
            values = lax.optimization_barrier((values, *gate))[0]
        came = flip(values, "dp", bit)
        gate[:] = [came]
        return came

    def blocks(self, values, axis, order):
        size = values.shape[axis] // self.n_dp
        parts = [lax.slice_in_dim(values, i * size, (i + 1) * size, axis=axis) for i in order]
        return jnp.concatenate(parts, axis)

    def ordered(self, values, axis):
        order = [i for low in (0, 1) for i in range(low, self.n_dp, 2)]
        return self.blocks(values, axis, order)

    def restored(self, values, axis):
        half = self.n_dp // 2
        return self.blocks(values, axis, [i // 2 + half * (i % 2) for i in range(self.n_dp)])

    def columns_ordered(self, wide, first=0):
        size, half = wide // self.n_dp, self.n_dp // 2
        return [
            (first + i * size, size, (i % 2 * half + i // 2) * size) for i in range(self.n_dp)
        ]

    def columns_restored(self, wide):
        return [(to, size, first) for first, size, to in self.columns_ordered(wide)]

    def restored_rows(self, values):
        rows, wide = values.shape
        if wide // self.n_dp % 128:
            return self.restored(values, 1)
        stores = [(0, c, w, 0, None, to) for c, w, to in self.columns_restored(wide)]
        return move([values], [], [(None, rows)], stores, [values.shape])[0]

    def after(self, values, *names):
        return lax.optimization_barrier((values, *(self.marks[n] for n in names)))[0]

    def halves(self, shards, extra=()):
        mine = jnp.concatenate([*(self.half(s, self.z) for s in shards), *extra], 1)
        partner = jnp.concatenate([*(self.half(s, 1 - self.z) for s in shards), *extra], 1)
        return mine, partner

    def near_gather(self, line):
        return lax.all_gather(line, "dp", axis=0, tiled=True, axis_index_groups=self.pairs)

    def swap(self, *shards, extra=()):
        mine, partner = self.halves(shards, extra)
        return mine, self.send(partner, PAIR)

    def gather_weight(self, mine, came, *early):
        pieces = {0: mine, PAIR: came}
        for bit in self.far_bits:
            for mask in list(pieces):
                pieces[mask | bit] = self.send(pieces[mask], bit)
        rows = mine.shape[0]
        starts = [((self.dp ^ mask) // 2) * rows for mask in pieces]
        line = place(list(pieces.values()), starts, 0, self.n_dp // 2 * rows)
        self.gates["far"] += [line, *early]
        return self.near_gather(line)

    def start_line(self, name, mine, came):
        rows = mine.shape[0]
        line = place([mine, came], [self.z * rows, (1 - self.z) * rows], 0, 2 * rows)
        self.marks[name + ".pair"] = line
        return line

    def finish_line(self, name, line, widths=None, hold=None):
        for bit in self.far_bits:
            rows = line.shape[0]
            came = self.send(line, bit)
            if hold is not None:
                came = lax.optimization_barrier((came, hold))[0]
            own = self.dp_bit(bit)
            cut = widths if bit == self.far_bits[-1] else None
            line = place([line, came], [own * rows, (1 - own) * rows], 0, 2 * rows, widths=cut)
        self.marks[name + ".far"] = came
        self.marks[name + ".line"] = line if widths is None else line[0]
        return line

    def gather_packed(self, packed):
        value = packed[None]
        for bit in [PAIR] + self.far_bits:
            other = flip(value, "dp", bit)
            low = self.dp_bit(bit) == 0
            value = jnp.concatenate(
                [jnp.where(low, value, other), jnp.where(low, other, value)]
            )
        other = flip(value, "dp", 1)
        value = jnp.where(
            self.dp % 2 == 0, jnp.stack([value, other], 1), jnp.stack([other, value], 1)
        )
        return value.reshape((-1,) + packed.shape)

    def split_dp(self, values):
        rows = values.shape[0] // self.n_dp
        return values.reshape((2,) * len(self.dp_bits) + (rows,) + values.shape[1:])

    def sum_dp(self, values):
        values = self.split_dp(values)
        for k, bit in enumerate(reversed(self.dp_bits)):
            mine = self.dp_bit(bit)
            away = narrow(pick(values, 0, 1 - mine))
            kept = pick(values, 0, mine).astype(f32)
            values = narrow(kept + flip(away, "dp", bit).astype(f32))
        return values

    def near_sum(self, grad):
        return lax.psum_scatter(
            grad, "dp", scatter_dimension=0, tiled=True, axis_index_groups=self.pairs
        )

    def square_sum(self, grad):
        return lax.psum_scatter(
            grad, "dp", scatter_dimension=0, tiled=True, axis_index_groups=self.square
        )

    def join_halves(self, name, *summed, parts=None):
        values = [v.reshape(2, v.shape[0] // 2, v.shape[1]) for v in summed]
        return self.join(name, values, parts)

    def scatter_unit(self, name, *summed, parts=None):
        rows = 2 * summed[0].shape[0] // self.n_dp
        left = [b for b in reversed(self.dp_bits) if b != 1]
        values = [v.reshape((2,) * len(left) + (rows, v.shape[1])) for v in summed]
        for bit in self.far_bits:
            at = left.index(bit)
            mine = self.dp_bit(bit)
            away = jnp.concatenate([pick(v, at, 1 - mine) for v in values], -1)
            if bit == self.far_bits[0]:
                self.marks[name + ".ready"] = away
            came = self.send(away, bit)
            first, added = 0, []
            for v in values:
                width = v.shape[-1]
                part = came[..., first : first + width].astype(f32)
                added.append(narrow(pick(v, at, mine).astype(f32) + part))
                first += width
            values = added
            left.pop(at)
        self.marks[name + ".sum"] = came
        return self.join(name, values, parts)

    def join(self, name, values, parts):
        away = jnp.concatenate([pick(v, 0, 1 - self.z) for v in values], -1)
        self.marks[name + ".turn"] = away
        other = self.send(away, PAIR)
        self.marks[name + ".swap"] = other
        out, first = [], 0
        for v, count in zip(values, parts or (1,) * len(values)):
            mine = pick(v, 0, self.z)
            width = v.shape[-1] // count
            for i in range(count):
                a = mine[:, i * width : (i + 1) * width]
                b = other[:, first : first + width]
                joined = jnp.where(
                    self.z == 0, jnp.concatenate([a, b], 1), jnp.concatenate([b, a], 1)
                )
                out.append(joined.astype(f32))
                first += width
        return out


    def hop(self, values, name):
        if name == "z":
            return flip(values, "dp", PAIR)
        return flip(values, "tensor", 2 if name == "x" else 1)

    def halve(self, values, order, names, kind=jnp.bfloat16):
        order = list(order)
        for name in names:
            at = order.index(name)
            mine = getattr(self, name)
            away = pick(values, at, 1 - mine).astype(kind)
            kept = pick(values, at, mine).astype(f32)
            values = kept + self.hop(away, name).astype(f32)
            order.pop(at)
            if order:
                values = values.astype(kind)
        return values

    def reduce_tokens(self, part):
        rows, wide = part.shape
        blocks = part.reshape(2, 2, 2, rows // 8, wide)
        first = self.halve(blocks, "zxc", "c")
        cut = wide // 2
        return jnp.concatenate(
            [
                self.halve(narrow(first)[..., :cut], "zx", "xz"),
                self.halve(narrow(first)[..., cut:], "zx", "zx"),
            ],
            -1,
        )

    def reduce_features(self, part):
        if self.n_dp != 8:
            wide, rows = part.shape
            part = self.restored(part, 0).reshape(2, 2, 2, wide // 8, rows)
            part = part.transpose(2, 0, 1, 3, 4).reshape(wide, rows)
        return self.reduce_tokens(part)

    def spread(self, shard, cut_at):
        by_z = self.hop(shard, "z")
        by_x = self.hop(shard, "x")
        far_a = self.hop(by_z[:cut_at], "x")
        far_b = self.hop(by_x[cut_at:], "z")
        pieces = [(0, 0, None, shard), (1, 0, None, by_z), (0, 1, None, by_x)]
        pieces += [(1, 1, 0, far_a), (1, 1, 1, far_b)]
        out = []
        for dz, dx, part, piece in pieces:
            out.append((dz, dx, 0, part, piece))
            out.append((dz, dx, 1, part, self.hop(piece, "c")))
        return out

    def gather_tokens(self, shard):
        rows = shard.shape[0]
        pieces, starts = [], []
        for dz, dx, dc, part, piece in self.spread(shard, rows // 2):
            block = (self.z ^ dz) * 4 + (self.x ^ dx) * 2 + (self.c ^ dc)
            starts.append(block * rows + (rows // 2 if part == 1 else 0))
            pieces.append(piece)
        return place(pieces, starts, 0, 8 * rows)

    def gather_features(self, shard):
        wide = shard.shape[1]
        by_z = self.hop(shard, "z")
        by_x = self.hop(shard, "x")
        far = self.hop(by_z, "x")
        pieces, starts = [], []
        for dz, dx, piece in ((0, 0, shard), (1, 0, by_z), (0, 1, by_x), (1, 1, far)):
            for dc, value in ((0, piece), (1, self.hop(piece, "c"))):
                block = (self.x ^ dx) * 4 + (self.c ^ dc) * 2 + (self.z ^ dz)
                if self.n_dp == 8:
                    block = block % 2 * 4 + block // 2
                starts.append(block * wide)
                pieces.append(value)
        whole = place(pieces, starts, 1, 8 * wide)
        return whole if self.n_dp == 8 else self.ordered(whole, 1)

    def gather_own(self, shard, columns=None):
        rows = shard.shape[0]
        by_x = self.hop(shard, "x")
        pieces, starts = [], []
        for dx, piece in ((0, shard), (1, by_x)):
            for dc, value in ((0, piece), (1, self.hop(piece, "c"))):
                starts.append(((self.x ^ dx) * 2 + (self.c ^ dc)) * rows)
                pieces.append(value)
        return place(pieces, starts, 0, 4 * rows, columns)

    def gather_small(self, row):
        value = row
        for name in "cxz":
            mine = getattr(self, name)
            other = self.hop(value, name)
            value = jnp.where(
                mine == 0,
                jnp.concatenate([value, other]),
                jnp.concatenate([other, value]),
            )
        return value

    def sum_everywhere(self, values, tensor=True):
        for bit in self.dp_bits:
            values = values + flip(values, "dp", bit)
        if tensor:
            for bit in (1, 2):
                values = values + flip(values, "tensor", bit)
        return values


def small_rows(size):
    return -(-size // 128)


def pack(arrays, lead):
    rows = []
    for a in arrays:
        flat = a.reshape(lead, -1)
        size = flat.shape[1]
        flat = jnp.pad(flat, ((0, 0), (0, small_rows(size) * 128 - size)))
        rows.append(flat.reshape(lead, -1, 128))
    total = sum(r.shape[1] for r in rows)
    fill = -total % 64
    if fill:
        rows.append(jnp.zeros((lead, fill, 128), arrays[0].dtype))
    return jnp.concatenate(rows, 1)


def unpack(packed, shapes):
    out, at = [], 0
    lead = packed.shape[0]
    for shape in shapes:
        size = 1
        for s in shape:
            size *= s
        rows = small_rows(size)
        part = packed[:, at : at + rows].reshape(lead, rows * 128)[:, :size]
        out.append(part.reshape((lead,) + tuple(shape)))
        at += rows
    return out


def rows_joined(values):
    return values.reshape((values.shape[0] * values.shape[1],) + values.shape[2:])


def conv_act(pre, weight, bias, segments):
    length = pre.shape[1]
    taps = weight.shape[1]
    total = jnp.zeros_like(pre) + bias
    for tap in range(taps):
        lag = taps - 1 - tap
        shifted = jnp.pad(pre, ((0, 0), (lag, 0), (0, 0)))[:, :length]
        earlier = jnp.pad(segments, ((0, 0), (lag, 0)), constant_values=-1)[:, :length]
        keeping = (earlier == segments).astype(f32)[:, :, None]
        total = total + weight[:, tap] * shifted * keeping
    return jax.nn.silu(total)


def gelu_product(gate_pre, up_pre):
    return jax.nn.gelu(gate_pre, approximate=True) * up_pre


def decay_piece(step_pre, step_bias, decay_log):
    sizes = jax.nn.softplus(step_pre + step_bias)
    return (jnp.cumsum(sizes * -jnp.exp(decay_log), axis=1), sizes)


def mixed_piece(core, mamba_act, mamba_gate, skip_scale):
    wide = jnp.broadcast_to(skip_scale[:, None], (skip_scale.shape[0], HEAD_M)).reshape(-1)
    with_skip = core + wide * mamba_act
    return with_skip * jax.nn.silu(mamba_gate)


def dot_nn(left, right):
    return jnp.dot(left, right, preferred_element_type=f32)


def dot_nt(left, right):
    return lax.dot_general(left, right, (((1,), (1,)), ((), ())), preferred_element_type=f32)


def dot_tn(left, right):
    return lax.dot_general(left, right, (((0,), (0,)), ((), ())), preferred_element_type=f32)


def same_document(down, across):
    shape = (down.shape[0], across.shape[1])
    later = lax.broadcasted_iota(jnp.int32, shape, 0) >= lax.broadcasted_iota(
        jnp.int32, shape, 1
    )
    return later & (down == across)


def turn(values, cosine, sine):
    return values * cosine + pltpu.roll(values, HEAD_SIZE // 2, 1) * sine


def attend_probabilities(query, key, kept):
    scores = jnp.where(kept, dot_nt(query, key) * HEAD_SIZE ** (-0.5), -1e30)
    raised = jnp.exp(scores - jnp.max(scores, axis=1, keepdims=True))
    return raised / jnp.sum(raised, axis=1, keepdims=True)


def attend_kernel(q_ref, k_ref, v_ref, cos_ref, sin_ref, down_ref, across_ref, qo, ko, out):
    cosine, sine = cos_ref[...], sin_ref[...]
    query = narrow(turn(q_ref[...], cosine, sine))
    key = narrow(turn(k_ref[...], cosine, sine))
    qo[...] = query
    ko[...] = key
    kept = same_document(down_ref[...], across_ref[...])
    probabilities = narrow(attend_probabilities(query, key, kept))
    out[...] = narrow(dot_nn(probabilities, v_ref[...]))


def attend_back_kernel(
    q_ref, k_ref, v_ref, g_ref, cos_ref, sin_ref, down_ref, across_ref, dq, dk, dv
):
    query, key, grad = q_ref[...], k_ref[...], g_ref[...]
    kept = same_document(down_ref[...], across_ref[...])
    probabilities = attend_probabilities(query, key, kept)
    dv[...] = narrow(dot_tn(narrow(probabilities), grad))
    grad_probs = dot_nt(grad, v_ref[...])
    inner = jnp.sum(probabilities * grad_probs, axis=1, keepdims=True)
    grad_scores = narrow(probabilities * (grad_probs - inner))
    cosine, sine = cos_ref[...], sin_ref[...]
    scale = HEAD_SIZE ** (-0.5)
    dq[...] = narrow(turn(dot_nn(grad_scores, key) * scale, cosine, -sine))
    dk[...] = narrow(turn(dot_tn(grad_scores, query) * scale, cosine, -sine))


def of_head(j):
    lane = lax.broadcasted_iota(jnp.int32, (1, 2 * HEAD_M), 1)
    return (lane >= j * HEAD_M) & (lane < (j + 1) * HEAD_M)


def decay_of(acc_ref, turned_ref, j, kept):
    lagged = acc_ref[:, j : j + 1] - turned_ref[j : j + 1, :]
    return jnp.where(kept, jnp.exp(jnp.where(kept, lagged, 0.0)), 0.0)


def weighted_of(act_ref, size_ref):
    return narrow(act_ref[...] * jnp.where(of_head(0), size_ref[:, 0:1], size_ref[:, 1:2]))


def mix_kernel(act_ref, size_ref, acc_ref, turned_ref, in_ref, out_ref, down_ref, across_ref, core):
    kept = same_document(down_ref[...], across_ref[...])
    gram = dot_nt(out_ref[...], in_ref[...])
    weighted = weighted_of(act_ref, size_ref)
    parts = [
        dot_nn(narrow(gram * decay_of(acc_ref, turned_ref, j, kept)), weighted) for j in (0, 1)
    ]
    core[...] = jnp.where(of_head(0), parts[0], parts[1])


def mix_back_kernel(
    grad_ref,
    act_ref,
    size_ref,
    acc_ref,
    turned_ref,
    in_ref,
    out_ref,
    down_ref,
    across_ref,
    dact,
    dsize,
    dgram,
    dacc,
    dturned,
    total,
):
    kept = same_document(down_ref[...], across_ref[...])
    gram = dot_nt(out_ref[...], in_ref[...])
    weighted = weighted_of(act_ref, size_ref)
    grad = grad_ref[...]

    @pl.when(pl.program_id(1) == 0)
    def _():
        total[...] = jnp.zeros_like(total)

    parts = []
    for j in (0, 1):
        decay = decay_of(acc_ref, turned_ref, j, kept)
        mixing = gram * decay
        parts.append(dot_tn(narrow(mixing), grad))
        grad_mixing = dot_nt(jnp.where(of_head(j), grad, jnp.zeros_like(grad)), weighted)
        total[...] += grad_mixing * decay
        grad_lag = grad_mixing * mixing
        dacc[:, j : j + 1] = jnp.sum(grad_lag, axis=1, keepdims=True)
        dturned[j : j + 1, :] = jnp.sum(grad_lag, axis=0, keepdims=True)
    grad_weighted = jnp.where(of_head(0), parts[0], parts[1])
    dact[...] = grad_weighted * jnp.where(of_head(0), size_ref[:, 0:1], size_ref[:, 1:2])
    product = grad_weighted * act_ref[...]
    for j in (0, 1):
        dsize[:, j : j + 1] = jnp.sum(
            jnp.where(of_head(j), product, 0.0), axis=1, keepdims=True
        )

    @pl.when(pl.program_id(1) == pl.num_programs(1) - 1)
    def _():
        dgram[...] = narrow(total[...])


def by_columns(S):
    return pl.BlockSpec((S, 128), lambda b, h: (b, h))


def by_sequence(S):
    return pl.BlockSpec((S, 128), lambda b, h: (b, 0))


def marks_specs(S):
    return [
        pl.BlockSpec((S, 1), lambda b, h: (b, 0)),
        pl.BlockSpec((None, 1, S), lambda b, h: (b, 0, 0)),
    ]


def attend_forward(query_pre, key_pre, value_low, cosine, sine, marks):
    T, wide = query_pre.shape
    S = T // 2
    low = jax.ShapeDtypeStruct((T, wide), jnp.bfloat16)
    return pl.pallas_call(
        attend_kernel,
        grid=(2, wide // 128),
        in_specs=[by_columns(S)] * 3 + [by_sequence(S)] * 2 + marks_specs(S),
        out_specs=[by_columns(S)] * 3,
        out_shape=[low] * 3,
    )(query_pre, key_pre, value_low, cosine, sine, *marks)


def attend_backward(query_rot, key_rot, value_low, grad, cosine, sine, marks):
    T, wide = query_rot.shape
    S = T // 2
    low = jax.ShapeDtypeStruct((T, wide), jnp.bfloat16)
    return pl.pallas_call(
        attend_back_kernel,
        grid=(2, wide // 128),
        in_specs=[by_columns(S)] * 4 + [by_sequence(S)] * 2 + marks_specs(S),
        out_specs=[by_columns(S)] * 3,
        out_shape=[low] * 3,
    )(query_rot, key_rot, value_low, grad, cosine, sine, *marks)


def by_heads(values):
    _, S, heads = values.shape
    turned = values.transpose(0, 2, 1).reshape(2, heads // 2, 2, S)
    return turned.transpose(0, 1, 3, 2), turned


def heads_specs(S):
    return (
        pl.BlockSpec((None, None, S, 2), lambda b, h: (b, h, 0, 0)),
        pl.BlockSpec((None, None, 2, S), lambda b, h: (b, h, 0, 0)),
    )


def mix_forward(act, sizes, accum, accum_turned, state_in, state_out, marks):
    T, wide = act.shape
    S = T // 2
    down, across = heads_specs(S)
    return pl.pallas_call(
        mix_kernel,
        grid=(2, wide // 128),
        in_specs=[by_columns(S), down, down, across]
        + [by_sequence(S)] * 2
        + marks_specs(S),
        out_specs=by_columns(S),
        out_shape=jax.ShapeDtypeStruct((T, wide), f32),
    )(act, sizes, accum, accum_turned, state_in, state_out, *marks)


def mix_backward(grad, act, sizes, accum, accum_turned, state_in, state_out, marks):
    T, wide = act.shape
    S = T // 2
    down, across = heads_specs(S)
    return pl.pallas_call(
        mix_back_kernel,
        grid=(2, wide // 128),
        in_specs=[by_columns(S), by_columns(S), down, down, across]
        + [by_sequence(S)] * 2
        + marks_specs(S),
        out_specs=[
            by_columns(S),
            down,
            pl.BlockSpec((None, S, S), lambda b, h: (b, 0, 0)),
            down,
            across,
        ],
        out_shape=[
            jax.ShapeDtypeStruct((T, wide), f32),
            jax.ShapeDtypeStruct(accum.shape, f32),
            jax.ShapeDtypeStruct((2, S, S), jnp.bfloat16),
            jax.ShapeDtypeStruct(accum.shape, f32),
            jax.ShapeDtypeStruct(accum_turned.shape, f32),
        ],
        scratch_shapes=[pltpu.VMEM((S, S), f32)],
    )(grad, act, sizes, accum, accum_turned, state_in, state_out, *marks)


def body(
    hidden,
    embedding,
    teacher_mid,
    teacher_out,
    segment_ids,
    rope_pos,
    valid_mask,
    gain_attn,
    w_query,
    w_key,
    w_value,
    query_down,
    query_up,
    w_attn_out,
    gain_mlp,
    w_gate,
    w_up,
    gate_down,
    gate_up,
    w_down,
    w_proj,
    gain_mamba,
    w_in_gate,
    w_in_main,
    w_in_state,
    w_in_step,
    conv_main,
    conv_main_bias,
    conv_state,
    conv_state_bias,
    gain_gated,
    w_mamba_out,
    step_bias,
    decay_log,
    skip_scale,
):
    me = Place()
    n_dp = me.n_dp
    S = hidden.shape[0]
    T = 2 * S
    quarter = S // 4
    z = me.z

    def own_rows(values):
        return lax.dynamic_slice_in_dim(values, me.tensor * quarter, quarter, 0)

    def own_tokens(values):
        return lax.dynamic_slice_in_dim(values, (z * 4 + me.tensor) * quarter, quarter, 0)

    def own_half(values, axis=-1):
        axis = axis % values.ndim
        width = values.shape[axis] // 2
        return lax.dynamic_slice_in_dim(values, z * width, width, axis)

    def filled(values, rows):
        fill = rows - values.shape[0]
        return jnp.pad(values, ((0, fill), (0, 128 - values.shape[1])))

    tiny = (
        gain_mlp,
        gain_mamba,
        conv_main,
        conv_main_bias,
        conv_state,
        conv_state_bias,
        gain_gated,
    )
    tiny_shapes = tuple(a.shape for a in tiny)
    tiny_pack = pack([a[None] for a in tiny], 1)[0]
    row_count = w_attn_out.shape[0]
    marks = jnp.stack([segment_ids, rope_pos])
    marks_other = me.hop(marks, "z")
    small = me.gather_packed(pack([gain_attn[None], query_up[None]], 1)[0])
    gain_attn_all, query_up_all = map(
        rows_joined, unpack(small, (gain_attn.shape, query_up.shape))
    )
    query_up_all = own_half(query_up_all)
    marks = jnp.stack([segment_ids, rope_pos])
    marks_other = me.hop(marks, "z")
    own_cat = jnp.concatenate([hidden, embedding], 1)
    gain_attn_f = gain_attn_all.astype(f32)
    normed_own = narrow(rms_scale(own_cat.astype(f32), gain_attn_f))
    normed_came = me.hop(own_rows(normed_own), "z")
    near_lane, far_lane = me.gates["pair"], me.gates["far"]
    swaps = {"query": me.swap(w_query)}
    near_lane += [small, marks_other]
    swaps["key"] = me.swap(w_key)
    near_lane += [normed_came]
    swaps["value"] = me.swap(w_value, extra=(query_down,))
    swaps["attn_out"] = me.swap(
        w_attn_out,
        extra=(
            gate_down,
            w_in_state,
            filled(gate_up.reshape(-1, 128), row_count),
            filled(w_in_step, row_count),
            filled(tiny_pack, row_count),
        ),
    )
    swaps["gate_up"] = me.swap(w_gate, w_up)
    swaps["late"] = me.swap(w_down, w_proj, w_in_gate, w_in_main, w_mamba_out)
    w_query_all = me.gather_weight(*swaps["query"])
    w_key_all = me.gather_weight(*swaps["key"])
    w_value_more = me.gather_weight(*swaps["value"])
    far_lane += [swaps["gate_up"][1]]
    attn_out_line = me.start_line("attn_out", *swaps["attn_out"])
    gate_up_line = me.start_line("gate_up", *swaps["gate_up"])
    late_line = me.start_line("late", *swaps["late"])
    w_attn_out_more = me.near_gather(me.finish_line("attn_out", attn_out_line))
    far_lane += [swaps["late"][1]]
    units = w_down.shape[1] // 2
    channels = w_in_gate.shape[1] // 2
    wide = w_value.shape[1] // 2
    w_value_all = w_value_more[:, :wide]
    query_down_all = w_value_more[:, wide:]

    def rows_back(columns, like):
        flat = columns.reshape(n_dp, -1, 128)[:, : like.size // 128]
        return rows_joined(me.restored(flat, 0).reshape((n_dp,) + like.shape))

    wide = w_attn_out.shape[1] // 2
    w_attn_out_all = w_attn_out_more[:, :wide]
    more = w_attn_out_more[:, wide:]
    gate_down_all = more[:, :128]
    w_in_state_all = more[:, 128:384]
    gate_up_all = own_half(rows_back(more[:, 384:512], gate_up))
    w_in_step_all = own_half(more[:, 512 : 512 + w_in_step.shape[1]])
    tiny_all = more[:, 640:].reshape(n_dp, -1, 128)[:, : tiny_pack.shape[0]]
    (
        gain_mlp_all,
        gain_mamba_all,
        conv_main_all,
        conv_main_bias_all,
        conv_state_all,
        conv_state_bias_all,
        gain_gated_all,
    ) = unpack(tiny_all, tiny_shapes)
    gain_mlp_all, gain_mamba_all = gain_mlp_all.reshape(-1), gain_mamba_all.reshape(-1)
    (
        conv_main_all,
        conv_main_bias_all,
        conv_state_all,
        conv_state_bias_all,
        gain_gated_all,
    ) = (
        rows_joined(me.restored(a, 0))
        for a in (
            conv_main_all,
            conv_main_bias_all,
            conv_state_all,
            conv_state_bias_all,
            gain_gated_all,
        )
    )
    conv_main_all = own_half(conv_main_all, 0).astype(f32)
    conv_main_bias_all = own_half(conv_main_bias_all, 0).astype(f32)
    gain_gated_f = own_half(gain_gated_all, 0).astype(f32)
    even = D // n_dp % 128 == 0
    order_d = me.columns_ordered(D) if even else [(0, D, 0)]
    hidden_shard, teacher_mid_shard, teacher_out_shard = move(
        [hidden, teacher_mid, teacher_out],
        [me.tensor * quarter],
        [(0, quarter)] * 3,
        [(i, c, w, i, None, to) for i in range(3) for c, w, to in order_d],
        [(quarter, D)] * 3,
    )
    if not even:
        hidden_shard = me.ordered(hidden_shard, 1)
        teacher_mid_shard = me.ordered(teacher_mid_shard, 1)
        teacher_out_shard = me.ordered(teacher_out_shard, 1)

    both = jnp.where(z == 0, jnp.stack([marks, marks_other], 1), jnp.stack([marks_other, marks], 1))
    segments, positions = both[0], both[1]
    marks_laid = (segments.reshape(T, 1), segments.reshape(2, 1, S))
    count = me.sum_everywhere(
        jnp.broadcast_to(jnp.sum(valid_mask.astype(f32)), (8, 128)), tensor=False
    )[0, 0]
    half = HEAD_SIZE // 2
    inverse = 10000.0 ** (-jnp.arange(half, dtype=f32) / half)
    angles = positions.reshape(T, 1).astype(f32) * inverse
    cosine = jnp.concatenate([jnp.cos(angles)] * 2, 1)
    sine = jnp.concatenate([-jnp.sin(angles), jnp.sin(angles)], 1)

    cat_shard = own_rows(own_cat).astype(f32)
    _, cat_back = jax.vjp(rms_scale, cat_shard, gain_attn_f)
    normed_other = me.gather_own(normed_came)
    normed_cat = place(
        [normed_own, normed_other], [z * S, (1 - z) * S], 0, T, me.columns_ordered(2 * D)
    )
    normed_cat_shard = own_tokens(normed_cat)
    normed_cat = me.after(normed_cat, "attn_out.far", "late.pair")
    query_low = narrow(times_right(normed_cat, query_down_all))
    query_pre = times_right(normed_cat, w_query_all) + times_right(query_low, query_up_all)
    key_pre = times_right(normed_cat, w_key_all)
    value_low = times_right(normed_cat, w_value_all, jnp.bfloat16)
    query_rot, key_rot, attended_low = attend_forward(
        query_pre, key_pre, value_low, cosine, sine, marks_laid
    )
    w_gate_up = me.near_gather(me.finish_line("gate_up", gate_up_line, hold=attended_low))
    down_line, in_line = me.finish_line(
        "late", late_line, [units + w_proj.shape[1] // 2, 3 * channels]
    )
    w_down_proj = me.near_gather(down_line)
    w_in_out = me.near_gather(in_line)
    w_down_all = w_down_proj[:, :units]
    w_proj_all = w_down_proj[:, units:]
    w_in_all = w_in_out[:, : 2 * channels]
    w_mamba_out_all = w_in_out[:, 2 * channels :]
    attended_low = me.after(attended_low, "gate_up.line")
    attn_part = times_trans(attended_low, w_attn_out_all, jnp.bfloat16)
    attn_shard = me.reduce_tokens(attn_part)

    hidden_shard = hidden_shard.astype(f32)
    first_sum = hidden_shard + attn_shard
    normed_mid_f, mid_back = jax.vjp(rms_scale, first_sum, gain_mlp_all.astype(f32))
    normed_mid_shard = narrow(normed_mid_f)
    normed_mid = me.gather_tokens(me.after(normed_mid_shard, "late.line"))
    gate_low = narrow(times_right(normed_mid, gate_down_all))
    gate_up_pre = times_right(normed_mid, w_gate_up)
    gate_pre = gate_up_pre[:, :units] + times_right(gate_low, gate_up_all)
    up_pre = gate_up_pre[:, units:]
    inner, inner_back = jax.vjp(gelu_product, gate_pre, up_pre)
    inner = narrow(inner)
    mlp_part = narrow(
        times_trans(w_down_all, inner) + times_trans(w_attn_out_all, attended_low)
    )
    shared_out = narrow(me.reduce_features(mlp_part))
    projected = me.reduce_tokens(
        narrow(
            lax.dot_general(
                shared_out, w_proj_all, (((0,), (1,)), ((), ())), preferred_element_type=f32
            )
        )
    )
    middle = hidden_shard + projected

    normed_last_f, last_back = jax.vjp(rms_scale, middle, gain_mamba_all.astype(f32))
    normed_last_shard = narrow(normed_last_f)
    normed_last = me.gather_tokens(normed_last_shard)
    mamba_in = times_right(normed_last, w_in_all)
    mamba_gate = mamba_in[:, :channels].reshape(2, S, channels)
    mamba_pre = mamba_in[:, channels:].reshape(2, S, channels)
    state_pre = times_right(normed_last, w_in_state_all).reshape(2, S, 2 * STATE)
    mamba_here = w_in_step_all.shape[1]
    step_pre = times_right(normed_last, w_in_step_all).reshape(2, S, mamba_here)
    convolve = partial(conv_act, segments=segments)
    mamba_act, main_conv_back = jax.vjp(convolve, mamba_pre, conv_main_all, conv_main_bias_all)
    state_act, state_conv_back = jax.vjp(
        convolve, state_pre, conv_state_all.astype(f32), conv_state_bias_all.astype(f32)
    )
    state_in = narrow(state_act[..., :STATE])
    state_out = narrow(state_act[..., STATE:])
    (accum, step_sizes), decay_back = jax.vjp(
        decay_piece,
        step_pre,
        own_half(step_bias, 0).astype(f32),
        own_half(decay_log, 0).astype(f32),
    )
    sizes_down, _ = by_heads(step_sizes)
    accum_down, accum_across = by_heads(accum)
    act_flat = mamba_act.reshape(T, channels)
    in_flat, out_flat = state_in.reshape(T, STATE), state_out.reshape(T, STATE)
    mix_inputs = (act_flat, sizes_down, accum_down, accum_across, in_flat, out_flat, marks_laid)
    core = mix_forward(*mix_inputs).reshape(2, S, channels)
    mixed, mixed_back = jax.vjp(
        mixed_piece, core, mamba_act, mamba_gate, own_half(skip_scale, 0).astype(f32)
    )
    square_part = jnp.sum(mixed * mixed, axis=-1).reshape(2, 2, 2, 1, quarter)
    square_total = me.halve(square_part, "zxc", "cxz", f32).reshape(quarter)
    scaled = narrow(mixed * gain_gated_f).reshape(T, channels)
    mamba_sum = me.reduce_tokens(times_trans(scaled, w_mamba_out_all, jnp.bfloat16))
    inverse_rms = lax.rsqrt(square_total / DI + eps)[:, None]
    mamba_branch = inverse_rms * mamba_sum
    final_sum = middle + mamba_branch

    valid_rows = own_rows(valid_mask).astype(f32)[:, None]
    miss_mid = middle - teacher_mid_shard.astype(f32)
    miss_out = final_sum - teacher_out_shard.astype(f32)
    square_mid = jnp.sum(valid_rows * miss_mid * miss_mid)
    square_out = jnp.sum(valid_rows * miss_out * miss_out)
    factor = S * n_dp / count
    grad_final = factor * valid_rows * miss_out
    row_inner = jnp.sum(grad_final * mamba_branch, axis=-1)
    pull = row_inner * inverse_rms[:, 0] * inverse_rms[:, 0] / DI
    branch_grad = me.gather_tokens(narrow(inverse_rms * grad_final))
    pull_all = me.gather_small(pull).reshape(2, S, 1)

    dw_mamba_out = trans_times(branch_grad, scaled, jnp.bfloat16)
    sum_mamba_out = me.square_sum(dw_mamba_out)
    grad_scaled = times_right(branch_grad, w_mamba_out_all).reshape(2, S, channels)
    grad_gain_gated = jnp.sum(grad_scaled * mixed, axis=(0, 1))
    grad_mixed = grad_scaled * gain_gated_f - mixed * pull_all
    grad_core, grad_heads, grad_gate_z, grad_skip_scale = mixed_back(grad_mixed)
    act_part, dsize, gram_grad, dacc, dturned = mix_backward(
        narrow(grad_core).reshape(T, channels), *mix_inputs
    )

    def from_down(values):
        return values.transpose(0, 2, 1, 3).reshape(2, S, mamba_here)

    grad_accum = from_down(dacc) - dturned.reshape(2, mamba_here, S).transpose(0, 2, 1)
    grad_step_pre, grad_step_bias, grad_decay_log = decay_back((grad_accum, from_down(dsize)))
    grad_heads = grad_heads + act_part.reshape(2, S, channels)
    grad_state_part = jnp.concatenate(
        [
            jnp.einsum("bts,bte->bse", gram_grad, state_out, preferred_element_type=f32),
            jnp.einsum("bts,bse->bte", gram_grad, state_in, preferred_element_type=f32),
        ],
        axis=-1,
    )
    state_shard = me.reduce_tokens(narrow(grad_state_part).reshape(T, 2 * STATE))
    grad_state = me.gather_tokens(narrow(state_shard)).astype(f32).reshape(2, S, 2 * STATE)
    grad_mamba_pre, grad_conv_main, grad_conv_main_bias = main_conv_back(
        grad_heads.reshape(2, S, channels)
    )
    grad_in = jnp.concatenate([narrow(grad_gate_z), narrow(grad_mamba_pre)], -1).reshape(T, -1)
    step_grad_low = narrow(grad_step_pre).reshape(T, -1)
    sum_in = me.square_sum(trans_times(normed_last, grad_in, jnp.bfloat16))
    grad_w_in_step = me.restored(trans_times(normed_last, step_grad_low, jnp.bfloat16), 0)
    last_part = times_trans(grad_in, w_in_all) + times_trans(step_grad_low, w_in_step_all)
    last_part = lax.optimization_barrier((narrow(last_part), sum_mamba_out))[0]
    last_shard = me.reduce_tokens(last_part)
    grad_state_pre, grad_conv_state, grad_conv_state_bias = state_conv_back(grad_state)
    state_grad_low = own_tokens(narrow(grad_state_pre).reshape(T, -1))
    grad_w_in_state = trans_times(normed_last_shard, state_grad_low, jnp.bfloat16)
    grad_middle, grad_gain_mamba = last_back(
        last_shard + times_trans(state_grad_low, w_in_state_all)
    )
    grad_middle = grad_middle + grad_final + factor * valid_rows * miss_mid

    projected_grad = me.gather_tokens(narrow(grad_middle))
    sum_proj = me.near_sum(
        narrow(
            lax.dot_general(
                projected_grad, shared_out, (((0,), (1,)), ((), ())), preferred_element_type=f32
            )
        )
    )
    mlp_grad = me.gather_features(times_right(projected_grad, w_proj_all, jnp.bfloat16))
    mlp_grad = lax.optimization_barrier((mlp_grad, sum_in))[0]
    dw_down = trans_times(mlp_grad, inner, jnp.bfloat16)
    sum_down = me.near_sum(dw_down)
    grad_gate_pre, grad_up_pre = inner_back(times_right(mlp_grad, w_down_all))
    gate_grad = narrow(grad_gate_pre)
    up_grad = narrow(grad_up_pre)
    pre_grad = jnp.concatenate([gate_grad, up_grad], 1)
    dw_gate_up = trans_times(normed_mid, pre_grad, jnp.bfloat16)
    sum_gate_up = me.near_sum(dw_gate_up)
    mid_part = times_trans(pre_grad, w_gate_up, jnp.bfloat16)
    mid_part = lax.optimization_barrier((mid_part, dw_down, dw_gate_up))[0]
    low_part = times_trans(gate_grad, gate_up_all, jnp.bfloat16)
    mid_shard = me.reduce_tokens(mid_part)
    gate_low_grad = narrow(me.reduce_tokens(low_part))
    grad_w_gate, grad_w_up = me.scatter_unit("gate_up", sum_gate_up, parts=(2,))
    grad_gate_up = trans_times(gate_low, gate_grad, jnp.bfloat16)
    grad_gate_down = trans_times(normed_mid_shard, gate_low_grad, jnp.bfloat16)
    grad_first, grad_gain_mlp = mid_back(mid_shard + times_trans(gate_low_grad, gate_down_all))

    attn_grad_shard = narrow(own_tokens(mlp_grad).astype(f32) + grad_first)
    attn_grad = me.gather_tokens(attn_grad_shard)
    sum_attn_out = me.near_sum(trans_times(attn_grad, attended_low, jnp.bfloat16))
    attended_grad = times_right(attn_grad, w_attn_out_all, jnp.bfloat16)
    attended_grad = me.after(attended_grad, "gate_up.ready")
    query_grad, key_grad, value_grad = attend_backward(
        query_rot, key_rot, value_low, attended_grad, cosine, sine, marks_laid
    )
    sum_value = me.near_sum(trans_times(normed_cat, value_grad, jnp.bfloat16))
    sum_key = me.near_sum(trans_times(normed_cat, key_grad, jnp.bfloat16))
    sum_query = me.near_sum(trans_times(normed_cat, query_grad, jnp.bfloat16))
    cat_part = narrow(
        times_trans(query_grad, w_query_all)
        + times_trans(key_grad, w_key_all)
        + times_trans(value_grad, w_value_all)
    )
    low_part = times_trans(query_grad, query_up_all, jnp.bfloat16)
    cat_part = me.after(cat_part, "gate_up.sum")
    cat_shard_sum = me.reduce_tokens(cat_part)
    query_low_grad = narrow(me.reduce_tokens(low_part))
    def later(values):
        return lax.optimization_barrier((values, cat_shard_sum))[0]

    grad_w_proj, grad_w_down = me.scatter_unit("block", later(sum_proj), later(sum_down))
    (grad_w_attn_out,) = me.scatter_unit("d_attn_out", later(sum_attn_out))
    (grad_w_value,) = me.scatter_unit("d_value", later(sum_value))
    (grad_w_key,) = me.scatter_unit("key", sum_key)
    (grad_w_query,) = me.scatter_unit("query", sum_query)
    grad_w_mamba_out, grad_w_in_gate, grad_w_in_main = me.join_halves(
        "mixer", later(sum_mamba_out), later(sum_in), parts=(1, 2)
    )
    grad_query_up = trans_times(query_low, query_grad, jnp.bfloat16)
    grad_query_down = trans_times(normed_cat_shard, query_low_grad, jnp.bfloat16)
    grad_concat, grad_gain_attn = cat_back(
        me.restored_rows(cat_shard_sum + times_trans(query_low_grad, query_down_all))
    )
    stream = me.restored_rows(grad_first + grad_middle)
    grad_both = jnp.concatenate([grad_concat[:, :D] + stream, grad_concat[:, D:]], 1)
    grad_both = me.gather_own(narrow(grad_both)).astype(f32)
    if even:
        final_low = lax.optimization_barrier((narrow(final_sum), cat_part))[0]
        output = me.gather_own(final_low, me.columns_restored(D))
    else:
        output = me.gather_own(me.restored(narrow(final_sum), 1))

    def by_dp(values):
        return values.reshape((n_dp, values.shape[0] // n_dp) + values.shape[1:])

    def both_halves(values, axis):
        axis = axis % values.ndim
        nothing = jnp.zeros_like(values)
        return jnp.where(
            z == 0,
            jnp.concatenate([values, nothing], axis),
            jnp.concatenate([nothing, values], axis),
        )

    first = (me.tensor == 0) & (z == 0)
    shared = (
        me.restored(grad_gain_mlp, 0),
        me.restored(grad_gain_mamba, 0),
        jnp.where(first, grad_conv_state, 0.0),
        jnp.where(first, grad_conv_state_bias, 0.0),
        me.restored(grad_gate_down, 0),
        me.restored(grad_w_in_state, 0),
    )
    shared_out_shapes = (
        gain_mlp.shape,
        gain_mamba.shape,
        conv_state.shape,
        conv_state_bias.shape,
        gate_down.shape,
        w_in_state.shape,
    )
    shared += (grad_gain_attn, me.restored(grad_query_down, 0))
    shared_out_shapes += (gain_attn.shape, query_down.shape)
    split = (
        both_halves(grad_conv_main, 0),
        both_halves(grad_conv_main_bias, 0),
        both_halves(grad_gain_gated, 0),
        both_halves(grad_gate_up, 1),
        both_halves(grad_w_in_step, 1),
        both_halves(grad_query_up, 1),
    )
    split_shapes = (
        conv_main.shape,
        conv_main_bias.shape,
        gain_gated.shape,
        gate_up.shape,
        w_in_step.shape,
        query_up.shape,
    )
    shared_rows = pack([by_dp(narrow(a)) for a in shared], n_dp)
    part_rows = shared_rows.shape[1] // 4
    blocks = shared_rows.reshape(n_dp, 2, 2, part_rows, 128).transpose(1, 2, 0, 3, 4)
    shared_mine = narrow(me.halve(blocks, "xc", "cx"))
    split_rows = pack([by_dp(narrow(a)) for a in split], n_dp)
    small_mine = me.sum_dp(rows_joined(jnp.concatenate([shared_mine, split_rows], 1)))
    shared_sum = me.gather_own(small_mine[:part_rows])
    (
        out_gain_mlp,
        out_gain_mamba,
        out_conv_state,
        out_conv_state_bias,
        out_gate_down,
        out_w_in_state,
        out_gain_attn,
        out_query_down,
    ) = [v[0].astype(f32) for v in unpack(shared_sum[None], shared_out_shapes)]
    (
        out_conv_main,
        out_conv_main_bias,
        out_gain_gated,
        out_gate_up,
        out_w_in_step,
        out_query_up,
    ) = [v[0].astype(f32) for v in unpack(small_mine[None, part_rows:], split_shapes)]
    grad_step_bias, grad_decay_log, grad_skip_scale, square_mid, square_out = (
        lax.optimization_barrier(
            (grad_step_bias, grad_decay_log, grad_skip_scale, square_mid, square_out, cat_part)
        )[:5]
    )
    head_rows = jnp.stack(
        [
            both_halves(grad_step_bias, 0),
            both_halves(grad_decay_log, 0),
            both_halves(grad_skip_scale, 0),
        ]
    )
    head_sums = me.sum_everywhere(head_rows, tensor=False)
    losses = me.sum_everywhere(
        jnp.stack(
            [jnp.broadcast_to(square_mid, (128,)), jnp.broadcast_to(square_out, (128,))]
        )
    )
    loss_mid = losses[0, 0] / (count * D)
    loss_out = losses[1, 0] / (count * D)
    return (
        output,
        loss_mid,
        loss_out,
        grad_both[:, :D],
        grad_both[:, D:],
        out_gain_attn,
        grad_w_query,
        grad_w_key,
        grad_w_value,
        out_query_down,
        out_query_up,
        grad_w_attn_out,
        out_gain_mlp,
        grad_w_gate,
        grad_w_up,
        out_gate_down,
        out_gate_up,
        grad_w_down,
        grad_w_proj,
        out_gain_mamba,
        grad_w_in_gate,
        grad_w_in_main,
        out_w_in_state,
        out_w_in_step,
        out_conv_main,
        out_conv_main_bias,
        out_conv_state,
        out_conv_state_bias,
        out_gain_gated,
        grad_w_mamba_out,
        head_sums[0],
        head_sums[1],
        head_sums[2],
    )


def solution(mesh):
    in_specs = (
        P("dp", None),
        P("dp", None),
        P("dp", None),
        P("dp", None),
        P("dp"),
        P("dp"),
        P("dp"),
        P("dp"),
        P("dp", "tensor"),
        P("dp", "tensor"),
        P("dp", "tensor"),
        P("dp", None),
        P("dp", "tensor"),
        P("dp", "tensor"),
        P("dp"),
        P("dp", "tensor"),
        P("dp", "tensor"),
        P("dp", None),
        P("dp", "tensor"),
        P("dp", "tensor"),
        P("dp", "tensor"),
        P("dp"),
        P("dp", "tensor"),
        P("dp", "tensor"),
        P("dp", None),
        P("dp", "tensor"),
        P(("tensor", "dp"), None),
        P(("tensor", "dp")),
        P("dp", None),
        P("dp"),
        P(("tensor", "dp")),
        P("dp", "tensor"),
        P("tensor"),
        P("tensor"),
        P("tensor"),
    )
    out_specs = (
        P("dp", None),
        P(),
        P(),
        P("dp", None),
        P("dp", None),
        P("dp"),
        P("dp", "tensor"),
        P("dp", "tensor"),
        P("dp", "tensor"),
        P("dp", None),
        P("dp", "tensor"),
        P("dp", "tensor"),
        P("dp"),
        P("dp", "tensor"),
        P("dp", "tensor"),
        P("dp", None),
        P("dp", "tensor"),
        P("dp", "tensor"),
        P("dp", "tensor"),
        P("dp"),
        P("dp", "tensor"),
        P("dp", "tensor"),
        P("dp", None),
        P("dp", "tensor"),
        P(("tensor", "dp"), None),
        P(("tensor", "dp")),
        P("dp", None),
        P("dp"),
        P(("tensor", "dp")),
        P("dp", "tensor"),
        P("tensor"),
        P("tensor"),
        P("tensor"),
    )
    return jax.shard_map(body, mesh=mesh, in_specs=in_specs, out_specs=out_specs, check_vma=False)
```

time: 3800 us -> 1840 us (0.48)
  waiting for transfers between devices: 2850 us -> 960 us
  blocking collectives: 364 us -> 0 us
  Pallas kernels: 0 us -> 147 us
  starting transfers between devices: 2.25 us -> 132 us
  local copies, waits for them, and re-layouts: 47.1 us -> 155 us
  matrix products: 365 us -> 279 us
    reduce_scatter x18 -> x9, waiting for transfers between devices: 1660 us -> 0.07 us  [the longest x7 0.05 us: near_sum(): lax.psum_scatter(grad, 'dp', scatter_dimension=0, tiled=True, axis_index_...]
    ppermute x0 -> x178, waiting for transfers between devices: none -> 956 us  [flip(): return lax.ppermute(values, axis, [(i, i ^ bit) for i in range(count)])]
    all_gather x14 -> x7, waiting for transfers between devices: 942 us -> 2.97 us  [near_gather(): lax.all_gather(line, 'dp', axis=0, tiled=True, axis_index_groups=self.pairs)]
    all_gather x11 -> x0, blocking collectives: 258 us -> none  [the longest x1 31.6 us: body(): lax.all_gather(gate_down, 'dp', axis=0, tiled=True)]
    psum x6 -> x0, waiting for transfers between devices: 196 us -> none  [the longest x1 60.9 us: body(): lax.psum(last_part.astype(jnp.bfloat16), 'tensor').astype(jnp.float32)]
    pallas_call x0 -> x28, Pallas kernels: none -> 147 us  [the longest x24 88.6 us: move(): pl.pallas_call(partial(move_kernel, tuple(loads), tuple(stores), len(piec...]
    ppermute x0 -> x178, starting transfers between devices: none -> 129 us  [flip(): return lax.ppermute(values, axis, [(i, i ^ bit) for i in range(count)])]
    unnamed x2 -> x0, blocking collectives: 55.1 us -> none
  transfers between devices with their start and end apart: 40 -> 194, of which waited for: 37 -> 104; matrix products, arithmetic and copies ran while one was open for 8% -> 25% of each run, Pallas kernels for 0% -> 7%
where the time goes in v1:
time: 1840 us; the launch traced here: 1830 us
  waiting for transfers between devices  960 us (52%)
  matrix products  279 us (15%)
  local copies, waits for them, and re-layouts  155 us (8%)
  Pallas kernels  147 us (8%)
  other arithmetic  133 us (7%)
  starting transfers between devices  132 us (7%)
  between operations  24.1 us (1%)
    ppermute x178, waiting for transfers between devices, flip(): return lax.ppermute(values, axis, [(i, i ^ bit) for i in range(count)])  956 us
    ppermute x178, starting transfers between devices, flip(): return lax.ppermute(values, axis, [(i, i ^ bit) for i in range(count)])  129 us
    dot_general x15, matrix products, times_right(): return jnp.dot(left, right, preferred_element_type=f32).astype(out)  99.8 us
    dot_general x15, matrix products, times_trans(): lax.dot_general(left, right, (((1,), (1,)), ((), ())), preferred_element_...  91.5 us
    pallas_call x24, Pallas kernels, move(): pl.pallas_call(partial(move_kernel, tuple(loads), tuple(stores), len(piec...  88.6 us
    dot_general x14, matrix products, trans_times(): lax.dot_general(left, right, (((0,), (0,)), ((), ())), preferred_element_...  79.3 us
    unnamed x548, local copies, waits for them, and re-layouts  51.8 us
  transfers between devices with their start and end apart: 194, of which 104 were waited for; matrix products, arithmetic and copies ran while one was open for 25% of the time, Pallas kernels for 7%

profile of v1, /device:TPU:0, one launch (start us, length us, event | category | flops | bytes accessed | tf_op | source)
XLA Modules:
  0.0 1831.2 jit_solution(13491542346533417369)
XLA Ops:
  15.1 20.8 %collective-permute-done.1 = bf16[1,192,128]{2,1,0:T(8,128)(2,1)S(1)} collective-permute-done((bf16[1,192,128]{2,1,0:T(8,128)(2,1)S(1)}, bf16[1,192,128]{2,1,0:T(8,128)(2,1)S(1)}, u32[]{:S(2)}, u32[]{:S(2)}) %collective-permute-start.1) | collective-permute-done | bytes 49184 | tf_op jit(solution)/shard_map/ppermute | solution.py:47
  41.6 10.3 collective-permute-done.2
  71.3 22.7 %collective-permute-done.13.refs_2_ = bf16[512,512]{1,0:T(8,128)(2,1)S(1)} collective-permute-done((bf16[512,512]{1,0:T(8,128)(2,1)S(1)}, bf16[512,512]{1,0:T(8,128)(2,1)S(1)}, u32[]{:S(2)}, u32[]{:S(2)}) %collective-permute-start.13) | collective-permute-done | bytes 524320 | tf_op jit(solution)/shard_map/ppermute | solution.py:47
  97.7 22.6 %collective-permute-done.14.refs_3_ = bf16[512,512]{1,0:T(8,128)(2,1)S(1)} collective-permute-done((bf16[512,512]{1,0:T(8,128)(2,1)S(1)}, bf16[512,512]{1,0:T(8,128)(2,1)S(1)}, u32[]{:S(2)}, u32[]{:S(2)}) %collective-permute-start.14) | collective-permute-done | bytes 524320 | tf_op jit(solution)/shard_map/ppermute | solution.py:47
  133.8 22.9 %collective-permute-done.6.refs_0_ = bf16[128,4096]{1,0:T(8,128)(2,1)} collective-permute-done((bf16[128,4096]{1,0:T(8,128)(2,1)S(1)}, bf16[128,4096]{1,0:T(8,128)(2,1)}, u32[]{:S(2)}, u32[]{:S(2)}) %collective-permute-start.6) | collective-permute-done | bytes 1048608 | tf_op jit(solution)/shard_map/ppermute | solution.py:47
  158.8 26.7 %collective-permute-done.7.refs_1_ = bf16[512,640]{1,0:T(8,128)(2,1)S(1)} collective-permute-done((bf16[512,640]{1,0:T(8,128)(2,1)S(1)}, bf16[512,640]{1,0:T(8,128)(2,1)S(1)}, u32[]{:S(2)}, u32[]{:S(2)}) %collective-permute-start.7) | collective-permute-done | bytes 655392 | tf_op jit(solution)/shard_map/ppermute | solution.py:47
  188.0 27.8 %collective-permute-done.16.refs_3_ = bf16[512,640]{1,0:T(8,128)(2,1)S(1)} collective-permute-done((bf16[512,640]{1,0:T(8,128)(2,1)S(1)}, bf16[512,640]{1,0:T(8,128)(2,1)S(1)}, u32[]{:S(2)}, u32[]{:S(2)}) %collective-permute-start.16) | collective-permute-done | bytes 655392 | tf_op jit(solution)/shard_map/ppermute | solution.py:47
  228.5 15.2 collective-permute-done.8.refs_1_
  246.1 20.8 %collective-permute-done.9.refs_1_ = bf16[256,2048]{1,0:T(8,128)(2,1)S(1)} collective-permute-done((bf16[256,2048]{1,0:T(8,128)(2,1)S(1)}, bf16[256,2048]{1,0:T(8,128)(2,1)S(1)}, u32[]{:S(2)}, u32[]{:S(2)}) %collective-permute-start.9) | collective-permute-done | bytes 1048608 | tf_op jit(solution)/shard_map/ppermute | solution.py:47
  286.2 7.0 shard_map.595
  296.5 32.0 %collective-permute-done.17.refs_1_ = bf16[512,1280]{1,0:T(8,128)(2,1)} collective-permute-done((bf16[512,1280]{1,0:T(8,128)(2,1)}, bf16[512,1280]{1,0:T(8,128)(2,1)}, u32[]{:S(2)}, u32[]{:S(2)}) %collective-permute-start.17) | collective-permute-done | bytes 1310752 | tf_op jit(solution)/shard_map/ppermute | solution.py:47
  336.4 10.4 fusion.257.k_ref
  352.9 8.2 fusion.61.v_ref
  362.9 11.3 convolution_add_fusion.1.q_ref
  374.1 11.5 shard_map.596
  385.6 37.8 %collective-permute-done.18.refs_1_ = bf16[512,2048]{1,0:T(8,128)(2,1)} collective-permute-done((bf16[512,2048]{1,0:T(8,128)(2,1)S(1)}, bf16[512,2048]{1,0:T(8,128)(2,1)}, u32[]{:S(2)}, u32[]{:S(2)}) %collective-permute-start.18) | collective-permute-done | bytes 2097184 | tf_op jit(solution)/shard_map/ppermute | solution.py:47
  440.3 113.8 %collective-permute-done.19.refs_1_ = bf16[512,2816]{1,0:T(8,128)(2,1)} collective-permute-done((bf16[512,2816]{1,0:T(8,128)(2,1)S(1)}, bf16[512,2816]{1,0:T(8,128)(2,1)}, u32[]{:S(2)}, u32[]{:S(2)}) %collective-permute-start.19) | collective-permute-done | bytes 2883616 | tf_op jit(solution)/shard_map/ppermute | solution.py:47
  568.3 7.9 collective-permute-done.26
  594.1 6.9 collective-permute-done.31.refs_4_
  610.2 7.6 fusion.58
  626.4 12.7 fusion.258
  646.0 9.8 add_convert_fusion.2
  664.1 11.8 collective-permute-done.40
  699.5 12.2 collective-permute-done.45
  725.0 8.9 collective-permute-done.50.refs_4_
  770.2 7.5 fusion.19
  783.1 10.5 shard_map.601
  831.6 8.3 collective-permute-done.62
  856.2 6.4 collective-permute-done.77
  899.5 23.1 %shard_map.603 = (f32[1024,512]{1,0:T(8,128)}, f32[2,4,512,2]{3,2,1,0:T(8,128)}, bf16[2,512,512]{2,1,0:T(8,128)(2,1)}, f32[2,4,512,2]{3,2,1,0:T(8,128)}, f32[2,4,2,512]{3,2,1,0:T(2,128)}) custom-call(bf16[1024,512]{1,0:T(8,128)(2,1)} %bitcast.883, f32[1024,512]{1,0:T(8,128)} %bitcast.862, f32[2,4,512,2]{3,2,1,0:T(8,128)} %bitcast.864, ...), custom_call_target="tpu_custom_call" | custom-call | tf_op jit(solution)/shard_map/pallas_call | solution.py:691
  927.2 9.9 reduce-window.16
  953.3 6.6 add_convert_fusion.1
  963.6 7.8 convolution_convert_fusion.10
  1005.9 22.6 %collective-permute-done.82 = bf16[2,128,1024]{2,1,0:T(8,128)(2,1)S(1)} collective-permute-done((bf16[2,128,1024]{2,1,0:T(8,128)(2,1)S(1)}, bf16[2,128,1024]{2,1,0:T(8,128)(2,1)S(1)}, u32[]{:S(2)}, u32[]{:S(2)}) %collective-permute-start.82) | collective-permute-done | bytes 524320 | tf_op jit(solution)/shard_map/ppermute | solution.py:47
  1049.3 9.8 collective-permute-done.101.refs_4_
  1061.7 6.4 collective-permute-done.99.refs_2_
  1088.3 12.2 collective-permute-done.108.refs_2_
  1102.8 10.8 collective-permute-done.112.refs_6_
  1120.1 12.2 fusion.10
  1133.6 11.8 convolution_convert_fusion
  1145.5 9.4 convolution_convert_fusion.9
  1155.0 12.2 convolution_convert_fusion.5
  1187.0 10.9 collective-permute-done.117
  1211.8 9.3 collective-permute-done.127.refs_4_
  1252.8 13.7 shard_map.608
  1266.5 10.4 convolution_convert_fusion.1
  1288.5 10.3 convolution_convert_fusion.2
  1307.7 10.0 convolution_convert_fusion.3
  1317.8 10.6 fusion.259
  1328.3 8.4 fusion.260
  1336.7 17.7 add_convert_fusion
  1358.3 44.7 %collective-permute-done.150 = bf16[2,128,64]{2,1,0:T(8,128)(2,1)S(1)} collective-permute-done((bf16[2,128,64]{2,1,0:T(8,128)(2,1)S(1)}, bf16[2,128,64]{2,1,0:T(8,128)(2,1)S(1)}, u32[]{:S(2)}, u32[]{:S(2)}) %collective-permute-start.150) | collective-permute-done | bytes 32800 | tf_op jit(solution)/shard_map/ppermute | solution.py:47
  1442.6 17.0 collective-permute-done.168
  1461.3 19.0 %collective-permute-done.145 = bf16[2,128,2048]{2,1,0:T(8,128)(2,1)S(1)} collective-permute-done((bf16[2,128,2048]{2,1,0:T(8,128)(2,1)S(1)}, bf16[2,128,2048]{2,1,0:T(8,128)(2,1)S(1)}, u32[]{:S(2)}, u32[]{:S(2)}) %collective-permute-start.145) | collective-permute-done | bytes 1048608 | tf_op jit(solution)/shard_map/ppermute | solution.py:47
  1512.4 11.5 concatenate.409
  1535.8 30.9 %collective-permute-done.163 = bf16[2,256,1280]{2,1,0:T(8,128)(2,1)} collective-permute-done((bf16[2,256,1280]{2,1,0:T(8,128)(2,1)}, bf16[2,256,1280]{2,1,0:T(8,128)(2,1)}, u32[]{:S(2)}, u32[]{:S(2)}) %collective-permute-start.163) | collective-permute-done | bytes 1310752 | tf_op jit(solution)/shard_map/ppermute | solution.py:47
  1575.2 11.9 collective-permute-done.156
  1612.6 42.5 %collective-permute-done.157 = bf16[2,2,784,128]{3,2,1,0:T(8,128)(2,1)} collective-permute-done((bf16[2,2,784,128]{3,2,1,0:T(8,128)(2,1)}, bf16[2,2,784,128]{3,2,1,0:T(8,128)(2,1)}, u32[]{:S(2)}, u32[]{:S(2)}) %collective-permute-start.157) | collective-permute-done | bytes 802848 | tf_op jit(solution)/shard_map/ppermute | solution.py:47
  1656.6 21.0 %collective-permute-done.165 = bf16[2,512,512]{2,1,0:T(8,128)(2,1)} collective-permute-done((bf16[2,512,512]{2,1,0:T(8,128)(2,1)S(1)}, bf16[2,512,512]{2,1,0:T(8,128)(2,1)}, u32[]{:S(2)}, u32[]{:S(2)}) %collective-permute-start.165) | collective-permute-done | bytes 1048608 | tf_op jit(solution)/shard_map/ppermute | solution.py:47
  1689.1 9.7 collective-permute-done.171
  1702.7 34.4 %collective-permute-done.166 = bf16[2,512,512]{2,1,0:T(8,128)(2,1)S(1)} collective-permute-done((bf16[2,512,512]{2,1,0:T(8,128)(2,1)S(1)}, bf16[2,512,512]{2,1,0:T(8,128)(2,1)S(1)}, u32[]{:S(2)}, u32[]{:S(2)}) %collective-permute-start.166) | collective-permute-done | bytes 1048608 | tf_op jit(solution)/shard_map/ppermute | solution.py:47
  1747.9 36.6 %collective-permute-done.167 = bf16[2,512,512]{2,1,0:T(8,128)(2,1)} collective-permute-done((bf16[2,512,512]{2,1,0:T(8,128)(2,1)S(1)}, bf16[2,512,512]{2,1,0:T(8,128)(2,1)}, u32[]{:S(2)}, u32[]{:S(2)}) %collective-permute-start.167) | collective-permute-done | bytes 1048608 | tf_op jit(solution)/shard_map/ppermute | solution.py:47
  1788.1 12.0 collective-permute-done.173
  1808.3 10.4 collective-permute-done.174
  (1406 shorter events, 716.9 us)
Async XLA Ops:
  7.3 329.2 %all-gather.14.cloned.1.call-start = ((), (), s32[]{:S(2)}) async-start(), calls=%async_computation.12 | async-start | bytes 6291456 | tf_op jit(solution)/shard_map/all_gather | solution.py:198
  8.7 31.7 %collective-permute-start = (bf16[512,512]{1,0:T(8,128)(2,1)S(1)}, bf16[512,512]{1,0:T(8,128)(2,1)}, u32[]{:S(2)}, u32[]{:S(2)}) collective-permute-start(bf16[512,512]{1,0:T(8,128)(2,1)S(1)} %get-tuple-element.423), channel_id=1, source_target_pairs={{0,8},{4,12},{8,0},{12,4},{16,24},{20,28},{24,16},{28,20},{1,9},{5... | collective-permute-start | bytes 1572872 | tf_op jit(solution)/shard_map/ppermute | solution.py:47
  11.8 28.6 %collective-permute-start.11 = (bf16[512,512]{1,0:T(8,128)(2,1)S(1)}, bf16[512,512]{1,0:T(8,128)(2,1)S(1)}, u32[]{:S(2)}, u32[]{:S(2)}) collective-permute-start(bf16[512,512]{1,0:T(8,128)(2,1)S(1)} %get-tuple-element.422.refs_0_), channel_id=1, source_target_pairs={{0,16},{4,20},{8,24},{12,28},{16,0},{20,4},{24,8},{28,12},{1,17},{... | collective-permute-start | bytes 1572872 | tf_op jit(solution)/shard_map/ppermute | solution.py:47
  40.4 25.5 %collective-permute-start.12 = (bf16[512,512]{1,0:T(8,128)(2,1)}, bf16[512,512]{1,0:T(8,128)(2,1)}, u32[]{:S(2)}, u32[]{:S(2)}) collective-permute-start(bf16[512,512]{1,0:T(8,128)(2,1)} %collective-permute-done.refs_1_), channel_id=1, source_target_pairs={{0,16},{4,20},{8,24},{12,28},{16,0},{20,4},{24,8},{28,12},{1,17},{... | collective-permute-start | bytes 1572872 | tf_op jit(solution)/shard_map/ppermute | solution.py:47
  69.0 25.0 %collective-permute-start.13 = (bf16[512,512]{1,0:T(8,128)(2,1)S(1)}, bf16[512,512]{1,0:T(8,128)(2,1)S(1)}, u32[]{:S(2)}, u32[]{:S(2)}) collective-permute-start(bf16[512,512]{1,0:T(8,128)(2,1)S(1)} %get-tuple-element.103.refs_0_), channel_id=1, source_target_pairs={{0,16},{4,20},{8,24},{12,28},{16,0},{20,4},{24,8},{28,12},{1,17},{... | collective-permute-start | bytes 1572872 | tf_op jit(solution)/shard_map/ppermute | solution.py:47
  94.8 25.6 %collective-permute-start.14 = (bf16[512,512]{1,0:T(8,128)(2,1)S(1)}, bf16[512,512]{1,0:T(8,128)(2,1)S(1)}, u32[]{:S(2)}, u32[]{:S(2)}) collective-permute-start(bf16[512,512]{1,0:T(8,128)(2,1)S(1)} %collective-permute-done.5.refs_1_), channel_id=1, source_target_pairs={{0,16},{4,20},{8,24},{12,28},{16,0},{20,4},{24,8},{28,12},{1,17},{... | collective-permute-start | bytes 1572872 | tf_op jit(solution)/shard_map/ppermute | solution.py:47
  124.2 222.6 %all-gather.12.cloned.1.call-start = ((), (), s32[]{:S(2)}) async-start(), calls=%async_computation.11 | async-start | bytes 7864320 | tf_op jit(solution)/shard_map/all_gather | solution.py:198
  131.6 25.1 %collective-permute-start.6 = (bf16[128,4096]{1,0:T(8,128)(2,1)S(1)}, bf16[128,4096]{1,0:T(8,128)(2,1)}, u32[]{:S(2)}, u32[]{:S(2)}) collective-permute-start(bf16[128,4096]{1,0:T(8,128)(2,1)S(1)} %constant_dynamic-slice_fusion.24), channel_id=1, source_target_pairs={{0,8},{4,12},{8,0},{12,4},{16,24},{20,28},{24,16},{28,20},{1,9},{5... | collective-permute-start | bytes 3145736 | tf_op jit(solution)/shard_map/ppermute | solution.py:47
  156.7 28.8 %collective-permute-start.7 = (bf16[512,640]{1,0:T(8,128)(2,1)S(1)}, bf16[512,640]{1,0:T(8,128)(2,1)S(1)}, u32[]{:S(2)}, u32[]{:S(2)}) collective-permute-start(bf16[512,640]{1,0:T(8,128)(2,1)S(1)} %get-tuple-element.98), channel_id=1, source_target_pairs={{0,8},{4,12},{8,0},{12,4},{16,24},{20,28},{24,16},{28,20},{1,9},{5... | collective-permute-start | bytes 1966088 | tf_op jit(solution)/shard_map/ppermute | solution.py:47
  157.0 30.7 %collective-permute-start.15 = (bf16[512,640]{1,0:T(8,128)(2,1)S(1)}, bf16[512,640]{1,0:T(8,128)(2,1)S(1)}, u32[]{:S(2)}, u32[]{:S(2)}) collective-permute-start(bf16[512,640]{1,0:T(8,128)(2,1)S(1)} %get-tuple-element.105.refs_0_), channel_id=1, source_target_pairs={{0,16},{4,20},{8,24},{12,28},{16,0},{20,4},{24,8},{28,12},{1,17},{... | collective-permute-start | bytes 1966088 | tf_op jit(solution)/shard_map/ppermute | solution.py:47
  187.7 28.2 %collective-permute-start.16 = (bf16[512,640]{1,0:T(8,128)(2,1)S(1)}, bf16[512,640]{1,0:T(8,128)(2,1)S(1)}, u32[]{:S(2)}, u32[]{:S(2)}) collective-permute-start(bf16[512,640]{1,0:T(8,128)(2,1)S(1)} %collective-permute-done.7.refs_1_), channel_id=1, source_target_pairs={{0,16},{4,20},{8,24},{12,28},{16,0},{20,4},{24,8},{28,12},{1,17},{... | collective-permute-start | bytes 1966088 | tf_op jit(solution)/shard_map/ppermute | solution.py:47
  220.1 142.7 %all-gather.10.cloned.1.call-start = ((), (), s32[]{:S(2)}) async-start(), calls=%async_computation.10 | async-start | bytes 6291456 | tf_op jit(solution)/shard_map/all_gather | solution.py:198
  222.9 206.5 %all-gather.16.cloned.1.call-start = ((), (), s32[]{:S(2)}) async-start(), calls=%async_computation.13 | async-start | bytes 7864320 | tf_op jit(solution)/shard_map/all_gather | solution.py:198
  243.8 23.2 %collective-permute-start.9 = (bf16[256,2048]{1,0:T(8,128)(2,1)S(1)}, bf16[256,2048]{1,0:T(8,128)(2,1)S(1)}, u32[]{:S(2)}, u32[]{:S(2)}) collective-permute-start(bf16[256,2048]{1,0:T(8,128)(2,1)S(1)} %pad_maximum_fusion.6), channel_id=1, source_target_pairs={{0,8},{4,12},{8,0},{12,4},{16,24},{20,28},{24,16},{28,20},{1,9},{5... | collective-permute-start | bytes 3145736 | tf_op jit(solution)/shard_map/ppermute | solution.py:47
  244.1 30.8 %collective-permute-start.21 = (bf16[128,4096]{1,0:T(8,128)(2,1)}, bf16[128,4096]{1,0:T(8,128)(2,1)}, u32[]{:S(2)}, u32[]{:S(2)}) collective-permute-start(bf16[128,4096]{1,0:T(8,128)(2,1)} %collective-permute-done.6.refs_0_), channel_id=1, source_target_pairs={{0,2},{1,3},{2,0},{3,1},{4,6},{5,7},{6,4},{7,5},{8,10},{9,11},{10,... | collective-permute-start | bytes 3145736 | tf_op jit(solution)/shard_map/ppermute | solution.py:47
  267.0 65.6 %collective-permute-start.10 = (bf16[256,2816]{1,0:T(8,128)(2,1)}, bf16[256,2816]{1,0:T(8,128)(2,1)}, u32[]{:S(2)}, u32[]{:S(2)}) collective-permute-start(bf16[256,2816]{1,0:T(8,128)(2,1)} %get-tuple-element.101), channel_id=1, source_target_pairs={{0,8},{4,12},{8,0},{12,4},{16,24},{20,28},{24,16},{28,20},{1,9},{5... | collective-permute-start | bytes 4325384 | tf_op jit(solution)/shard_map/ppermute | solution.py:47
  271.1 57.4 %collective-permute-start.17 = (bf16[512,1280]{1,0:T(8,128)(2,1)}, bf16[512,1280]{1,0:T(8,128)(2,1)}, u32[]{:S(2)}, u32[]{:S(2)}) collective-permute-start(bf16[512,1280]{1,0:T(8,128)(2,1)} %shard_map.589.refs_0_), channel_id=1, source_target_pairs={{0,16},{4,20},{8,24},{12,28},{16,0},{20,4},{24,8},{28,12},{1,17},{... | collective-permute-start | bytes 3932168 | tf_op jit(solution)/shard_map/ppermute | solution.py:47
  332.0 294.4 %all-gather.18.cloned.1.call-start = ((), (), s32[]{:S(2)}) async-start(), calls=%async_computation.14 | async-start | bytes 12582912 | tf_op jit(solution)/shard_map/all_gather | solution.py:198
  336.3 87.0 %collective-permute-start.18 = (bf16[512,2048]{1,0:T(8,128)(2,1)S(1)}, bf16[512,2048]{1,0:T(8,128)(2,1)}, u32[]{:S(2)}, u32[]{:S(2)}) collective-permute-start(bf16[512,2048]{1,0:T(8,128)(2,1)S(1)} %copy-done.22), channel_id=1, source_target_pairs={{0,16},{4,20},{8,24},{12,28},{16,0},{20,4},{24,8},{28,12},{1,17},{... | collective-permute-start | bytes 6291464 | tf_op jit(solution)/shard_map/ppermute | solution.py:47
  427.7 218.4 %all-gather.8.cloned.1.call-start = ((), (), s32[]{:S(2)}) async-start(), calls=%async_computation.9 | async-start | bytes 7864320 | tf_op jit(solution)/shard_map/all_gather | solution.py:198
  429.5 124.6 %collective-permute-start.19 = (bf16[512,2816]{1,0:T(8,128)(2,1)S(1)}, bf16[512,2816]{1,0:T(8,128)(2,1)}, u32[]{:S(2)}, u32[]{:S(2)}) collective-permute-start(bf16[512,2816]{1,0:T(8,128)(2,1)S(1)} %copy-done.15), channel_id=1, source_target_pairs={{0,16},{4,20},{8,24},{12,28},{16,0},{20,4},{24,8},{28,12},{1,17},{... | collective-permute-start | bytes 8650760 | tf_op jit(solution)/shard_map/ppermute | solution.py:47
  436.9 124.2 %collective-permute-start.23 = (bf16[2,2,128,2048]{3,2,1,0:T(8,128)(2,1)}, bf16[2,2,128,2048]{3,2,1,0:T(8,128)(2,1)}, u32[]{:S(2)}, u32[]{:S(2)}) collective-permute-start(bf16[2,2,128,2048]{3,2,1,0:T(8,128)(2,1)} %dynamic-slice_bitcast_fusion.7), channel_id=1, source_target_pairs={{0,1},{1,0},{2,3},{3,2},{4,5},{5,4},{6,7},{7,6},{8,9},{9,8},{10,11... | collective-permute-start | bytes 6291464 | tf_op jit(solution)/shard_map/ppermute | solution.py:47
  559.1 211.1 %all-gather.20.cloned.1.call-start = ((), (), s32[]{:S(2)}) async-start(), calls=%async_computation.15 | async-start | bytes 9437184 | tf_op jit(solution)/shard_map/all_gather | solution.py:198
  690.8 269.1 %reduce-scatter.10.cloned.1.call-start = ((), (), s32[]{:S(2)}) async-start(), calls=%async_computation.16 | async-start | bytes 2621440 | tf_op jit(solution)/shard_map/reduce_scatter | solution.py:267
  887.9 232.1 %reduce-scatter.12.cloned.1.call-start = ((), (), s32[]{:S(2)}) async-start(), calls=%async_computation.17 | async-start | bytes 5242880 | tf_op jit(solution)/shard_map/reduce_scatter | solution.py:267
  943.0 28.5 %collective-permute-start.84 = (bf16[2,2,128,256]{3,2,1,0:T(8,128)(2,1)}, bf16[2,2,128,256]{3,2,1,0:T(8,128)(2,1)}, u32[]{:S(2)}, u32[]{:S(2)}) collective-permute-start(bf16[2,2,128,256]{3,2,1,0:T(8,128)(2,1)} %fusion.132), channel_id=1, source_target_pairs={{0,1},{1,0},{2,3},{3,2},{4,5},{5,4},{6,7},{7,6},{8,9},{9,8},{10,11... | collective-permute-start | bytes 786440 | tf_op jit(solution)/shard_map/ppermute | solution.py:47
  963.2 34.2 %collective-permute-start.79 = (bf16[2,2,128,2048]{3,2,1,0:T(8,128)(2,1)}, bf16[2,2,128,2048]{3,2,1,0:T(8,128)(2,1)S(1)}, u32[]{:S(2)}, u32[]{:S(2)}) collective-permute-start(bf16[2,2,128,2048]{3,2,1,0:T(8,128)(2,1)} %dynamic-slice_bitcast_fusion.3), channel_id=1, source_target_pairs={{0,1},{1,0},{2,3},{3,2},{4,5},{5,4},{6,7},{7,6},{8,9},{9,8},{10,11... | collective-permute-start | bytes 6291464 | tf_op jit(solution)/shard_map/ppermute | solution.py:47
  971.4 278.2 %reduce-scatter.14.cloned.1.call-start = ((), (), s32[]{:S(2)}) async-start(), calls=%async_computation.18 | async-start | bytes 12582912 | tf_op jit(solution)/shard_map/reduce_scatter | solution.py:262
  1000.0 28.5 %collective-permute-start.82 = (bf16[2,128,1024]{2,1,0:T(8,128)(2,1)S(1)}, bf16[2,128,1024]{2,1,0:T(8,128)(2,1)S(1)}, u32[]{:S(2)}, u32[]{:S(2)}) collective-permute-start(bf16[2,128,1024]{2,1,0:T(8,128)(2,1)S(1)} %dynamic-slice_bitcast_fusion.34), channel_id=1, source_target_pairs={{0,8},{4,12},{8,0},{12,4},{16,24},{20,28},{24,16},{28,20},{1,9},{5... | collective-permute-start | bytes 1572872 | tf_op jit(solution)/shard_map/ppermute | solution.py:47
  1004.3 25.9 %collective-permute-start.80 = (bf16[2,128,1024]{2,1,0:T(8,128)(2,1)S(1)}, bf16[2,128,1024]{2,1,0:T(8,128)(2,1)S(1)}, u32[]{:S(2)}, u32[]{:S(2)}) collective-permute-start(bf16[2,128,1024]{2,1,0:T(8,128)(2,1)S(1)} %dynamic-slice_bitcast_fusion.35), channel_id=1, source_target_pairs={{0,2},{1,3},{2,0},{3,1},{4,6},{5,7},{6,4},{7,5},{8,10},{9,11},{10,... | collective-permute-start | bytes 1572872 | tf_op jit(solution)/shard_map/ppermute | solution.py:47
  1046.7 21.4 %collective-permute-start.99 = (bf16[128,2048]{1,0:T(8,128)(2,1)S(1)}, bf16[128,2048]{1,0:T(8,128)(2,1)S(1)}, u32[]{:S(2)}, u32[]{:S(2)}) collective-permute-start(bf16[128,2048]{1,0:T(8,128)(2,1)S(1)} %get-tuple-element.357.refs_0_), channel_id=1, source_target_pairs={{0,8},{4,12},{8,0},{12,4},{16,24},{20,28},{24,16},{28,20},{1,9},{5... | collective-permute-start | bytes 1572872 | tf_op jit(solution)/shard_map/ppermute | solution.py:47
  1049.3 26.2 %collective-permute-start.98 = (bf16[128,2048]{1,0:T(8,128)(2,1)S(1)}, bf16[128,2048]{1,0:T(8,128)(2,1)S(1)}, u32[]{:S(2)}, u32[]{:S(2)}) collective-permute-start(bf16[128,2048]{1,0:T(8,128)(2,1)S(1)} %get-tuple-element.357.refs_0_), channel_id=1, source_target_pairs={{0,1},{1,0},{2,3},{3,2},{4,5},{5,4},{6,7},{7,6},{8,9},{9,8},{10,11... | collective-permute-start | bytes 1572872 | tf_op jit(solution)/shard_map/ppermute | solution.py:47
  1145.4 358.3 %reduce-scatter.26.cloned.1.call-start = ((), (), s32[]{:S(2)}) async-start(), calls=%async_computation.24 | async-start | bytes 6291456 | tf_op jit(solution)/shard_map/reduce_scatter | solution.py:262
  1154.9 348.8 %reduce-scatter.24.cloned.1.call-start = ((), (), s32[]{:S(2)}) async-start(), calls=%async_computation.23 | async-start | bytes 1572864 | tf_op jit(solution)/shard_map/reduce_scatter | solution.py:262
  1174.3 352.0 %reduce-scatter.22.cloned.1.call-start = ((), (), s32[]{:S(2)}) async-start(), calls=%async_computation.22 | async-start | bytes 3145728 | tf_op jit(solution)/shard_map/reduce_scatter | solution.py:262
  1243.2 288.1 %reduce-scatter.20.cloned.1.call-start = ((), (), s32[]{:S(2)}) async-start(), calls=%async_computation.21 | async-start | bytes 6291456 | tf_op jit(solution)/shard_map/reduce_scatter | solution.py:262
  1277.0 254.2 %reduce-scatter.18.cloned.1.call-start = ((), (), s32[]{:S(2)}) async-start(), calls=%async_computation.20 | async-start | bytes 6291456 | tf_op jit(solution)/shard_map/reduce_scatter | solution.py:262
  1298.8 234.8 %reduce-scatter.16.cloned.1.call-start = ((), (), s32[]{:S(2)}) async-start(), calls=%async_computation.19 | async-start | bytes 6291456 | tf_op jit(solution)/shard_map/reduce_scatter | solution.py:262
  1307.5 46.9 %collective-permute-start.147 = (bf16[2,2,128,128]{3,2,1,0:T(8,128)(2,1)}, bf16[2,2,128,128]{3,2,1,0:T(8,128)(2,1)}, u32[]{:S(2)}, u32[]{:S(2)}) collective-permute-start(bf16[2,2,128,128]{3,2,1,0:T(8,128)(2,1)} %dynamic-slice_bitcast_fusion.65), channel_id=1, source_target_pairs={{0,1},{1,0},{2,3},{3,2},{4,5},{5,4},{6,7},{7,6},{8,9},{9,8},{10,11... | collective-permute-start | bytes 393224 | tf_op jit(solution)/shard_map/ppermute | solution.py:47
  1307.7 102.4 %collective-permute-start.133 = (bf16[2,256,2048]{2,1,0:T(8,128)(2,1)}, bf16[2,256,2048]{2,1,0:T(8,128)(2,1)S(1)}, u32[]{:S(2)}, u32[]{:S(2)}) collective-permute-start(bf16[2,256,2048]{2,1,0:T(8,128)(2,1)} %dynamic-slice_bitcast_fusion.1), channel_id=1, source_target_pairs={{0,16},{4,20},{8,24},{12,28},{16,0},{20,4},{24,8},{28,12},{1,17},{... | collective-permute-start | bytes 6291464 | tf_op jit(solution)/shard_map/ppermute | solution.py:47
  1355.5 47.5 %collective-permute-start.150 = (bf16[2,128,64]{2,1,0:T(8,128)(2,1)S(1)}, bf16[2,128,64]{2,1,0:T(8,128)(2,1)S(1)}, u32[]{:S(2)}, u32[]{:S(2)}) collective-permute-start(bf16[2,128,64]{2,1,0:T(8,128)(2,1)S(1)} %dynamic-slice_bitcast_fusion.67), channel_id=1, source_target_pairs={{0,8},{4,12},{8,0},{12,4},{16,24},{20,28},{24,16},{28,20},{1,9},{5... | collective-permute-start | bytes 98312 | tf_op jit(solution)/shard_map/ppermute | solution.py:47
  1357.3 47.0 %collective-permute-start.148 = (bf16[2,128,64]{2,1,0:T(8,128)(2,1)S(1)}, bf16[2,128,64]{2,1,0:T(8,128)(2,1)S(1)}, u32[]{:S(2)}, u32[]{:S(2)}) collective-permute-start(bf16[2,128,64]{2,1,0:T(8,128)(2,1)S(1)} %dynamic-slice_bitcast_fusion.68), channel_id=1, source_target_pairs={{0,2},{1,3},{2,0},{3,1},{4,6},{5,7},{6,4},{7,5},{8,10},{9,11},{10,... | collective-permute-start | bytes 98312 | tf_op jit(solution)/shard_map/ppermute | solution.py:47
  1412.8 23.2 %collective-permute-start.142 = (bf16[2,2,128,4096]{3,2,1,0:T(8,128)(2,1)S(1)}, bf16[2,2,128,4096]{3,2,1,0:T(8,128)(2,1)S(1)}, u32[]{:S(2)}, u32[]{:S(2)}) collective-permute-start(bf16[2,2,128,4096]{3,2,1,0:T(8,128)(2,1)S(1)} %dynamic-slice_bitcast_fusion), channel_id=1, source_target_pairs={{0,1},{1,0},{2,3},{3,2},{4,5},{5,4},{6,7},{7,6},{8,9},{9,8},{10,11... | collective-permute-start | bytes 12582920 | tf_op jit(solution)/shard_map/ppermute | solution.py:47
  1414.9 26.5 %collective-permute-start.135 = (bf16[128,2048]{1,0:T(8,128)(2,1)S(1)}, bf16[128,2048]{1,0:T(8,128)(2,1)}, u32[]{:S(2)}, u32[]{:S(2)}) collective-permute-start(bf16[128,2048]{1,0:T(8,128)(2,1)S(1)} %copy-done.59), channel_id=1, source_target_pairs={{0,2},{1,3},{2,0},{3,1},{4,6},{5,7},{6,4},{7,5},{8,10},{9,11},{10,... | collective-permute-start | bytes 1572872 | tf_op jit(solution)/shard_map/ppermute | solution.py:47
  1415.8 70.3 %collective-permute-start.134 = (bf16[128,2048]{1,0:T(8,128)(2,1)S(1)}, bf16[128,2048]{1,0:T(8,128)(2,1)}, u32[]{:S(2)}, u32[]{:S(2)}) collective-permute-start(bf16[128,2048]{1,0:T(8,128)(2,1)S(1)} %copy-done.59), channel_id=1, source_target_pairs={{0,1},{1,0},{2,3},{3,2},{4,5},{5,4},{6,7},{7,6},{8,9},{9,8},{10,11... | collective-permute-start | bytes 1572872 | tf_op jit(solution)/shard_map/ppermute | solution.py:47
  1433.5 26.1 %collective-permute-start.168 = (bf16[256,2048]{1,0:T(8,128)(2,1)S(1)}, bf16[256,2048]{1,0:T(8,128)(2,1)S(1)}, u32[]{:S(2)}, u32[]{:S(2)}) collective-permute-start(bf16[256,2048]{1,0:T(8,128)(2,1)S(1)} %get-tuple-element.147), channel_id=1, source_target_pairs={{0,8},{4,12},{8,0},{12,4},{16,24},{20,28},{24,16},{28,20},{1,9},{5... | collective-permute-start | bytes 3145736 | tf_op jit(solution)/shard_map/ppermute | solution.py:47
  1438.2 42.1 %collective-permute-start.145 = (bf16[2,128,2048]{2,1,0:T(8,128)(2,1)S(1)}, bf16[2,128,2048]{2,1,0:T(8,128)(2,1)S(1)}, u32[]{:S(2)}, u32[]{:S(2)}) collective-permute-start(bf16[2,128,2048]{2,1,0:T(8,128)(2,1)S(1)} %dynamic-slice_bitcast_fusion.15), channel_id=1, source_target_pairs={{0,8},{4,12},{8,0},{12,4},{16,24},{20,28},{24,16},{28,20},{1,9},{5... | collective-permute-start | bytes 3145736 | tf_op jit(solution)/shard_map/ppermute | solution.py:47
  1441.5 44.5 %collective-permute-start.136 = (bf16[128,2048]{1,0:T(8,128)(2,1)}, bf16[128,2048]{1,0:T(8,128)(2,1)S(1)}, u32[]{:S(2)}, u32[]{:S(2)}) collective-permute-start(bf16[128,2048]{1,0:T(8,128)(2,1)} %collective-permute-done.135.refs_2_), channel_id=1, source_target_pairs={{0,1},{1,0},{2,3},{3,2},{4,5},{5,4},{6,7},{7,6},{8,9},{9,8},{10,11... | collective-permute-start | bytes 1572872 | tf_op jit(solution)/shard_map/ppermute | solution.py:47
  1441.7 41.1 %collective-permute-start.143 = (bf16[2,128,2048]{2,1,0:T(8,128)(2,1)S(1)}, bf16[2,128,2048]{2,1,0:T(8,128)(2,1)S(1)}, u32[]{:S(2)}, u32[]{:S(2)}) collective-permute-start(bf16[2,128,2048]{2,1,0:T(8,128)(2,1)S(1)} %dynamic-slice_bitcast_fusion.16), channel_id=1, source_target_pairs={{0,2},{1,3},{2,0},{3,1},{4,6},{5,7},{6,4},{7,5},{8,10},{9,11},{10,... | collective-permute-start | bytes 3145736 | tf_op jit(solution)/shard_map/ppermute | solution.py:47
  1509.8 57.0 %collective-permute-start.163 = (bf16[2,256,1280]{2,1,0:T(8,128)(2,1)}, bf16[2,256,1280]{2,1,0:T(8,128)(2,1)}, u32[]{:S(2)}, u32[]{:S(2)}) collective-permute-start(bf16[2,256,1280]{2,1,0:T(8,128)(2,1)} %pad_maximum_fusion.5), channel_id=1, source_target_pairs={{0,16},{4,20},{8,24},{12,28},{16,0},{20,4},{24,8},{28,12},{1,17},{... | collective-permute-start | bytes 3932168 | tf_op jit(solution)/shard_map/ppermute | solution.py:47
  1511.3 24.5 %collective-permute-start.153 = (bf16[128,4096]{1,0:T(8,128)(2,1)}, bf16[128,4096]{1,0:T(8,128)(2,1)}, u32[]{:S(2)}, u32[]{:S(2)}) collective-permute-start(bf16[128,4096]{1,0:T(8,128)(2,1)} %pad_maximum_fusion.8.refs_0_), channel_id=1, source_target_pairs={{0,2},{1,3},{2,0},{3,1},{4,6},{5,7},{6,4},{7,5},{8,10},{9,11},{10,... | collective-permute-start | bytes 3145736 | tf_op jit(solution)/shard_map/ppermute | solution.py:47
  1512.3 96.3 %collective-permute-start.152 = (bf16[128,4096]{1,0:T(8,128)(2,1)}, bf16[128,4096]{1,0:T(8,128)(2,1)}, u32[]{:S(2)}, u32[]{:S(2)}) collective-permute-start(bf16[128,4096]{1,0:T(8,128)(2,1)} %pad_maximum_fusion.8.refs_0_), channel_id=1, source_target_pairs={{0,1},{1,0},{2,3},{3,2},{4,5},{5,4},{6,7},{7,6},{8,9},{9,8},{10,11... | collective-permute-start | bytes 3145736 | tf_op jit(solution)/shard_map/ppermute | solution.py:47
  1525.1 42.7 %collective-permute-start.155 = (bf16[2,8,336,128]{3,2,0,1:T(8,128)(2,1)}, bf16[2,8,336,128]{3,2,0,1:T(8,128)(2,1)}, u32[]{:S(2)}, u32[]{:S(2)}) collective-permute-start(bf16[2,8,336,128]{3,2,0,1:T(8,128)(2,1)} %dynamic-slice_bitcast_fusion.8), channel_id=1, source_target_pairs={{0,1},{1,0},{2,3},{3,2},{4,5},{5,4},{6,7},{7,6},{8,9},{9,8},{10,11... | collective-permute-start | bytes 4128776 | tf_op jit(solution)/shard_map/ppermute | solution.py:47
  1535.8 72.8 %collective-permute-start.154 = (bf16[128,4096]{1,0:T(8,128)(2,1)}, bf16[128,4096]{1,0:T(8,128)(2,1)}, u32[]{:S(2)}, u32[]{:S(2)}) collective-permute-start(bf16[128,4096]{1,0:T(8,128)(2,1)} %collective-permute-done.153.refs_2_), channel_id=1, source_target_pairs={{0,1},{1,0},{2,3},{3,2},{4,5},{5,4},{6,7},{7,6},{8,9},{9,8},{10,11... | collective-permute-start | bytes 3145736 | tf_op jit(solution)/shard_map/ppermute | solution.py:47
  1573.2 25.1 %collective-permute-start.164 = (bf16[2,256,512]{2,1,0:T(8,128)(2,1)}, bf16[2,256,512]{2,1,0:T(8,128)(2,1)}, u32[]{:S(2)}, u32[]{:S(2)}) collective-permute-start(bf16[2,256,512]{2,1,0:T(8,128)(2,1)} %dynamic-slice_bitcast_fusion.29), channel_id=1, source_target_pairs={{0,16},{4,20},{8,24},{12,28},{16,0},{20,4},{24,8},{28,12},{1,17},{... | collective-permute-start | bytes 1572872 | tf_op jit(solution)/shard_map/ppermute | solution.py:47
  1573.2 30.9 %collective-permute-start.169 = (bf16[256,1280]{1,0:T(8,128)(2,1)}, bf16[256,1280]{1,0:T(8,128)(2,1)}, u32[]{:S(2)}, u32[]{:S(2)}) collective-permute-start(bf16[256,1280]{1,0:T(8,128)(2,1)} %pad_maximum_fusion.12), channel_id=1, source_target_pairs={{0,8},{4,12},{8,0},{12,4},{16,24},{20,28},{24,16},{28,20},{1,9},{5... | collective-permute-start | bytes 1966088 | tf_op jit(solution)/shard_map/ppermute | solution.py:47
  1593.0 62.1 %collective-permute-start.157 = (bf16[2,2,784,128]{3,2,1,0:T(8,128)(2,1)}, bf16[2,2,784,128]{3,2,1,0:T(8,128)(2,1)}, u32[]{:S(2)}, u32[]{:S(2)}) collective-permute-start(bf16[2,2,784,128]{3,2,1,0:T(8,128)(2,1)} %dynamic-slice_bitcast_fusion.17), channel_id=1, source_target_pairs={{0,16},{4,20},{8,24},{12,28},{16,0},{20,4},{24,8},{28,12},{1,17},{... | collective-permute-start | bytes 2408456 | tf_op jit(solution)/shard_map/ppermute | solution.py:47
  1598.3 79.3 %collective-permute-start.165 = (bf16[2,512,512]{2,1,0:T(8,128)(2,1)S(1)}, bf16[2,512,512]{2,1,0:T(8,128)(2,1)}, u32[]{:S(2)}, u32[]{:S(2)}) collective-permute-start(bf16[2,512,512]{2,1,0:T(8,128)(2,1)S(1)} %dynamic-slice_bitcast_fusion.12), channel_id=1, source_target_pairs={{0,16},{4,20},{8,24},{12,28},{16,0},{20,4},{24,8},{28,12},{1,17},{... | collective-permute-start | bytes 3145736 | tf_op jit(solution)/shard_map/ppermute | solution.py:47
  1604.1 75.1 %collective-permute-start.170 = (bf16[256,512]{1,0:T(8,128)(2,1)}, bf16[256,512]{1,0:T(8,128)(2,1)}, u32[]{:S(2)}, u32[]{:S(2)}) collective-permute-start(bf16[256,512]{1,0:T(8,128)(2,1)} %get-tuple-element.149), channel_id=1, source_target_pairs={{0,8},{4,12},{8,0},{12,4},{16,24},{20,28},{24,16},{28,20},{1,9},{5... | collective-permute-start | bytes 786440 | tf_op jit(solution)/shard_map/ppermute | solution.py:47
  1656.5 29.6 %collective-permute-start.158 = (bf16[2,784,128]{2,1,0:T(8,128)(2,1)S(1)}, bf16[2,784,128]{2,1,0:T(8,128)(2,1)S(1)}, u32[]{:S(2)}, u32[]{:S(2)}) collective-permute-start(bf16[2,784,128]{2,1,0:T(8,128)(2,1)S(1)} %dynamic-slice_bitcast_fusion.44), channel_id=1, source_target_pairs={{0,8},{4,12},{8,0},{12,4},{16,24},{20,28},{24,16},{28,20},{1,9},{5... | collective-permute-start | bytes 1204232 | tf_op jit(solution)/shard_map/ppermute | solution.py:47
  1689.0 48.1 %collective-permute-start.166 = (bf16[2,512,512]{2,1,0:T(8,128)(2,1)S(1)}, bf16[2,512,512]{2,1,0:T(8,128)(2,1)S(1)}, u32[]{:S(2)}, u32[]{:S(2)}) collective-permute-start(bf16[2,512,512]{2,1,0:T(8,128)(2,1)S(1)} %copy-done.82), channel_id=1, source_target_pairs={{0,16},{4,20},{8,24},{12,28},{16,0},{20,4},{24,8},{28,12},{1,17},{... | collective-permute-start | bytes 3145736 | tf_op jit(solution)/shard_map/ppermute | solution.py:47
  1701.2 36.9 %collective-permute-start.161 = (bf16[336,128]{1,0:T(8,128)(2,1)}, bf16[336,128]{1,0:T(8,128)(2,1)}, u32[]{:S(2)}, u32[]{:S(2)}) collective-permute-start(bf16[336,128]{1,0:T(8,128)(2,1)} %slice.1422.refs_0_), channel_id=1, source_target_pairs={{0,2},{1,3},{2,0},{3,1},{4,6},{5,7},{6,4},{7,5},{8,10},{9,11},{10,... | collective-permute-start | bytes 258056 | tf_op jit(solution)/shard_map/ppermute | solution.py:47
  1737.1 47.4 %collective-permute-start.167 = (bf16[2,512,512]{2,1,0:T(8,128)(2,1)S(1)}, bf16[2,512,512]{2,1,0:T(8,128)(2,1)}, u32[]{:S(2)}, u32[]{:S(2)}) collective-permute-start(bf16[2,512,512]{2,1,0:T(8,128)(2,1)S(1)} %copy-done.81), channel_id=1, source_target_pairs={{0,16},{4,20},{8,24},{12,28},{16,0},{20,4},{24,8},{28,12},{1,17},{... | collective-permute-start | bytes 3145736 | tf_op jit(solution)/shard_map/ppermute | solution.py:47
  1746.1 40.0 %collective-permute-start.172 = (bf16[512,512]{1,0:T(8,128)(2,1)S(1)}, bf16[512,512]{1,0:T(8,128)(2,1)S(1)}, u32[]{:S(2)}, u32[]{:S(2)}) collective-permute-start(bf16[512,512]{1,0:T(8,128)(2,1)S(1)} %get-tuple-element.151), channel_id=1, source_target_pairs={{0,8},{4,12},{8,0},{12,4},{16,24},{20,28},{24,16},{28,20},{1,9},{5... | collective-permute-start | bytes 1572872 | tf_op jit(solution)/shard_map/ppermute | solution.py:47
  (370 other events, 3643.7 us)
Sparse Core Ops, SparseCore 0:
  124.3 55.7 all-gather.13
  220.3 68.2 all-gather.11
  290.7 56.7 all-gather.9
  349.4 68.5 all-gather.15
  427.8 103.6 all-gather.17
  559.2 67.9 all-gather.7
  690.9 79.2 all-gather.19
  888.0 52.1 reduce-scatter.9
  971.5 86.8 reduce-scatter.11
  1145.6 99.1 reduce-scatter.13
  1247.1 54.2 reduce-scatter.25
  1303.5 20.3 reduce-scatter.23
  1326.8 31.8 reduce-scatter.21
  1360.8 54.3 reduce-scatter.19
  1417.4 54.2 reduce-scatter.17
  1474.5 54.3 reduce-scatter.15

commit v2 on v1

--- a/solution.py
+++ b/solution.py
@@ -212,10 +212,11 @@
         self.gates["far"] += [line, *early]
         return self.near_gather(line)
 
-    def start_line(self, name, mine, came):
+    def start_line(self, name, mine, came, widths=None):
         rows = mine.shape[0]
-        line = place([mine, came], [self.z * rows, (1 - self.z) * rows], 0, 2 * rows)
-        self.marks[name + ".pair"] = line
+        starts = [self.z * rows, (1 - self.z) * rows]
+        line = place([mine, came], starts, 0, 2 * rows, widths=widths)
+        self.marks[name + ".pair"] = line if widths is None else line[0]
         return line
 
     def finish_line(self, name, line, widths=None, hold=None):
@@ -820,11 +821,13 @@
     far_lane += [swaps["gate_up"][1]]
     attn_out_line = me.start_line("attn_out", *swaps["attn_out"])
     gate_up_line = me.start_line("gate_up", *swaps["gate_up"])
-    late_line = me.start_line("late", *swaps["late"])
     w_attn_out_more = me.near_gather(me.finish_line("attn_out", attn_out_line))
     far_lane += [swaps["late"][1]]
     units = w_down.shape[1] // 2
     channels = w_in_gate.shape[1] // 2
+    down_line, in_line = me.start_line(
+        "late", *swaps["late"], [units + w_proj.shape[1] // 2, 3 * channels]
+    )
     wide = w_value.shape[1] // 2
     w_value_all = w_value_more[:, :wide]
     query_down_all = w_value_more[:, wide:]
@@ -912,15 +915,9 @@
         query_pre, key_pre, value_low, cosine, sine, marks_laid
     )
     w_gate_up = me.near_gather(me.finish_line("gate_up", gate_up_line, hold=attended_low))
-    down_line, in_line = me.finish_line(
-        "late", late_line, [units + w_proj.shape[1] // 2, 3 * channels]
-    )
-    w_down_proj = me.near_gather(down_line)
-    w_in_out = me.near_gather(in_line)
+    w_down_proj = me.near_gather(me.finish_line("down", down_line))
     w_down_all = w_down_proj[:, :units]
     w_proj_all = w_down_proj[:, units:]
-    w_in_all = w_in_out[:, : 2 * channels]
-    w_mamba_out_all = w_in_out[:, 2 * channels :]
     attended_low = me.after(attended_low, "gate_up.line")
     attn_part = times_trans(attended_low, w_attn_out_all, jnp.bfloat16)
     attn_shard = me.reduce_tokens(attn_part)
@@ -929,7 +926,10 @@
     first_sum = hidden_shard + attn_shard
     normed_mid_f, mid_back = jax.vjp(rms_scale, first_sum, gain_mlp_all.astype(f32))
     normed_mid_shard = narrow(normed_mid_f)
-    normed_mid = me.gather_tokens(me.after(normed_mid_shard, "late.line"))
+    normed_mid = me.gather_tokens(me.after(normed_mid_shard, "down.line"))
+    w_in_out = me.near_gather(me.finish_line("in", in_line, hold=normed_mid))
+    w_in_all = w_in_out[:, : 2 * channels]
+    w_mamba_out_all = w_in_out[:, 2 * channels :]
     gate_low = narrow(times_right(normed_mid, gate_down_all))
     gate_up_pre = times_right(normed_mid, w_gate_up)
     gate_pre = gate_up_pre[:, :units] + times_right(gate_low, gate_up_all)
@@ -939,6 +939,7 @@
     mlp_part = narrow(
         times_trans(w_down_all, inner) + times_trans(w_attn_out_all, attended_low)
     )
+    mlp_part = me.after(mlp_part, "in.line")
     shared_out = narrow(me.reduce_features(mlp_part))
     projected = me.reduce_tokens(
         narrow(
@@ -1095,13 +1096,13 @@
         return lax.optimization_barrier((values, cat_shard_sum))[0]
 
     grad_w_proj, grad_w_down = me.scatter_unit("block", later(sum_proj), later(sum_down))
+    grad_w_mamba_out, grad_w_in_gate, grad_w_in_main = me.join_halves(
+        "mixer", later(sum_mamba_out), later(sum_in), parts=(1, 2)
+    )
     (grad_w_attn_out,) = me.scatter_unit("d_attn_out", later(sum_attn_out))
     (grad_w_value,) = me.scatter_unit("d_value", later(sum_value))
     (grad_w_key,) = me.scatter_unit("key", sum_key)
     (grad_w_query,) = me.scatter_unit("query", sum_query)
-    grad_w_mamba_out, grad_w_in_gate, grad_w_in_main = me.join_halves(
-        "mixer", later(sum_mamba_out), later(sum_in), parts=(1, 2)
-    )
     grad_query_up = trans_times(query_low, query_grad, jnp.bfloat16)
     grad_query_down = trans_times(normed_cat_shard, query_low_grad, jnp.bfloat16)
     grad_concat, grad_gain_attn = cat_back(

time: 1840 us -> 1820 us (0.989)
  waiting for transfers between devices: 960 us -> 927 us
    ppermute x178 -> x179, waiting for transfers between devices: 956 us -> 922 us  [flip(): return lax.ppermute(values, axis, [(i, i ^ bit) for i in range(count)])]
    ppermute x178 -> x179, starting transfers between devices: 129 us -> 136 us  [flip(): return lax.ppermute(values, axis, [(i, i ^ bit) for i in range(count)])]
    pallas_call x24 -> x25, Pallas kernels: 88.6 us -> 90.6 us  [move(): pl.pallas_call(partial(move_kernel, tuple(loads), tuple(stores), len(piec...]
    unnamed x548 -> x562, local copies, waits for them, and re-layouts: 51.8 us -> 51.2 us
  transfers between devices with their start and end apart: 194 -> 195, of which waited for: 104 -> 104; matrix products, arithmetic and copies ran while one was open for 25% -> 25% of each run, Pallas kernels for 7% -> 7%
where the time goes in v2:
time: 1820 us; the launch traced here: 1810 us
  waiting for transfers between devices  927 us (51%)
  matrix products  279 us (15%)
  local copies, waits for them, and re-layouts  158 us (9%)
  Pallas kernels  149 us (8%)
  starting transfers between devices  139 us (8%)
  other arithmetic  135 us (7%)
  between operations  24.3 us (1%)
    ppermute x179, waiting for transfers between devices, flip(): return lax.ppermute(values, axis, [(i, i ^ bit) for i in range(count)])  922 us
    ppermute x179, starting transfers between devices, flip(): return lax.ppermute(values, axis, [(i, i ^ bit) for i in range(count)])  136 us
    dot_general x15, matrix products, times_right(): return jnp.dot(left, right, preferred_element_type=f32).astype(out)  99.7 us
    dot_general x15, matrix products, times_trans(): lax.dot_general(left, right, (((1,), (1,)), ((), ())), preferred_element_...  91.1 us
    pallas_call x25, Pallas kernels, move(): pl.pallas_call(partial(move_kernel, tuple(loads), tuple(stores), len(piec...  90.6 us
    dot_general x14, matrix products, trans_times(): lax.dot_general(left, right, (((0,), (0,)), ((), ())), preferred_element_...  79 us
    unnamed x562, local copies, waits for them, and re-layouts  51.2 us
  transfers between devices with their start and end apart: 195, of which 104 were waited for; matrix products, arithmetic and copies ran while one was open for 25% of the time, Pallas kernels for 7%

profile of v2, /device:TPU:0, one launch (start us, length us, event | category | flops | bytes accessed | tf_op | source)
XLA Modules:
  0.0 1811.3 jit_solution(17582241228957347885)
XLA Ops:
  15.1 20.8 %collective-permute-done.1 = bf16[1,192,128]{2,1,0:T(8,128)(2,1)S(1)} collective-permute-done((bf16[1,192,128]{2,1,0:T(8,128)(2,1)S(1)}, bf16[1,192,128]{2,1,0:T(8,128)(2,1)S(1)}, u32[]{:S(2)}, u32[]{:S(2)}) %collective-permute-start.1) | collective-permute-done | bytes 49184 | tf_op jit(solution)/shard_map/ppermute | solution.py:47
  41.6 10.3 collective-permute-done.2
  71.3 22.7 %collective-permute-done.13.refs_2_ = bf16[512,512]{1,0:T(8,128)(2,1)S(1)} collective-permute-done((bf16[512,512]{1,0:T(8,128)(2,1)S(1)}, bf16[512,512]{1,0:T(8,128)(2,1)S(1)}, u32[]{:S(2)}, u32[]{:S(2)}) %collective-permute-start.13) | collective-permute-done | bytes 524320 | tf_op jit(solution)/shard_map/ppermute | solution.py:47
  97.7 22.6 %collective-permute-done.14.refs_3_ = bf16[512,512]{1,0:T(8,128)(2,1)S(1)} collective-permute-done((bf16[512,512]{1,0:T(8,128)(2,1)S(1)}, bf16[512,512]{1,0:T(8,128)(2,1)S(1)}, u32[]{:S(2)}, u32[]{:S(2)}) %collective-permute-start.14) | collective-permute-done | bytes 524320 | tf_op jit(solution)/shard_map/ppermute | solution.py:47
  133.8 22.9 %collective-permute-done.6.refs_0_ = bf16[128,4096]{1,0:T(8,128)(2,1)} collective-permute-done((bf16[128,4096]{1,0:T(8,128)(2,1)S(1)}, bf16[128,4096]{1,0:T(8,128)(2,1)}, u32[]{:S(2)}, u32[]{:S(2)}) %collective-permute-start.6) | collective-permute-done | bytes 1048608 | tf_op jit(solution)/shard_map/ppermute | solution.py:47
  158.8 26.7 %collective-permute-done.7.refs_1_ = bf16[512,640]{1,0:T(8,128)(2,1)S(1)} collective-permute-done((bf16[512,640]{1,0:T(8,128)(2,1)S(1)}, bf16[512,640]{1,0:T(8,128)(2,1)S(1)}, u32[]{:S(2)}, u32[]{:S(2)}) %collective-permute-start.7) | collective-permute-done | bytes 655392 | tf_op jit(solution)/shard_map/ppermute | solution.py:47
  188.0 27.8 %collective-permute-done.16.refs_3_ = bf16[512,640]{1,0:T(8,128)(2,1)S(1)} collective-permute-done((bf16[512,640]{1,0:T(8,128)(2,1)S(1)}, bf16[512,640]{1,0:T(8,128)(2,1)S(1)}, u32[]{:S(2)}, u32[]{:S(2)}) %collective-permute-start.16) | collective-permute-done | bytes 655392 | tf_op jit(solution)/shard_map/ppermute | solution.py:47
  228.5 15.2 collective-permute-done.8.refs_1_
  246.1 20.8 %collective-permute-done.9.refs_1_ = bf16[256,2048]{1,0:T(8,128)(2,1)S(1)} collective-permute-done((bf16[256,2048]{1,0:T(8,128)(2,1)S(1)}, bf16[256,2048]{1,0:T(8,128)(2,1)S(1)}, u32[]{:S(2)}, u32[]{:S(2)}) %collective-permute-start.9) | collective-permute-done | bytes 1048608 | tf_op jit(solution)/shard_map/ppermute | solution.py:47
  286.1 7.0 shard_map.595
  296.4 32.1 %collective-permute-done.17.refs_1_ = bf16[512,1280]{1,0:T(8,128)(2,1)} collective-permute-done((bf16[512,1280]{1,0:T(8,128)(2,1)}, bf16[512,1280]{1,0:T(8,128)(2,1)}, u32[]{:S(2)}, u32[]{:S(2)}) %collective-permute-start.17) | collective-permute-done | bytes 1310752 | tf_op jit(solution)/shard_map/ppermute | solution.py:47
  336.5 10.4 fusion.257.k_ref
  353.0 8.2 fusion.62.v_ref
  362.9 11.3 convolution_add_fusion.1.q_ref
  374.1 11.5 shard_map.596
  385.6 37.8 %collective-permute-done.18.refs_1_ = bf16[512,2048]{1,0:T(8,128)(2,1)} collective-permute-done((bf16[512,2048]{1,0:T(8,128)(2,1)S(1)}, bf16[512,2048]{1,0:T(8,128)(2,1)}, u32[]{:S(2)}, u32[]{:S(2)}) %collective-permute-start.18) | collective-permute-done | bytes 2097184 | tf_op jit(solution)/shard_map/ppermute | solution.py:47
  439.4 56.9 %collective-permute-done.19.refs_1_ = bf16[512,1280]{1,0:T(8,128)(2,1)} collective-permute-done((bf16[512,1280]{1,0:T(8,128)(2,1)S(1)}, bf16[512,1280]{1,0:T(8,128)(2,1)}, u32[]{:S(2)}, u32[]{:S(2)}) %collective-permute-start.19) | collective-permute-done | bytes 1310752 | tf_op jit(solution)/shard_map/ppermute | solution.py:47
  509.4 32.3 %collective-permute-done.26 = bf16[2,128,1024]{2,1,0:T(8,128)(2,1)S(1)} collective-permute-done((bf16[2,128,1024]{2,1,0:T(8,128)(2,1)S(1)}, bf16[2,128,1024]{2,1,0:T(8,128)(2,1)S(1)}, u32[]{:S(2)}, u32[]{:S(2)}) %collective-permute-start.26) | collective-permute-done | bytes 524320 | tf_op jit(solution)/shard_map/ppermute | solution.py:47
  549.6 22.0 %collective-permute-done.25 = bf16[128,1024]{1,0:T(8,128)(2,1)S(1)} collective-permute-done((bf16[128,1024]{1,0:T(8,128)(2,1)S(1)}, bf16[128,1024]{1,0:T(8,128)(2,1)S(1)}, u32[]{:S(2)}, u32[]{:S(2)}) %collective-permute-start.25) | collective-permute-done | bytes 262176 | tf_op jit(solution)/shard_map/ppermute | solution.py:47
  577.1 10.0 collective-permute-done.31.refs_4_
  596.7 7.6 fusion.59
  616.6 12.7 fusion.258
  636.3 9.8 add_convert_fusion.2
  655.1 11.1 collective-permute-done.41
  690.4 11.3 collective-permute-done.46
  716.0 8.7 collective-permute-done.51.refs_4_
  761.5 7.5 fusion.20
  774.3 10.5 shard_map.602
  822.9 8.3 collective-permute-done.63
  890.8 23.1 %shard_map.604 = (f32[1024,512]{1,0:T(8,128)}, f32[2,4,512,2]{3,2,1,0:T(8,128)}, bf16[2,512,512]{2,1,0:T(8,128)(2,1)}, f32[2,4,512,2]{3,2,1,0:T(8,128)}, f32[2,4,2,512]{3,2,1,0:T(2,128)}) custom-call(bf16[1024,512]{1,0:T(8,128)(2,1)} %bitcast.883, f32[1024,512]{1,0:T(8,128)} %bitcast.862, f32[2,4,512,2]{3,2,1,0:T(8,128)} %bitcast.864, ...), custom_call_target="tpu_custom_call" | custom-call | tf_op jit(solution)/shard_map/pallas_call | solution.py:692
  916.2 9.9 reduce-window.16
  954.1 7.8 convolution_convert_fusion.10
  996.1 23.0 %collective-permute-done.83 = bf16[2,128,1024]{2,1,0:T(8,128)(2,1)S(1)} collective-permute-done((bf16[2,128,1024]{2,1,0:T(8,128)(2,1)S(1)}, bf16[2,128,1024]{2,1,0:T(8,128)(2,1)S(1)}, u32[]{:S(2)}, u32[]{:S(2)}) %collective-permute-start.83) | collective-permute-done | bytes 524320 | tf_op jit(solution)/shard_map/ppermute | solution.py:47
  1039.8 9.7 collective-permute-done.102.refs_4_
  1051.8 6.7 collective-permute-done.100.refs_2_
  1079.1 12.1 collective-permute-done.109.refs_2_
  1093.6 10.8 collective-permute-done.113.refs_6_
  1110.9 12.2 fusion.10
  1124.4 11.8 convolution_convert_fusion
  1136.3 9.4 convolution_convert_fusion.9
  1145.8 12.2 convolution_convert_fusion.5
  1178.0 10.9 collective-permute-done.118
  1202.7 9.1 collective-permute-done.128.refs_4_
  1243.9 13.5 shard_map.609
  1257.4 10.4 convolution_convert_fusion.1
  1282.2 10.2 convolution_convert_fusion.2
  1301.3 9.7 convolution_convert_fusion.3
  1311.0 10.6 fusion.259
  1321.6 8.3 fusion.260
  1329.9 17.6 add_convert_fusion
  1351.4 45.3 %collective-permute-done.151 = bf16[2,128,64]{2,1,0:T(8,128)(2,1)S(1)} collective-permute-done((bf16[2,128,64]{2,1,0:T(8,128)(2,1)S(1)}, bf16[2,128,64]{2,1,0:T(8,128)(2,1)S(1)}, u32[]{:S(2)}, u32[]{:S(2)}) %collective-permute-start.151) | collective-permute-done | bytes 32800 | tf_op jit(solution)/shard_map/ppermute | solution.py:47
  1436.2 17.0 collective-permute-done.169
  1455.0 19.0 %collective-permute-done.146 = bf16[2,128,2048]{2,1,0:T(8,128)(2,1)S(1)} collective-permute-done((bf16[2,128,2048]{2,1,0:T(8,128)(2,1)S(1)}, bf16[2,128,2048]{2,1,0:T(8,128)(2,1)S(1)}, u32[]{:S(2)}, u32[]{:S(2)}) %collective-permute-start.146) | collective-permute-done | bytes 1048608 | tf_op jit(solution)/shard_map/ppermute | solution.py:47
  1508.0 13.8 concatenate.409
  1534.1 33.7 %collective-permute-done.164 = bf16[2,256,1280]{2,1,0:T(8,128)(2,1)} collective-permute-done((bf16[2,256,1280]{2,1,0:T(8,128)(2,1)}, bf16[2,256,1280]{2,1,0:T(8,128)(2,1)}, u32[]{:S(2)}, u32[]{:S(2)}) %collective-permute-start.164) | collective-permute-done | bytes 1310752 | tf_op jit(solution)/shard_map/ppermute | solution.py:47
  1575.7 17.1 collective-permute-done.165
  1611.2 6.7 fusion.234
  1618.0 15.6 collective-permute-done.171
  1639.5 36.1 %collective-permute-done.158 = bf16[2,2,784,128]{3,2,1,0:T(8,128)(2,1)} collective-permute-done((bf16[2,2,784,128]{3,2,1,0:T(8,128)(2,1)}, bf16[2,2,784,128]{3,2,1,0:T(8,128)(2,1)}, u32[]{:S(2)}, u32[]{:S(2)}) %collective-permute-start.158) | collective-permute-done | bytes 802848 | tf_op jit(solution)/shard_map/ppermute | solution.py:47
  1679.7 8.5 collective-permute-done.159
  1699.8 23.7 %collective-permute-done.173 = bf16[512,512]{1,0:T(8,128)(2,1)S(1)} collective-permute-done((bf16[512,512]{1,0:T(8,128)(2,1)S(1)}, bf16[512,512]{1,0:T(8,128)(2,1)S(1)}, u32[]{:S(2)}, u32[]{:S(2)}) %collective-permute-start.173) | collective-permute-done | bytes 524320 | tf_op jit(solution)/shard_map/ppermute | solution.py:47
  1730.1 7.2 collective-permute-done.167
  1748.0 37.2 %collective-permute-done.168 = bf16[2,512,512]{2,1,0:T(8,128)(2,1)} collective-permute-done((bf16[2,512,512]{2,1,0:T(8,128)(2,1)}, bf16[2,512,512]{2,1,0:T(8,128)(2,1)}, u32[]{:S(2)}, u32[]{:S(2)}) %collective-permute-start.168) | collective-permute-done | bytes 1048608 | tf_op jit(solution)/shard_map/ppermute | solution.py:47
  1790.5 10.1 collective-permute-done.175
  (1423 shorter events, 730.0 us)
Async XLA Ops:
  7.3 329.2 %all-gather.14.cloned.1.call-start = ((), (), s32[]{:S(2)}) async-start(), calls=%async_computation.12 | async-start | bytes 6291456 | tf_op jit(solution)/shard_map/all_gather | solution.py:198
  8.7 31.7 %collective-permute-start = (bf16[512,512]{1,0:T(8,128)(2,1)S(1)}, bf16[512,512]{1,0:T(8,128)(2,1)}, u32[]{:S(2)}, u32[]{:S(2)}) collective-permute-start(bf16[512,512]{1,0:T(8,128)(2,1)S(1)} %get-tuple-element.429), channel_id=1, source_target_pairs={{0,8},{4,12},{8,0},{12,4},{16,24},{20,28},{24,16},{28,20},{1,9},{5... | collective-permute-start | bytes 1572872 | tf_op jit(solution)/shard_map/ppermute | solution.py:47
  11.8 28.6 %collective-permute-start.11 = (bf16[512,512]{1,0:T(8,128)(2,1)S(1)}, bf16[512,512]{1,0:T(8,128)(2,1)S(1)}, u32[]{:S(2)}, u32[]{:S(2)}) collective-permute-start(bf16[512,512]{1,0:T(8,128)(2,1)S(1)} %get-tuple-element.428.refs_0_), channel_id=1, source_target_pairs={{0,16},{4,20},{8,24},{12,28},{16,0},{20,4},{24,8},{28,12},{1,17},{... | collective-permute-start | bytes 1572872 | tf_op jit(solution)/shard_map/ppermute | solution.py:47
  94.8 25.6 %collective-permute-start.14 = (bf16[512,512]{1,0:T(8,128)(2,1)S(1)}, bf16[512,512]{1,0:T(8,128)(2,1)S(1)}, u32[]{:S(2)}, u32[]{:S(2)}) collective-permute-start(bf16[512,512]{1,0:T(8,128)(2,1)S(1)} %collective-permute-done.5.refs_1_), channel_id=1, source_target_pairs={{0,16},{4,20},{8,24},{12,28},{16,0},{20,4},{24,8},{28,12},{1,17},{... | collective-permute-start | bytes 1572872 | tf_op jit(solution)/shard_map/ppermute | solution.py:47
  124.2 222.6 %all-gather.12.cloned.1.call-start = ((), (), s32[]{:S(2)}) async-start(), calls=%async_computation.11 | async-start | bytes 7864320 | tf_op jit(solution)/shard_map/all_gather | solution.py:198
  156.7 28.8 %collective-permute-start.7 = (bf16[512,640]{1,0:T(8,128)(2,1)S(1)}, bf16[512,640]{1,0:T(8,128)(2,1)S(1)}, u32[]{:S(2)}, u32[]{:S(2)}) collective-permute-start(bf16[512,640]{1,0:T(8,128)(2,1)S(1)} %get-tuple-element.101), channel_id=1, source_target_pairs={{0,8},{4,12},{8,0},{12,4},{16,24},{20,28},{24,16},{28,20},{1,9},{5... | collective-permute-start | bytes 1966088 | tf_op jit(solution)/shard_map/ppermute | solution.py:47
  157.0 30.7 %collective-permute-start.15 = (bf16[512,640]{1,0:T(8,128)(2,1)S(1)}, bf16[512,640]{1,0:T(8,128)(2,1)S(1)}, u32[]{:S(2)}, u32[]{:S(2)}) collective-permute-start(bf16[512,640]{1,0:T(8,128)(2,1)S(1)} %get-tuple-element.109.refs_0_), channel_id=1, source_target_pairs={{0,16},{4,20},{8,24},{12,28},{16,0},{20,4},{24,8},{28,12},{1,17},{... | collective-permute-start | bytes 1966088 | tf_op jit(solution)/shard_map/ppermute | solution.py:47
  187.7 28.2 %collective-permute-start.16 = (bf16[512,640]{1,0:T(8,128)(2,1)S(1)}, bf16[512,640]{1,0:T(8,128)(2,1)S(1)}, u32[]{:S(2)}, u32[]{:S(2)}) collective-permute-start(bf16[512,640]{1,0:T(8,128)(2,1)S(1)} %collective-permute-done.7.refs_1_), channel_id=1, source_target_pairs={{0,16},{4,20},{8,24},{12,28},{16,0},{20,4},{24,8},{28,12},{1,17},{... | collective-permute-start | bytes 1966088 | tf_op jit(solution)/shard_map/ppermute | solution.py:47
  220.1 142.7 %all-gather.10.cloned.1.call-start = ((), (), s32[]{:S(2)}) async-start(), calls=%async_computation.10 | async-start | bytes 6291456 | tf_op jit(solution)/shard_map/all_gather | solution.py:198
  222.9 205.0 %all-gather.16.cloned.1.call-start = ((), (), s32[]{:S(2)}) async-start(), calls=%async_computation.13 | async-start | bytes 7864320 | tf_op jit(solution)/shard_map/all_gather | solution.py:198
  244.1 30.8 %collective-permute-start.21 = (bf16[128,4096]{1,0:T(8,128)(2,1)}, bf16[128,4096]{1,0:T(8,128)(2,1)}, u32[]{:S(2)}, u32[]{:S(2)}) collective-permute-start(bf16[128,4096]{1,0:T(8,128)(2,1)} %collective-permute-done.6.refs_0_), channel_id=1, source_target_pairs={{0,2},{1,3},{2,0},{3,1},{4,6},{5,7},{6,4},{7,5},{8,10},{9,11},{10,... | collective-permute-start | bytes 3145736 | tf_op jit(solution)/shard_map/ppermute | solution.py:47
  267.0 65.6 %collective-permute-start.10 = (bf16[256,2816]{1,0:T(8,128)(2,1)}, bf16[256,2816]{1,0:T(8,128)(2,1)}, u32[]{:S(2)}, u32[]{:S(2)}) collective-permute-start(bf16[256,2816]{1,0:T(8,128)(2,1)} %get-tuple-element.104), channel_id=1, source_target_pairs={{0,8},{4,12},{8,0},{12,4},{16,24},{20,28},{24,16},{28,20},{1,9},{5... | collective-permute-start | bytes 4325384 | tf_op jit(solution)/shard_map/ppermute | solution.py:47
  271.1 57.4 %collective-permute-start.17 = (bf16[512,1280]{1,0:T(8,128)(2,1)}, bf16[512,1280]{1,0:T(8,128)(2,1)}, u32[]{:S(2)}, u32[]{:S(2)}) collective-permute-start(bf16[512,1280]{1,0:T(8,128)(2,1)} %shard_map.589.refs_0_), channel_id=1, source_target_pairs={{0,16},{4,20},{8,24},{12,28},{16,0},{20,4},{24,8},{28,12},{1,17},{... | collective-permute-start | bytes 3932168 | tf_op jit(solution)/shard_map/ppermute | solution.py:47
  332.0 284.6 %all-gather.18.cloned.1.call-start = ((), (), s32[]{:S(2)}) async-start(), calls=%async_computation.14 | async-start | bytes 12582912 | tf_op jit(solution)/shard_map/all_gather | solution.py:198
  336.4 87.0 %collective-permute-start.18 = (bf16[512,2048]{1,0:T(8,128)(2,1)S(1)}, bf16[512,2048]{1,0:T(8,128)(2,1)}, u32[]{:S(2)}, u32[]{:S(2)}) collective-permute-start(bf16[512,2048]{1,0:T(8,128)(2,1)S(1)} %copy-done.20), channel_id=1, source_target_pairs={{0,16},{4,20},{8,24},{12,28},{16,0},{20,4},{24,8},{28,12},{1,17},{... | collective-permute-start | bytes 6291464 | tf_op jit(solution)/shard_map/ppermute | solution.py:47
  427.7 208.6 %all-gather.8.cloned.1.call-start = ((), (), s32[]{:S(2)}) async-start(), calls=%async_computation.9 | async-start | bytes 7864320 | tf_op jit(solution)/shard_map/all_gather | solution.py:198
  436.0 65.9 %collective-permute-start.23 = (bf16[2,2,128,2048]{3,2,1,0:T(8,128)(2,1)}, bf16[2,2,128,2048]{3,2,1,0:T(8,128)(2,1)S(1)}, u32[]{:S(2)}, u32[]{:S(2)}) collective-permute-start(bf16[2,2,128,2048]{3,2,1,0:T(8,128)(2,1)} %dynamic-slice_bitcast_fusion.7), channel_id=1, source_target_pairs={{0,1},{1,0},{2,3},{3,2},{4,5},{5,4},{6,7},{7,6},{8,9},{9,8},{10,11... | collective-permute-start | bytes 6291464 | tf_op jit(solution)/shard_map/ppermute | solution.py:47
  436.0 60.3 %collective-permute-start.19 = (bf16[512,1280]{1,0:T(8,128)(2,1)S(1)}, bf16[512,1280]{1,0:T(8,128)(2,1)}, u32[]{:S(2)}, u32[]{:S(2)}) collective-permute-start(bf16[512,1280]{1,0:T(8,128)(2,1)S(1)} %copy-done.62), channel_id=1, source_target_pairs={{0,16},{4,20},{8,24},{12,28},{16,0},{20,4},{24,8},{28,12},{1,17},{... | collective-permute-start | bytes 3932168 | tf_op jit(solution)/shard_map/ppermute | solution.py:47
  496.3 112.9 %collective-permute-start.37 = (bf16[512,1536]{1,0:T(8,128)(2,1)}, bf16[512,1536]{1,0:T(8,128)(2,1)}, u32[]{:S(2)}, u32[]{:S(2)}) collective-permute-start(bf16[512,1536]{1,0:T(8,128)(2,1)} %get-tuple-element.120.refs_0_), channel_id=1, source_target_pairs={{0,16},{4,20},{8,24},{12,28},{16,0},{20,4},{24,8},{28,12},{1,17},{... | collective-permute-start | bytes 4718600 | tf_op jit(solution)/shard_map/ppermute | solution.py:47
  499.8 261.6 %all-gather.20.cloned.1.call-start = ((), (), s32[]{:S(2)}) async-start(), calls=%async_computation.15 | async-start | bytes 9437184 | tf_op jit(solution)/shard_map/all_gather | solution.py:198
  504.5 37.3 %collective-permute-start.26 = (bf16[2,128,1024]{2,1,0:T(8,128)(2,1)S(1)}, bf16[2,128,1024]{2,1,0:T(8,128)(2,1)S(1)}, u32[]{:S(2)}, u32[]{:S(2)}) collective-permute-start(bf16[2,128,1024]{2,1,0:T(8,128)(2,1)S(1)} %dynamic-slice_bitcast_fusion.42), channel_id=1, source_target_pairs={{0,8},{4,12},{8,0},{12,4},{16,24},{20,28},{24,16},{28,20},{1,9},{5... | collective-permute-start | bytes 1572872 | tf_op jit(solution)/shard_map/ppermute | solution.py:47
  507.2 36.0 %collective-permute-start.24 = (bf16[2,128,1024]{2,1,0:T(8,128)(2,1)S(1)}, bf16[2,128,1024]{2,1,0:T(8,128)(2,1)S(1)}, u32[]{:S(2)}, u32[]{:S(2)}) collective-permute-start(bf16[2,128,1024]{2,1,0:T(8,128)(2,1)S(1)} %dynamic-slice_bitcast_fusion.43), channel_id=1, source_target_pairs={{0,2},{1,3},{2,0},{3,1},{4,6},{5,7},{6,4},{7,5},{8,10},{9,11},{10,... | collective-permute-start | bytes 1572872 | tf_op jit(solution)/shard_map/ppermute | solution.py:47
  543.5 28.2 %collective-permute-start.25 = (bf16[128,1024]{1,0:T(8,128)(2,1)S(1)}, bf16[128,1024]{1,0:T(8,128)(2,1)S(1)}, u32[]{:S(2)}, u32[]{:S(2)}) collective-permute-start(bf16[128,1024]{1,0:T(8,128)(2,1)S(1)} %dynamic-slice_bitcast_fusion.61), channel_id=1, source_target_pairs={{0,8},{4,12},{8,0},{12,4},{16,24},{20,28},{24,16},{28,20},{1,9},{5... | collective-permute-start | bytes 786440 | tf_op jit(solution)/shard_map/ppermute | solution.py:47
  681.1 269.3 %reduce-scatter.10.cloned.1.call-start = ((), (), s32[]{:S(2)}) async-start(), calls=%async_computation.16 | async-start | bytes 2621440 | tf_op jit(solution)/shard_map/reduce_scatter | solution.py:268
  879.2 231.7 %reduce-scatter.12.cloned.1.call-start = ((), (), s32[]{:S(2)}) async-start(), calls=%async_computation.17 | async-start | bytes 5242880 | tf_op jit(solution)/shard_map/reduce_scatter | solution.py:268
  934.3 27.7 %collective-permute-start.85 = (bf16[2,2,128,256]{3,2,1,0:T(8,128)(2,1)}, bf16[2,2,128,256]{3,2,1,0:T(8,128)(2,1)}, u32[]{:S(2)}, u32[]{:S(2)}) collective-permute-start(bf16[2,2,128,256]{3,2,1,0:T(8,128)(2,1)} %fusion.132), channel_id=1, source_target_pairs={{0,1},{1,0},{2,3},{3,2},{4,5},{5,4},{6,7},{7,6},{8,9},{9,8},{10,11... | collective-permute-start | bytes 786440 | tf_op jit(solution)/shard_map/ppermute | solution.py:47
  953.7 34.0 %collective-permute-start.80 = (bf16[2,2,128,2048]{3,2,1,0:T(8,128)(2,1)}, bf16[2,2,128,2048]{3,2,1,0:T(8,128)(2,1)S(1)}, u32[]{:S(2)}, u32[]{:S(2)}) collective-permute-start(bf16[2,2,128,2048]{3,2,1,0:T(8,128)(2,1)} %dynamic-slice_bitcast_fusion.3), channel_id=1, source_target_pairs={{0,1},{1,0},{2,3},{3,2},{4,5},{5,4},{6,7},{7,6},{8,9},{9,8},{10,11... | collective-permute-start | bytes 6291464 | tf_op jit(solution)/shard_map/ppermute | solution.py:47
  961.9 278.8 %reduce-scatter.14.cloned.1.call-start = ((), (), s32[]{:S(2)}) async-start(), calls=%async_computation.18 | async-start | bytes 12582912 | tf_op jit(solution)/shard_map/reduce_scatter | solution.py:263
  990.4 28.8 %collective-permute-start.83 = (bf16[2,128,1024]{2,1,0:T(8,128)(2,1)S(1)}, bf16[2,128,1024]{2,1,0:T(8,128)(2,1)S(1)}, u32[]{:S(2)}, u32[]{:S(2)}) collective-permute-start(bf16[2,128,1024]{2,1,0:T(8,128)(2,1)S(1)} %dynamic-slice_bitcast_fusion.34), channel_id=1, source_target_pairs={{0,8},{4,12},{8,0},{12,4},{16,24},{20,28},{24,16},{28,20},{1,9},{5... | collective-permute-start | bytes 1572872 | tf_op jit(solution)/shard_map/ppermute | solution.py:47
  994.9 25.6 %collective-permute-start.81 = (bf16[2,128,1024]{2,1,0:T(8,128)(2,1)S(1)}, bf16[2,128,1024]{2,1,0:T(8,128)(2,1)S(1)}, u32[]{:S(2)}, u32[]{:S(2)}) collective-permute-start(bf16[2,128,1024]{2,1,0:T(8,128)(2,1)S(1)} %dynamic-slice_bitcast_fusion.35), channel_id=1, source_target_pairs={{0,2},{1,3},{2,0},{3,1},{4,6},{5,7},{6,4},{7,5},{8,10},{9,11},{10,... | collective-permute-start | bytes 1572872 | tf_op jit(solution)/shard_map/ppermute | solution.py:47
  1039.8 26.5 %collective-permute-start.99 = (bf16[128,2048]{1,0:T(8,128)(2,1)S(1)}, bf16[128,2048]{1,0:T(8,128)(2,1)S(1)}, u32[]{:S(2)}, u32[]{:S(2)}) collective-permute-start(bf16[128,2048]{1,0:T(8,128)(2,1)S(1)} %get-tuple-element.363.refs_0_), channel_id=1, source_target_pairs={{0,1},{1,0},{2,3},{3,2},{4,5},{5,4},{6,7},{7,6},{8,9},{9,8},{10,11... | collective-permute-start | bytes 1572872 | tf_op jit(solution)/shard_map/ppermute | solution.py:47
  1136.2 367.8 %reduce-scatter.26.cloned.1.call-start = ((), (), s32[]{:S(2)}) async-start(), calls=%async_computation.24 | async-start | bytes 6291456 | tf_op jit(solution)/shard_map/reduce_scatter | solution.py:263
  1145.7 358.3 %reduce-scatter.24.cloned.1.call-start = ((), (), s32[]{:S(2)}) async-start(), calls=%async_computation.23 | async-start | bytes 1572864 | tf_op jit(solution)/shard_map/reduce_scatter | solution.py:263
  1165.2 357.8 %reduce-scatter.22.cloned.1.call-start = ((), (), s32[]{:S(2)}) async-start(), calls=%async_computation.22 | async-start | bytes 3145728 | tf_op jit(solution)/shard_map/reduce_scatter | solution.py:263
  1234.3 293.8 %reduce-scatter.20.cloned.1.call-start = ((), (), s32[]{:S(2)}) async-start(), calls=%async_computation.21 | async-start | bytes 6291456 | tf_op jit(solution)/shard_map/reduce_scatter | solution.py:263
  1267.9 260.2 %reduce-scatter.18.cloned.1.call-start = ((), (), s32[]{:S(2)}) async-start(), calls=%async_computation.20 | async-start | bytes 6291456 | tf_op jit(solution)/shard_map/reduce_scatter | solution.py:263
  1292.4 237.9 %reduce-scatter.16.cloned.1.call-start = ((), (), s32[]{:S(2)}) async-start(), calls=%async_computation.19 | async-start | bytes 6291456 | tf_op jit(solution)/shard_map/reduce_scatter | solution.py:263
  1301.1 46.4 %collective-permute-start.148 = (bf16[2,2,128,128]{3,2,1,0:T(8,128)(2,1)}, bf16[2,2,128,128]{3,2,1,0:T(8,128)(2,1)}, u32[]{:S(2)}, u32[]{:S(2)}) collective-permute-start(bf16[2,2,128,128]{3,2,1,0:T(8,128)(2,1)} %dynamic-slice_bitcast_fusion.65), channel_id=1, source_target_pairs={{0,1},{1,0},{2,3},{3,2},{4,5},{5,4},{6,7},{7,6},{8,9},{9,8},{10,11... | collective-permute-start | bytes 393224 | tf_op jit(solution)/shard_map/ppermute | solution.py:47
  1301.3 102.4 %collective-permute-start.134 = (bf16[2,256,2048]{2,1,0:T(8,128)(2,1)}, bf16[2,256,2048]{2,1,0:T(8,128)(2,1)S(1)}, u32[]{:S(2)}, u32[]{:S(2)}) collective-permute-start(bf16[2,256,2048]{2,1,0:T(8,128)(2,1)} %dynamic-slice_bitcast_fusion.1), channel_id=1, source_target_pairs={{0,16},{4,20},{8,24},{12,28},{16,0},{20,4},{24,8},{28,12},{1,17},{... | collective-permute-start | bytes 6291464 | tf_op jit(solution)/shard_map/ppermute | solution.py:47
  1348.7 48.0 %collective-permute-start.151 = (bf16[2,128,64]{2,1,0:T(8,128)(2,1)S(1)}, bf16[2,128,64]{2,1,0:T(8,128)(2,1)S(1)}, u32[]{:S(2)}, u32[]{:S(2)}) collective-permute-start(bf16[2,128,64]{2,1,0:T(8,128)(2,1)S(1)} %dynamic-slice_bitcast_fusion.67), channel_id=1, source_target_pairs={{0,8},{4,12},{8,0},{12,4},{16,24},{20,28},{24,16},{28,20},{1,9},{5... | collective-permute-start | bytes 98312 | tf_op jit(solution)/shard_map/ppermute | solution.py:47
  1350.2 47.7 %collective-permute-start.149 = (bf16[2,128,64]{2,1,0:T(8,128)(2,1)S(1)}, bf16[2,128,64]{2,1,0:T(8,128)(2,1)S(1)}, u32[]{:S(2)}, u32[]{:S(2)}) collective-permute-start(bf16[2,128,64]{2,1,0:T(8,128)(2,1)S(1)} %dynamic-slice_bitcast_fusion.68), channel_id=1, source_target_pairs={{0,2},{1,3},{2,0},{3,1},{4,6},{5,7},{6,4},{7,5},{8,10},{9,11},{10,... | collective-permute-start | bytes 98312 | tf_op jit(solution)/shard_map/ppermute | solution.py:47
  1408.5 26.5 %collective-permute-start.136 = (bf16[128,2048]{1,0:T(8,128)(2,1)S(1)}, bf16[128,2048]{1,0:T(8,128)(2,1)}, u32[]{:S(2)}, u32[]{:S(2)}) collective-permute-start(bf16[128,2048]{1,0:T(8,128)(2,1)S(1)} %copy-done.57), channel_id=1, source_target_pairs={{0,2},{1,3},{2,0},{3,1},{4,6},{5,7},{6,4},{7,5},{8,10},{9,11},{10,... | collective-permute-start | bytes 1572872 | tf_op jit(solution)/shard_map/ppermute | solution.py:47
  1409.4 70.2 %collective-permute-start.135 = (bf16[128,2048]{1,0:T(8,128)(2,1)S(1)}, bf16[128,2048]{1,0:T(8,128)(2,1)}, u32[]{:S(2)}, u32[]{:S(2)}) collective-permute-start(bf16[128,2048]{1,0:T(8,128)(2,1)S(1)} %copy-done.57), channel_id=1, source_target_pairs={{0,1},{1,0},{2,3},{3,2},{4,5},{5,4},{6,7},{7,6},{8,9},{9,8},{10,11... | collective-permute-start | bytes 1572872 | tf_op jit(solution)/shard_map/ppermute | solution.py:47
  1427.1 26.1 %collective-permute-start.169 = (bf16[256,2048]{1,0:T(8,128)(2,1)S(1)}, bf16[256,2048]{1,0:T(8,128)(2,1)S(1)}, u32[]{:S(2)}, u32[]{:S(2)}) collective-permute-start(bf16[256,2048]{1,0:T(8,128)(2,1)S(1)} %get-tuple-element.155), channel_id=1, source_target_pairs={{0,8},{4,12},{8,0},{12,4},{16,24},{20,28},{24,16},{28,20},{1,9},{5... | collective-permute-start | bytes 3145736 | tf_op jit(solution)/shard_map/ppermute | solution.py:47
  1432.0 42.0 %collective-permute-start.146 = (bf16[2,128,2048]{2,1,0:T(8,128)(2,1)S(1)}, bf16[2,128,2048]{2,1,0:T(8,128)(2,1)S(1)}, u32[]{:S(2)}, u32[]{:S(2)}) collective-permute-start(bf16[2,128,2048]{2,1,0:T(8,128)(2,1)S(1)} %dynamic-slice_bitcast_fusion.15), channel_id=1, source_target_pairs={{0,8},{4,12},{8,0},{12,4},{16,24},{20,28},{24,16},{28,20},{1,9},{5... | collective-permute-start | bytes 3145736 | tf_op jit(solution)/shard_map/ppermute | solution.py:47
  1435.1 44.5 %collective-permute-start.137 = (bf16[128,2048]{1,0:T(8,128)(2,1)}, bf16[128,2048]{1,0:T(8,128)(2,1)S(1)}, u32[]{:S(2)}, u32[]{:S(2)}) collective-permute-start(bf16[128,2048]{1,0:T(8,128)(2,1)} %collective-permute-done.136.refs_2_), channel_id=1, source_target_pairs={{0,1},{1,0},{2,3},{3,2},{4,5},{5,4},{6,7},{7,6},{8,9},{9,8},{10,11... | collective-permute-start | bytes 1572872 | tf_op jit(solution)/shard_map/ppermute | solution.py:47
  1435.3 41.1 %collective-permute-start.144 = (bf16[2,128,2048]{2,1,0:T(8,128)(2,1)S(1)}, bf16[2,128,2048]{2,1,0:T(8,128)(2,1)S(1)}, u32[]{:S(2)}, u32[]{:S(2)}) collective-permute-start(bf16[2,128,2048]{2,1,0:T(8,128)(2,1)S(1)} %dynamic-slice_bitcast_fusion.16), channel_id=1, source_target_pairs={{0,2},{1,3},{2,0},{3,1},{4,6},{5,7},{6,4},{7,5},{8,10},{9,11},{10,... | collective-permute-start | bytes 3145736 | tf_op jit(solution)/shard_map/ppermute | solution.py:47
  1503.1 30.8 %collective-permute-start.154 = (bf16[128,4096]{1,0:T(8,128)(2,1)}, bf16[128,4096]{1,0:T(8,128)(2,1)}, u32[]{:S(2)}, u32[]{:S(2)}) collective-permute-start(bf16[128,4096]{1,0:T(8,128)(2,1)} %pad_maximum_fusion.8.refs_0_), channel_id=1, source_target_pairs={{0,2},{1,3},{2,0},{3,1},{4,6},{5,7},{6,4},{7,5},{8,10},{9,11},{10,... | collective-permute-start | bytes 3145736 | tf_op jit(solution)/shard_map/ppermute | solution.py:47
  1504.0 103.2 %collective-permute-start.153 = (bf16[128,4096]{1,0:T(8,128)(2,1)}, bf16[128,4096]{1,0:T(8,128)(2,1)}, u32[]{:S(2)}, u32[]{:S(2)}) collective-permute-start(bf16[128,4096]{1,0:T(8,128)(2,1)} %pad_maximum_fusion.8.refs_0_), channel_id=1, source_target_pairs={{0,1},{1,0},{2,3},{3,2},{4,5},{5,4},{6,7},{7,6},{8,9},{9,8},{10,11... | collective-permute-start | bytes 3145736 | tf_op jit(solution)/shard_map/ppermute | solution.py:47
  1507.5 60.2 %collective-permute-start.164 = (bf16[2,256,1280]{2,1,0:T(8,128)(2,1)}, bf16[2,256,1280]{2,1,0:T(8,128)(2,1)}, u32[]{:S(2)}, u32[]{:S(2)}) collective-permute-start(bf16[2,256,1280]{2,1,0:T(8,128)(2,1)} %pad_maximum_fusion.5), channel_id=1, source_target_pairs={{0,16},{4,20},{8,24},{12,28},{16,0},{20,4},{24,8},{28,12},{1,17},{... | collective-permute-start | bytes 3932168 | tf_op jit(solution)/shard_map/ppermute | solution.py:47
  1523.0 49.8 %collective-permute-start.156 = (bf16[2,8,336,128]{3,2,0,1:T(8,128)(2,1)}, bf16[2,8,336,128]{3,2,0,1:T(8,128)(2,1)}, u32[]{:S(2)}, u32[]{:S(2)}) collective-permute-start(bf16[2,8,336,128]{3,2,0,1:T(8,128)(2,1)} %dynamic-slice_bitcast_fusion.8), channel_id=1, source_target_pairs={{0,1},{1,0},{2,3},{3,2},{4,5},{5,4},{6,7},{7,6},{8,9},{9,8},{10,11... | collective-permute-start | bytes 4128776 | tf_op jit(solution)/shard_map/ppermute | solution.py:47
  1533.8 73.4 %collective-permute-start.155 = (bf16[128,4096]{1,0:T(8,128)(2,1)}, bf16[128,4096]{1,0:T(8,128)(2,1)}, u32[]{:S(2)}, u32[]{:S(2)}) collective-permute-start(bf16[128,4096]{1,0:T(8,128)(2,1)} %collective-permute-done.154.refs_2_), channel_id=1, source_target_pairs={{0,1},{1,0},{2,3},{3,2},{4,5},{5,4},{6,7},{7,6},{8,9},{9,8},{10,11... | collective-permute-start | bytes 3145736 | tf_op jit(solution)/shard_map/ppermute | solution.py:47
  1570.6 28.1 %collective-permute-start.170 = (bf16[256,1280]{1,0:T(8,128)(2,1)S(1)}, bf16[256,1280]{1,0:T(8,128)(2,1)S(1)}, u32[]{:S(2)}, u32[]{:S(2)}) collective-permute-start(bf16[256,1280]{1,0:T(8,128)(2,1)S(1)} %pad_maximum_fusion.12), channel_id=1, source_target_pairs={{0,8},{4,12},{8,0},{12,4},{16,24},{20,28},{24,16},{28,20},{1,9},{5... | collective-permute-start | bytes 1966088 | tf_op jit(solution)/shard_map/ppermute | solution.py:47
  1574.6 26.8 %collective-permute-start.157 = (bf16[8,336,128]{2,1,0:T(8,128)(2,1)S(1)}, bf16[8,336,128]{2,1,0:T(8,128)(2,1)S(1)}, u32[]{:S(2)}, u32[]{:S(2)}) collective-permute-start(bf16[8,336,128]{2,1,0:T(8,128)(2,1)S(1)} %dynamic-slice_bitcast_fusion.18), channel_id=1, source_target_pairs={{0,2},{1,3},{2,0},{3,1},{4,6},{5,7},{6,4},{7,5},{8,10},{9,11},{10,... | collective-permute-start | bytes 2064392 | tf_op jit(solution)/shard_map/ppermute | solution.py:47
  1592.8 85.3 %collective-permute-start.166 = (bf16[2,512,512]{2,1,0:T(8,128)(2,1)}, bf16[2,512,512]{2,1,0:T(8,128)(2,1)}, u32[]{:S(2)}, u32[]{:S(2)}) collective-permute-start(bf16[2,512,512]{2,1,0:T(8,128)(2,1)} %dynamic-slice_bitcast_fusion.12), channel_id=1, source_target_pairs={{0,16},{4,20},{8,24},{12,28},{16,0},{20,4},{24,8},{28,12},{1,17},{... | collective-permute-start | bytes 3145736 | tf_op jit(solution)/shard_map/ppermute | solution.py:47
  1598.7 34.8 %collective-permute-start.171 = (bf16[256,1536]{1,0:T(8,128)(2,1)}, bf16[256,1536]{1,0:T(8,128)(2,1)}, u32[]{:S(2)}, u32[]{:S(2)}) collective-permute-start(bf16[256,1536]{1,0:T(8,128)(2,1)} %pad_maximum_fusion.11), channel_id=1, source_target_pairs={{0,8},{4,12},{8,0},{12,4},{16,24},{20,28},{24,16},{28,20},{1,9},{5... | collective-permute-start | bytes 2359304 | tf_op jit(solution)/shard_map/ppermute | solution.py:47
  1604.4 71.1 %collective-permute-start.158 = (bf16[2,2,784,128]{3,2,1,0:T(8,128)(2,1)}, bf16[2,2,784,128]{3,2,1,0:T(8,128)(2,1)}, u32[]{:S(2)}, u32[]{:S(2)}) collective-permute-start(bf16[2,2,784,128]{3,2,1,0:T(8,128)(2,1)} %dynamic-slice_bitcast_fusion.17), channel_id=1, source_target_pairs={{0,16},{4,20},{8,24},{12,28},{16,0},{20,4},{24,8},{28,12},{1,17},{... | collective-permute-start | bytes 2408456 | tf_op jit(solution)/shard_map/ppermute | solution.py:47
  1633.6 56.7 %collective-permute-start.172 = (bf16[256,512]{1,0:T(8,128)(2,1)S(1)}, bf16[256,512]{1,0:T(8,128)(2,1)S(1)}, u32[]{:S(2)}, u32[]{:S(2)}) collective-permute-start(bf16[256,512]{1,0:T(8,128)(2,1)S(1)} %copy-done.135), channel_id=1, source_target_pairs={{0,8},{4,12},{8,0},{12,4},{16,24},{20,28},{24,16},{28,20},{1,9},{5... | collective-permute-start | bytes 786440 | tf_op jit(solution)/shard_map/ppermute | solution.py:47
  1689.6 47.7 %collective-permute-start.167 = (bf16[2,512,512]{2,1,0:T(8,128)(2,1)}, bf16[2,512,512]{2,1,0:T(8,128)(2,1)}, u32[]{:S(2)}, u32[]{:S(2)}) collective-permute-start(bf16[2,512,512]{2,1,0:T(8,128)(2,1)} %dynamic-slice_bitcast_fusion.13), channel_id=1, source_target_pairs={{0,16},{4,20},{8,24},{12,28},{16,0},{20,4},{24,8},{28,12},{1,17},{... | collective-permute-start | bytes 3145736 | tf_op jit(solution)/shard_map/ppermute | solution.py:47
  1690.3 33.3 %collective-permute-start.173 = (bf16[512,512]{1,0:T(8,128)(2,1)S(1)}, bf16[512,512]{1,0:T(8,128)(2,1)S(1)}, u32[]{:S(2)}, u32[]{:S(2)}) collective-permute-start(bf16[512,512]{1,0:T(8,128)(2,1)S(1)} %get-tuple-element.159), channel_id=1, source_target_pairs={{0,8},{4,12},{8,0},{12,4},{16,24},{20,28},{24,16},{28,20},{1,9},{5... | collective-permute-start | bytes 1572872 | tf_op jit(solution)/shard_map/ppermute | solution.py:47
  1696.5 28.7 %collective-permute-start.161 = (bf16[336,128]{1,0:T(8,128)(2,1)S(1)}, bf16[336,128]{1,0:T(8,128)(2,1)S(1)}, u32[]{:S(2)}, u32[]{:S(2)}) collective-permute-start(bf16[336,128]{1,0:T(8,128)(2,1)S(1)} %slice.1422.refs_0_), channel_id=1, source_target_pairs={{0,1},{1,0},{2,3},{3,2},{4,5},{5,4},{6,7},{7,6},{8,9},{9,8},{10,11... | collective-permute-start | bytes 258056 | tf_op jit(solution)/shard_map/ppermute | solution.py:47
  1699.3 25.9 %collective-permute-start.163 = (bf16[336,128]{1,0:T(8,128)(2,1)S(1)}, bf16[336,128]{1,0:T(8,128)(2,1)S(1)}, u32[]{:S(2)}, u32[]{:S(2)}) collective-permute-start(bf16[336,128]{1,0:T(8,128)(2,1)S(1)} %collective-permute-done.162.refs_2_), channel_id=1, source_target_pairs={{0,1},{1,0},{2,3},{3,2},{4,5},{5,4},{6,7},{7,6},{8,9},{9,8},{10,11... | collective-permute-start | bytes 258056 | tf_op jit(solution)/shard_map/ppermute | solution.py:47
  1737.3 47.9 %collective-permute-start.168 = (bf16[2,512,512]{2,1,0:T(8,128)(2,1)}, bf16[2,512,512]{2,1,0:T(8,128)(2,1)}, u32[]{:S(2)}, u32[]{:S(2)}) collective-permute-start(bf16[2,512,512]{2,1,0:T(8,128)(2,1)} %dynamic-slice_bitcast_fusion.14), channel_id=1, source_target_pairs={{0,16},{4,20},{8,24},{12,28},{16,0},{20,4},{24,8},{28,12},{1,17},{... | collective-permute-start | bytes 3145736 | tf_op jit(solution)/shard_map/ppermute | solution.py:47
  1743.4 43.4 %collective-permute-start.174 = (bf16[512,512]{1,0:T(8,128)(2,1)}, bf16[512,512]{1,0:T(8,128)(2,1)S(1)}, u32[]{:S(2)}, u32[]{:S(2)}) collective-permute-start(bf16[512,512]{1,0:T(8,128)(2,1)} %get-tuple-element.160), channel_id=1, source_target_pairs={{0,8},{4,12},{8,0},{12,4},{16,24},{20,28},{24,16},{28,20},{1,9},{5... | collective-permute-start | bytes 1572872 | tf_op jit(solution)/shard_map/ppermute | solution.py:47
  (378 other events, 3881.4 us)
Sparse Core Ops, SparseCore 0:
  124.3 55.7 all-gather.13
  220.3 68.2 all-gather.11
  290.7 56.7 all-gather.9
  349.4 68.5 all-gather.15
  427.8 103.7 all-gather.17
  533.0 68.5 all-gather.7
  681.2 80.1 all-gather.19
  879.3 52.1 reduce-scatter.9
  962.1 86.5 reduce-scatter.11
  1136.4 98.7 reduce-scatter.13
  1237.5 54.3 reduce-scatter.25
  1294.0 20.3 reduce-scatter.23
  1317.2 31.8 reduce-scatter.21
  1351.2 54.2 reduce-scatter.19
  1407.8 54.3 reduce-scatter.17
  1464.9 54.2 reduce-scatter.15
